TPU v7x, 32 devices: a whole 2x2x4 slice. The times are simulated.
32 devices in a mesh: ctx: 8 (over z, x), fsdp: 4 (over y, core).
Axes of the slice: x: 2, y: 2, z: 4, core: 2. Of those that a mesh axis runs over, the one named last changes fastest.
Arguments:
- clean_in: bfloat16 [16, 2, 512, 768], P('fsdp', None, 'ctx'), may hold values from -6 to 6
- segments: int32 [16, 2, 512], P('fsdp', None, 'ctx'), may hold values from 0 to 6, as said below
- noise: int32 [16, 2, 512], P('fsdp', None, 'ctx'), may hold values 0 or 1
- mask_embed: bfloat16 [768], P('fsdp'), may hold values from -6 to 6
- norm1_gain: bfloat16 [768], P('fsdp'), may hold values from 0.25 to 1.75
- qkv_weight: bfloat16 [768, 2304], P('fsdp'), may hold values from -0.21875 to 0.21875
- out_weight: bfloat16 [768, 768], P('fsdp'), may hold values from -0.875 to 0.875
- norm2_gain: bfloat16 [768], P('fsdp'), may hold values from 0.25 to 1.75
- up_weight: bfloat16 [768, 3072], P('fsdp'), may hold values from -0.21875 to 0.21875
- up_bias: bfloat16 [3072], P('fsdp'), may hold values from -3 to 3
- down_weight: bfloat16 [3072, 768], P('fsdp'), may hold values from -0.109375 to 0.109375
- down_bias: bfloat16 [768], P('fsdp'), may hold values from -3 to 3
- out_grad: bfloat16 [16, 2, 2, 512, 768], P('fsdp', None, None, 'ctx'), may hold values from -6 to 6
Outputs:
- block_out: bfloat16 [16, 2, 2, 512, 768], P('fsdp', None, None, 'ctx')
- input_grad: float32 [16, 2, 512, 768], P('fsdp', None, 'ctx')
- mask_embed_grad: float32 [768], P('fsdp')
- norm1_gain_grad: float32 [768], P('fsdp')
- qkv_weight_grad: float32 [768, 2304], P('fsdp')
- out_weight_grad: float32 [768, 768], P('fsdp')
- norm2_gain_grad: float32 [768], P('fsdp')
- up_weight_grad: float32 [768, 3072], P('fsdp')
- up_bias_grad: float32 [3072], P('fsdp')
- down_weight_grad: float32 [3072, 768], P('fsdp')
- down_bias_grad: float32 [768], P('fsdp')
Inputs may be any that keep to these rules, and one draw needn't show every extreme that they name: `segments`: document numbers never fall as the position grows within a sequence, and distinct documents have distinct numbers; the first document is numbered 0 and the last of a sequence has the largest number; each document has 2000 tokens at most, only the last of a sequence has fewer than 200, and the first has min(2000, max(200, 576)).
All inputs are finite; a program needn't handle non-finite values. No bound on the sum of `noise` on one device may be relied on, other than what follows from the above.
Results may differ from a plain program's by a relative error of at most 0.012.
Values may be sent and summed in bfloat16 or wider, within the bound.
A program may use at most 384 MiB of HBM per device.

v0:
```python
from functools import partial

import jax
import jax.numpy as jnp
from jax import lax
from jax.sharding import PartitionSpec as P

D = 768
HEADS = 12
HEAD = 64
FF = 3072
BLK = 16


EPS = 1e-05
together = 4


def normalize(values):
    centre = values - jnp.mean(values, axis=-1, keepdims=True)
    scale = lax.rsqrt(jnp.mean(centre * centre, axis=-1, keepdims=True) + EPS)
    return (centre * scale, scale)


def norm_back(grad_in, normed, scale):
    centred = grad_in - jnp.mean(grad_in, axis=-1, keepdims=True)
    return scale * (centred - normed * jnp.mean(grad_in * normed, axis=-1, keepdims=True))


def rope_tables(positions):
    half_head = HEAD // 2
    frequency = 10000.0 ** (-(jnp.arange(half_head, dtype=jnp.float32) * 2.0) / HEAD)
    angles = positions.astype(jnp.float32)[:, None] * frequency[None, :]
    return (jnp.cos(angles), jnp.sin(angles))


def rotate(values, cos_part, sin_part, reverse):
    count = values.shape[0]
    heads = values.reshape(count, HEADS, HEAD)
    half_head = HEAD // 2
    leading = heads[..., :half_head]
    trailing = heads[..., half_head:]
    cosine = cos_part[:, None, :]
    sine_part = sin_part[:, None, :]
    if reverse:
        parts = [leading * cosine + trailing * sine_part, trailing * cosine - leading * sine_part]
    else:
        parts = [leading * cosine - trailing * sine_part, trailing * cosine + leading * sine_part]
    return jnp.concatenate(parts, axis=-1).reshape(count, D)


def split_heads(values):
    count = values.shape[0]
    return values.reshape(count, HEADS // together, together * HEAD).transpose(1, 0, 2)


def join_heads(values):
    groups, count, width = values.shape
    return values.transpose(1, 0, 2).reshape(count, groups * width)


def allowed_pairs(query_copy, query_block, query_doc, key_copy, key_block, key_doc):
    same_doc = query_doc[:, None] == key_doc[None, :]
    query_noisy = (query_copy == 0)[:, None]
    key_noisy = (key_copy == 0)[None, :]
    query_column = query_block[:, None]
    key_row = key_block[None, :]
    inner = query_noisy & key_noisy & (key_row == query_column)
    earlier = query_noisy & ~key_noisy & (key_row < query_column)
    causal = ~query_noisy & ~key_noisy & (key_row <= query_column)
    return same_doc & (inner | earlier | causal)


def masked_scores(query_group, key_group, allowed):
    query_heads = query_group.reshape(query_group.shape[0], together, HEAD)
    key_heads = key_group.reshape(key_group.shape[0], together, HEAD)
    raw = jnp.einsum(
        "qhd,khd->hqk", query_heads, key_heads, preferred_element_type=jnp.float32
    ) * HEAD ** (-0.5)
    return (jnp.where(allowed[None], raw, -1e30), query_heads, key_heads)


def group_forward(items, allowed):
    query_group, key_group, value_group = items
    count = query_group.shape[0]
    scores, query_heads, key_heads = masked_scores(query_group, key_group, allowed)
    value_heads = value_group.reshape(value_group.shape[0], together, HEAD)
    top = jnp.max(scores, axis=-1, keepdims=True)
    weights = jnp.exp(scores - top)
    total = jnp.sum(weights, axis=-1, keepdims=True)
    probs = (weights / total).astype(jnp.bfloat16)
    mixed = jnp.einsum("hqk,khd->qhd", probs, value_heads, preferred_element_type=jnp.float32)
    return (mixed.reshape(count, together * HEAD), (top + jnp.log(total))[..., 0])


def group_backward(items, allowed, tail):
    query_group, key_group, value_group, grad_group, log_total = items
    count = query_group.shape[0]
    key_count = key_group.shape[0]
    scores, query_heads, key_heads = masked_scores(query_group, key_group, allowed)
    value_heads = value_group.reshape(key_count, together, HEAD)
    grad_heads = grad_group.reshape(count, together, HEAD)
    probs = jnp.exp(scores - log_total[..., None])
    prob_grad = jnp.einsum(
        "qhd,khd->hqk", grad_heads, value_heads, preferred_element_type=jnp.float32
    )
    centre = jnp.sum(probs * prob_grad, axis=-1, keepdims=True)
    score_grad = (probs * (prob_grad - centre)).astype(jnp.bfloat16)
    query_grad = jnp.einsum(
        "hqk,khd->qhd", score_grad, key_heads, preferred_element_type=jnp.float32
    ) * HEAD ** (-0.5)
    tail_probs = probs.astype(jnp.bfloat16)
    value_grad = jnp.einsum(
        "hqk,qhd->khd", tail_probs, grad_heads, preferred_element_type=jnp.float32
    )
    key_grad = jnp.einsum(
        "hqk,qhd->khd", score_grad, query_heads, preferred_element_type=jnp.float32
    ) * HEAD ** (-0.5)
    return (
        query_grad.reshape(count, together * HEAD),
        key_grad.reshape(tail, together * HEAD),
        value_grad.reshape(tail, together * HEAD),
        centre[..., 0],
    )


def reduce_grads(grads):
    shards = (
        lax.psum_scatter(grads[0], "fsdp", scatter_dimension=0, tiled=True),
        lax.psum_scatter(grads[1], "fsdp", scatter_dimension=0, tiled=True),
        lax.psum_scatter(grads[2], "fsdp", scatter_dimension=0, tiled=True),
        lax.psum_scatter(grads[3], "fsdp", scatter_dimension=0, tiled=True),
        lax.psum_scatter(grads[4], "fsdp", scatter_dimension=0, tiled=True),
        lax.psum_scatter(grads[5], "fsdp", scatter_dimension=0, tiled=True),
        lax.psum_scatter(grads[6], "fsdp", scatter_dimension=0, tiled=True),
        lax.psum_scatter(grads[7], "fsdp", scatter_dimension=0, tiled=True),
        lax.psum_scatter(grads[8], "fsdp", scatter_dimension=0, tiled=True),
    )
    return lax.psum(
        (
            shards[0],
            shards[1],
            shards[2],
            shards[3],
            shards[4],
            shards[5],
            shards[6],
            shards[7],
            shards[8],
        ),
        "ctx",
    )


def add_tuples(left_items, right_items):
    return tuple((left_item + right_item for left_item, right_item in zip(left_items, right_items)))


def body(
    clean_in,
    segments,
    noise,
    mask_embed,
    norm1_gain,
    qkv_weight,
    out_weight,
    norm2_gain,
    up_weight,
    up_bias,
    down_weight,
    down_bias,
    out_grad,
):
    qkv_full, out_full, gain_low, embed_low = (
        lax.all_gather(qkv_weight, "fsdp", axis=0, tiled=True),
        lax.all_gather(out_weight, "fsdp", axis=0, tiled=True),
        lax.all_gather(norm1_gain, "fsdp", axis=0, tiled=True),
        lax.all_gather(mask_embed, "fsdp", axis=0, tiled=True),
    )
    up_full, up_low, down_full, down_low, gain_two_low = (
        lax.all_gather(up_weight, "fsdp", axis=0, tiled=True),
        lax.all_gather(up_bias, "fsdp", axis=0, tiled=True),
        lax.all_gather(down_weight, "fsdp", axis=0, tiled=True),
        lax.all_gather(down_bias, "fsdp", axis=0, tiled=True),
        lax.all_gather(norm2_gain, "fsdp", axis=0, tiled=True),
    )
    gain_one = gain_low.astype(jnp.float32)
    gain_two = gain_two_low.astype(jnp.float32)
    embed_row = embed_low.astype(jnp.float32)
    up_shift = up_low.astype(jnp.float32)
    down_shift = down_low.astype(jnp.float32)
    micro_count = clean_in.shape[0]
    piece = clean_in.shape[2]
    local_rows = 2 * piece
    ctx_count = lax.axis_size("ctx")
    ctx_rank = lax.axis_index("ctx")
    span = jnp.arange(piece, dtype=jnp.int32)
    local_pos = jnp.concatenate(
        [ctx_rank * piece + span, (2 * ctx_count - 1 - ctx_rank) * piece + span]
    )
    ranks = jnp.arange(ctx_count, dtype=jnp.int32)[:, None]
    far_pos = jnp.concatenate(
        [ranks * piece + span[None, :], (2 * ctx_count - 1 - ranks) * piece + span[None, :]], axis=1
    ).reshape(-1)
    seq_len = ctx_count * local_rows
    cos_part, sin_part = rope_tables(jnp.concatenate([local_pos, local_pos]))
    query_copy = jnp.concatenate(
        [jnp.zeros((local_rows,), jnp.int32), jnp.ones((local_rows,), jnp.int32)]
    )
    key_copy = jnp.concatenate(
        [jnp.ones((seq_len,), jnp.int32), jnp.zeros((local_rows,), jnp.int32)]
    )
    query_block = jnp.concatenate([local_pos, local_pos]) // BLK
    key_block = jnp.concatenate([far_pos, local_pos]) // BLK
    full_shapes = ((D,), (D,), (D, 3 * D), (D, D), (D,), (D, FF), (FF,), (FF, D), (D,))
    totals = tuple((jnp.zeros(shape_item, jnp.float32) for shape_item in full_shapes))
    tail = seq_len + local_rows
    outputs = []
    input_grads = []
    for micro_step in range(micro_count):
        clean_rows = clean_in[micro_step].reshape(local_rows, D).astype(jnp.float32)
        noise_rows = noise[micro_step].reshape(-1)
        masked_rows = noise_rows[:, None] == 1
        doc_local = segments[micro_step].reshape(-1).astype(jnp.float32)
        noisy_rows = jnp.where(masked_rows, embed_row[None, :], clean_rows)
        stacked = jnp.concatenate([noisy_rows, clean_rows], axis=0)
        normed_one, scale_one = normalize(stacked)
        h_one = (normed_one * gain_one).astype(jnp.bfloat16)
        projected = jnp.dot(h_one, qkv_full, preferred_element_type=jnp.float32)
        queries = rotate(projected[:, :D], cos_part, sin_part, False).astype(jnp.bfloat16)
        keys = rotate(projected[:, D : 2 * D], cos_part, sin_part, False).astype(jnp.bfloat16)
        values = projected[:, 2 * D :].astype(jnp.bfloat16)
        far_keys, far_values, far_docs = (
            lax.all_gather(keys[local_rows:], "ctx", axis=0, tiled=True),
            lax.all_gather(values[local_rows:], "ctx", axis=0, tiled=True),
            lax.all_gather(doc_local.astype(jnp.bfloat16), "ctx", axis=0, tiled=True),
        )
        key_all = jnp.concatenate([far_keys, keys[:local_rows]], axis=0)
        value_all = jnp.concatenate([far_values, values[:local_rows]], axis=0)
        query_doc = jnp.concatenate([doc_local, doc_local])
        key_doc = jnp.concatenate([far_docs.astype(jnp.float32), doc_local])
        allowed = allowed_pairs(query_copy, query_block, query_doc, key_copy, key_block, key_doc)
        query_groups = split_heads(queries)
        key_groups = split_heads(key_all)
        value_groups = split_heads(value_all)
        mixed_groups, log_totals = lax.map(
            partial(group_forward, allowed=allowed), (query_groups, key_groups, value_groups)
        )
        mixed = join_heads(mixed_groups).astype(jnp.bfloat16)
        resid = stacked + jnp.dot(mixed, out_full, preferred_element_type=jnp.float32)
        normed_two, scale_two = normalize(resid)
        h_two = (normed_two * gain_two).astype(jnp.bfloat16)
        hidden = jnp.dot(h_two, up_full, preferred_element_type=jnp.float32) + up_shift
        active = jax.nn.gelu(hidden, approximate=True).astype(jnp.bfloat16)
        result = resid + jnp.dot(active, down_full, preferred_element_type=jnp.float32) + down_shift
        outputs.append(result.astype(jnp.bfloat16).reshape(2, 2, piece, D))
        cotangent = out_grad[micro_step].reshape(2 * local_rows, D).astype(jnp.float32)
        grad_out = cotangent.astype(jnp.bfloat16)
        down_grad = jnp.einsum("rf,rd->fd", active, grad_out, preferred_element_type=jnp.float32)
        down_shift_grad = jnp.sum(grad_out.astype(jnp.float32), axis=0)
        grad_active = jnp.einsum(
            "rd,fd->rf", grad_out, down_full, preferred_element_type=jnp.float32
        )
        unused, gelu_back = jax.vjp(partial(jax.nn.gelu, approximate=True), hidden)
        grad_hidden = gelu_back(grad_active)[0].astype(jnp.bfloat16)
        up_grad = jnp.einsum("rd,rf->df", h_two, grad_hidden, preferred_element_type=jnp.float32)
        up_shift_grad = jnp.sum(grad_hidden.astype(jnp.float32), axis=0)
        grad_h_two = jnp.einsum(
            "rf,df->rd", grad_hidden, up_full, preferred_element_type=jnp.float32
        )
        gain_two_grad = jnp.sum(grad_h_two * normed_two, axis=0)
        grad_resid = cotangent + norm_back(grad_h_two * gain_two, normed_two, scale_two)
        grad_attn = grad_resid.astype(jnp.bfloat16)
        out_grad_full = jnp.einsum(
            "rd,re->de", mixed, grad_attn, preferred_element_type=jnp.float32
        )
        grad_mixed = jnp.einsum(
            "re,de->rd", grad_attn, out_full, preferred_element_type=jnp.float32
        ).astype(jnp.bfloat16)
        query_grads, key_grads, value_grads, centres = lax.map(
            partial(group_backward, allowed=allowed, tail=tail),
            (query_groups, key_groups, value_groups, split_heads(grad_mixed), log_totals),
        )
        query_grad = join_heads(query_grads)
        key_grad_all = join_heads(key_grads)
        value_grad_all = join_heads(value_grads)
        key_mine, value_mine = (
            lax.psum_scatter(key_grad_all[:seq_len], "ctx", scatter_dimension=0, tiled=True),
            lax.psum_scatter(value_grad_all[:seq_len], "ctx", scatter_dimension=0, tiled=True),
        )
        key_grad = jnp.concatenate([key_grad_all[seq_len:], key_mine], axis=0)
        value_grad = jnp.concatenate([value_grad_all[seq_len:], value_mine], axis=0)
        grad_proj = jnp.concatenate(
            [
                rotate(query_grad, cos_part, sin_part, True),
                rotate(key_grad, cos_part, sin_part, True),
                value_grad,
            ],
            axis=1,
        ).astype(jnp.bfloat16)
        qkv_grad = jnp.einsum("rd,re->de", h_one, grad_proj, preferred_element_type=jnp.float32)
        grad_h_one = jnp.einsum(
            "re,de->rd", grad_proj, qkv_full, preferred_element_type=jnp.float32
        )
        gain_one_grad = jnp.sum(grad_h_one * normed_one, axis=0)
        grad_rows = grad_resid + norm_back(grad_h_one * gain_one, normed_one, scale_one)
        grad_noisy = grad_rows[:local_rows]
        input_grads.append(
            (grad_rows[local_rows:] + jnp.where(masked_rows, 0.0, grad_noisy)).reshape(2, piece, D)
        )
        embed_grad = jnp.sum(jnp.where(masked_rows, grad_noisy, 0.0), axis=0)
        step_grads = (
            embed_grad,
            gain_one_grad,
            qkv_grad,
            out_grad_full,
            gain_two_grad,
            up_grad,
            up_shift_grad,
            down_grad,
            down_shift_grad,
        )
        totals = add_tuples(totals, step_grads)
    reduced = reduce_grads(totals)
    block_out = jnp.stack(outputs)
    input_grad = jnp.stack(input_grads)
    return (
        block_out,
        input_grad,
        reduced[0],
        reduced[1],
        reduced[2],
        reduced[3],
        reduced[4],
        reduced[5],
        reduced[6],
        reduced[7],
        reduced[8],
    )


def solution(mesh):
    placed = (
        P("fsdp", None, "ctx", None),
        P("fsdp", None, "ctx"),
        P("fsdp", None, "ctx"),
        P("fsdp"),
        P("fsdp"),
        P("fsdp", None),
        P("fsdp", None),
        P("fsdp"),
        P("fsdp", None),
        P("fsdp"),
        P("fsdp", None),
        P("fsdp"),
        P("fsdp", None, None, "ctx", None),
    )
    return jax.shard_map(
        body,
        mesh=mesh,
        in_specs=placed,
        out_specs=(
            P("fsdp", None, None, "ctx", None),
            P("fsdp", None, "ctx", None),
            P("fsdp"),
            P("fsdp"),
            P("fsdp", None),
            P("fsdp", None),
            P("fsdp"),
            P("fsdp", None),
            P("fsdp"),
            P("fsdp", None),
            P("fsdp"),
        ),
        check_vma=False,
    )
```

profile of v0, /device:TPU:0, one launch (start us, length us, event | category | flops | bytes accessed | tf_op | source)
XLA Modules:
  0.0 1734.3 jit_solution(16462985884417258598)
XLA Ops:
  14.1 9.1 all-reduce.12
  28.0 15.1 all-gather.18.cloned.1.call-done
  60.6 20.4 %all-gather = bf16[8,1,128]{2,1,0:T(2,128)(2,1)S(1)} all-gather(bf16[1,1,128]{2,1,0:T(2,128)(2,1)S(1)} %get-tuple-element.1187), channel_id=1, replica_groups=mesh['ctx'=8,'fsdp'=4] {'ctx'}, dimensions={0}, use_global_device_ids=true | all-gather | bytes 2304 | tf_op jit(solution)/shard_map/all_gather | solution.py:236
  94.1 16.2 all-gather.2
  114.5 18.3 %all-gather.3 = bf16[8,1,128]{2,1,0:T(2,128)(2,1)S(1)} all-gather(bf16[1,1,128]{2,1,0:T(2,128)(2,1)S(1)} %get-tuple-element.1191), channel_id=1, replica_groups=mesh['ctx'=8,'fsdp'=4] {'ctx'}, dimensions={0}, use_global_device_ids=true | all-gather | bytes 2304 | tf_op jit(solution)/shard_map/all_gather | solution.py:236
  182.5 20.9 %while.112 = (s32[]{:T(128)}, bf16[3,256,256]{1,2,0:T(8,128)(2,1)}, f32[3,4,256]{2,1,0:T(4,128)S(1)}, bf16[3,1152,256]{1,2,0:T(8,128)(2,1)S(1)}, bf16[3,256,256]...) while((s32[]{:T(128)}, bf16[3,256,256]{1,2,0:T(8,128)(2,1)}, ...), condition=%wide.region_5.6_spmd.clone, body=%wide.region_2.5_spmd.clone.sunk | while | flops 315259904 | bytes 19117988 | solution.py:246
  206.5 24.0 %all-gather.26.cloned.1.call-done = bf16[768,3072]{1,0:T(8,128)(2,1)} async-done(((bf16[192,3072]{1,0:T(8,128)(2,1)}), bf16[768,3072]{1,0:T(8,128)(2,1)}) %all-gather.26.cloned.1.call-update) | async-done | bytes 4718608 | tf_op jit(solution)/shard_map/all_gather | solution.py:181
  230.5 9.5 convert_reduce_fusion.3
  251.7 35.7 %while.116 = (s32[]{:T(128)}, f32[3,256,256]{1,2,0:T(8,128)}, f32[3,1152,256]{1,2,0:T(8,128)}, f32[3,1152,256]{1,2,0:T(8,128)}, bf16[3,1152,256]{1,2,0:T(8,128)(...) while((s32[]{:T(128)}, f32[3,256,256]{1,2,0:T(8,128)}, ...), condition=%wide.region_36.37_spmd.clone, body=%wide.region_34.36_spmd.clone.sunk | while | flops 769784832 | bytes 49055688 | solution.py:280
  301.2 5.6 fusion.168
  306.8 5.5 fusion.169
  330.4 38.0 %all-gather.32.cloned.1.call-done = bf16[1024,768]{0,1:T(8,128)(2,1)} async-done(((bf16[128,768]{0,1:T(8,128)(2,1)}), bf16[1024,768]{0,1:T(8,128)(2,1)}) %all-gather.32.cloned.1.call-update) | async-done | bytes 1572880 | tf_op jit(solution)/shard_map/all_gather | solution.py:234
  371.3 24.2 %while.113 = (s32[]{:T(128)}, bf16[3,256,256]{1,2,0:T(8,128)(2,1)}, f32[3,4,256]{2,1,0:T(4,128)S(1)}, bf16[3,1152,256]{1,2,0:T(8,128)(2,1)}, bf16[3,256,256]{1,2...) while((s32[]{:T(128)}, bf16[3,256,256]{1,2,0:T(8,128)(2,1)}, ...), condition=%wide.region_13.14_spmd.clone, body=%wide.region_10.13_spmd.clone.sunk | while | flops 315259904 | bytes 19117988 | solution.py:246
  395.5 49.8 %reduce-scatter.13.cloned.1.call-done = f32[128,768]{0,1:T(8,128)} async-done(((f32[1024,768]{0,1:T(8,128)}), f32[128,768]{0,1:T(8,128)}) %reduce-scatter.13.cloned.1.call-update) | async-done | bytes 393232 | tf_op jit(solution)/shard_map/reduce_scatter | solution.py:288
  451.4 8.1 convert_reduce_fusion.2
  459.5 6.0 multiply_reduce_fusion.6
  466.6 27.1 %all-gather.36.cloned.1.call-done = bf16[1024,768]{0,1:T(8,128)(2,1)} async-done(((bf16[128,768]{0,1:T(8,128)(2,1)}), bf16[1024,768]{0,1:T(8,128)(2,1)}) %all-gather.36.cloned.1.call-update) | async-done | bytes 1572880 | tf_op jit(solution)/shard_map/all_gather | solution.py:234
  497.1 25.3 %while.114 = (s32[]{:T(128)}, bf16[3,256,256]{1,2,0:T(8,128)(2,1)}, f32[3,4,256]{2,1,0:T(4,128)}, bf16[3,1152,256]{1,2,0:T(8,128)(2,1)S(1)}, bf16[3,256,256]{1,2...) while((s32[]{:T(128)}, bf16[3,256,256]{1,2,0:T(8,128)(2,1)}, ...), condition=%wide.region_21.22_spmd.clone, body=%wide.region_18.21_spmd.clone.sunk | while | flops 315259904 | bytes 19117988 | solution.py:246
  525.2 8.6 convert_reduce_fusion.1
  533.9 6.2 multiply_reduce_fusion.5
  545.0 36.4 %while.117 = (s32[]{:T(128)}, f32[3,256,256]{1,2,0:T(8,128)S(1)}, f32[3,1152,256]{1,2,0:T(8,128)}, f32[3,1152,256]{1,2,0:T(8,128)}, bf16[3,1152,256]{1,2,0:T(8,1...) while((s32[]{:T(128)}, f32[3,256,256]{1,2,0:T(8,128)S(1)}, ...), condition=%wide.region_45.46_spmd.clone, body=%wide.region_43.45_spmd.clone.sunk | while | flops 769784832 | bytes 49055688 | solution.py:280
  589.7 69.0 %reduce-scatter.17.cloned.1.call-done = f32[128,768]{0,1:T(8,128)} async-done(((f32[1024,768]{0,1:T(8,128)}), f32[128,768]{0,1:T(8,128)}) %reduce-scatter.17.cloned.1.call-update) | async-done | bytes 393232 | tf_op jit(solution)/shard_map/reduce_scatter | solution.py:288
  666.8 18.7 %all-gather.4 = bf16[8,1,128]{2,1,0:T(2,128)(2,1)S(1)} all-gather(bf16[1,1,128]{2,1,0:T(2,128)(2,1)S(1)} %get-tuple-element.1193), channel_id=1, replica_groups=mesh['ctx'=8,'fsdp'=4] {'ctx'}, dimensions={0}, use_global_device_ids=true | all-gather | bytes 2304 | tf_op jit(solution)/shard_map/all_gather | solution.py:236
  685.5 5.7 fusion.170
  691.2 13.3 all-gather.38.cloned.1.call-done
  716.2 34.4 %all-gather.40.cloned.1.call-done = bf16[1024,768]{0,1:T(8,128)(2,1)} async-done(((bf16[128,768]{0,1:T(8,128)(2,1)}), bf16[1024,768]{0,1:T(8,128)(2,1)}) %all-gather.40.cloned.1.call-update) | async-done | bytes 1572880 | tf_op jit(solution)/shard_map/all_gather | solution.py:234
  753.3 23.7 %while.115 = (s32[]{:T(128)}, bf16[3,256,256]{1,2,0:T(8,128)(2,1)}, f32[3,4,256]{2,1,0:T(4,128)S(1)}, bf16[3,1152,256]{1,2,0:T(8,128)(2,1)S(1)}, bf16[3,256,256]...) while((s32[]{:T(128)}, bf16[3,256,256]{1,2,0:T(8,128)(2,1)}, ...), condition=%wide.region_29.30_spmd.clone, body=%wide.region_26.29_spmd.clone.sunk | while | flops 315259904 | bytes 19117988 | solution.py:246
  779.2 8.3 convert_reduce_fusion
  787.5 6.3 multiply_reduce_fusion.4
  802.1 38.6 %while.118 = (s32[]{:T(128)}, f32[3,256,256]{1,2,0:T(8,128)}, f32[3,1152,256]{1,2,0:T(8,128)}, f32[3,1152,256]{1,2,0:T(8,128)}, bf16[3,1152,256]{1,2,0:T(8,128)(...) while((s32[]{:T(128)}, f32[3,256,256]{1,2,0:T(8,128)}, ...), condition=%wide.region_54.55_spmd.clone, body=%wide.region_52.54_spmd.clone.sunk | while | flops 769784832 | bytes 49055688 | solution.py:280
  850.9 31.4 %while.119 = (s32[]{:T(128)}, f32[3,256,256]{1,2,0:T(8,128)S(1)}, f32[3,1152,256]{1,2,0:T(8,128)}, f32[3,1152,256]{1,2,0:T(8,128)}, bf16[3,1152,256]{1,2,0:T(8,1...) while((s32[]{:T(128)}, f32[3,256,256]{1,2,0:T(8,128)S(1)}, ...), condition=%wide.region_63.64_spmd.clone, body=%wide.region_61.63_spmd.clone.sunk | while | flops 769784832 | bytes 49055688 | solution.py:280
  912.5 12.6 add_add_fusion.1
  929.4 5.9 fusion.133
  935.3 5.8 fusion.134
  941.2 11.2 add_add_fusion
  974.2 8.2 reduce-scatter.23.cloned.1.call-done
  984.1 76.0 %reduce-scatter.27.cloned.1.call-done = f32[128,768]{0,1:T(8,128)} async-done(((f32[1024,768]{0,1:T(8,128)}), f32[128,768]{0,1:T(8,128)}) %reduce-scatter.27.cloned.1.call-update) | async-done | bytes 393232 | tf_op jit(solution)/shard_map/reduce_scatter | solution.py:289
  1061.8 76.2 %reduce-scatter.21.cloned.1.call-done = f32[128,768]{0,1:T(8,128)} async-done(((f32[1024,768]{0,1:T(8,128)}), f32[128,768]{0,1:T(8,128)}) %reduce-scatter.21.cloned.1.call-update) | async-done | bytes 393232 | tf_op jit(solution)/shard_map/reduce_scatter | solution.py:288
  1141.8 74.0 %reduce-scatter.25.cloned.1.call-done = f32[128,768]{0,1:T(8,128)} async-done(((f32[1024,768]{0,1:T(8,128)}), f32[128,768]{0,1:T(8,128)}) %reduce-scatter.25.cloned.1.call-update) | async-done | bytes 393232 | tf_op jit(solution)/shard_map/reduce_scatter | solution.py:288
  1221.5 8.4 add_add_fusion.2
  1232.4 5.8 fusion.80
  1243.9 7.1 reduce-scatter.31.cloned.1.call-done
  1251.1 81.3 %reduce-scatter.33.cloned.1.call-done = f32[192,3072]{1,0:T(8,128)} async-done(((f32[768,3072]{1,0:T(8,128)}), f32[192,3072]{1,0:T(8,128)}) %reduce-scatter.33.cloned.1.call-update) | async-done | bytes 2359312 | tf_op jit(solution)/shard_map/reduce_scatter | solution.py:134
  1332.3 81.3 %reduce-scatter.35.cloned.1.call-done = f32[768,768]{1,0:T(8,128)} async-done(((f32[3072,768]{1,0:T(8,128)}), f32[768,768]{1,0:T(8,128)}) %reduce-scatter.35.cloned.1.call-update) | async-done | bytes 2359312 | tf_op jit(solution)/shard_map/reduce_scatter | solution.py:136
  1413.6 66.2 %reduce-scatter.29.cloned.1.call-done = f32[192,2304]{1,0:T(8,128)} async-done(((f32[768,2304]{1,0:T(8,128)}), f32[192,2304]{1,0:T(8,128)}) %reduce-scatter.29.cloned.1.call-update) | async-done | bytes 1769488 | tf_op jit(solution)/shard_map/reduce_scatter | solution.py:131
  1497.9 11.1 all-reduce.11
  1509.3 23.8 %all-reduce.9 = (f32[192]{0:T(256)}, f32[192]{0:T(256)}, f32[192]{0:T(256)}, f32[768]{0:T(1024)}, f32[192]{0:T(256)}) all-reduce(f32[192]{0:T(256)S(1)} %dynamic-slice.5, f32[192]{0:T(256)S(1)} %dynamic-slice.7, f32[192]{0:T(256)S(1)} %dynamic-slice.9, f32[768]{0:T(1024)S(1)} %dynamic-slice.11, ...), channel_id=1, replica_groups=mesh['ctx'=8,'fsdp'=4] {'ctx'}, use_global_device_ids=true, to_apply=%region_73.74 | all-reduce | flops 1536 | bytes 12288 | tf_op jit(solution)/shard_map/psum | solution.py:139
  1534.5 186.2 %all-reduce.15.cloned.1.call-done = (f32[192,2304]{1,0:T(8,128)}, f32[192,768]{1,0:T(8,128)}, f32[192,3072]{1,0:T(8,128)}, f32[768,768]{1,0:T(8,128)}) async-done(((f32[192,2304]{1,0:T(8,128)}, f32[192,768]{1,0:T(8,128)}, f32[192,3072]{1,0:T(8,128)}, f32[768,768]{1,0:T(8,128)}), (f32[192,2304]{1,0:T(8,128)}, f32[192,768]{1,0:T(8,128)}, f32[192,3072]{1,0:T(8,128)}, ...) | async-done | bytes 7077904 | tf_op jit(solution)/shard_map/psum | solution.py:139
  (1076 shorter events, 548.3 us)
Async XLA Ops:
  7.2 35.9 %all-gather.18.cloned.1.call-start = ((), (), s32[]{:S(2)}) async-start(), calls=%async_computation.12 | async-start | bytes 4423680 | tf_op jit(solution)/shard_map/all_gather | solution.py:175
  7.9 160.4 %all-gather.28.cloned.1.call-start = ((), (), s32[]{:S(2)}) async-start(), calls=%async_computation.17 | async-start | bytes 5898240 | tf_op jit(solution)/shard_map/all_gather | solution.py:183
  8.7 165.1 %all-gather.20.cloned.1.call-start = ((), (), s32[]{:S(2)}) async-start(), calls=%async_computation.13 | async-start | bytes 1769472 | tf_op jit(solution)/shard_map/all_gather | solution.py:235
  24.2 270.6 %copy-start.75 = (f32[768]{0:T(1024)}, f32[768]{0:T(1024)S(1)}, u32[]{:S(2)}) copy-start(f32[768]{0:T(1024)S(1)} %convert_element_type.333) | copy-start | bytes 9220
  47.1 132.5 %all-gather.22.cloned.1.call-start = ((), (), s32[]{:S(2)}) async-start(), calls=%async_computation.14 | async-start | bytes 1769472 | tf_op jit(solution)/shard_map/all_gather | solution.py:234
  53.1 88.3 %copy-start.1 = (bf16[768,2304]{1,0:T(8,128)(2,1)S(1)}, bf16[768,2304]{1,0:T(8,128)(2,1)}, u32[]{:S(2)}) copy-start(bf16[768,2304]{1,0:T(8,128)(2,1)} %all-gather.18.cloned.1.call-done) | copy-start | bytes 10616836
  54.0 149.4 %all-gather.24.cloned.1.call-start = ((), (), s32[]{:S(2)}) async-start(), calls=%async_computation.15 | async-start | bytes 1474560 | tf_op jit(solution)/shard_map/all_gather | solution.py:176
  54.5 175.9 %all-gather.26.cloned.1.call-start = ((), (), s32[]{:S(2)}) async-start(), calls=%async_computation.16 | async-start | bytes 5898240 | tf_op jit(solution)/shard_map/all_gather | solution.py:181
  55.1 260.1 %all-gather.30.cloned.1.call-start = ((), (), s32[]{:S(2)}) async-start(), calls=%async_computation.18 | async-start | bytes 1769472 | tf_op jit(solution)/shard_map/all_gather | solution.py:235
  60.6 84.4 %copy-start.173 = (f32[256]{0:T(256)}, f32[256]{0:T(256)S(1)}, u32[]{:S(2)}) copy-start(f32[256]{0:T(256)S(1)} %get-tuple-element.2097) | copy-start | bytes 3076
  94.1 50.9 %copy-start.170 = (f32[256]{0:T(256)}, f32[256]{0:T(256)S(1)}, u32[]{:S(2)}) copy-start(f32[256]{0:T(256)S(1)} %get-tuple-element.2241) | copy-start | bytes 3076
  145.9 176.3 %all-gather.34.cloned.1.call-start = ((), (), s32[]{:S(2)}) async-start(), calls=%async_computation.20 | async-start | bytes 1769472 | tf_op jit(solution)/shard_map/all_gather | solution.py:235
  168.3 200.1 %all-gather.32.cloned.1.call-start = ((), (), s32[]{:S(2)}) async-start(), calls=%async_computation.19 | async-start | bytes 1769472 | tf_op jit(solution)/shard_map/all_gather | solution.py:234
  203.3 36.7 %copy-start.179 = (f32[3,4,256]{2,1,0:T(4,128)}, f32[3,4,256]{2,1,0:T(4,128)S(1)}, u32[]{:S(2)}) copy-start(f32[3,4,256]{2,1,0:T(4,128)S(1)} %get-tuple-element.2093) | copy-start | bytes 36868
  205.4 36.7 %copy-start.192 = (f32[256]{0:T(256)}, f32[256]{0:T(256)S(1)}, u32[]{:S(2)}) copy-start(f32[256]{0:T(256)S(1)} %broadcast_multiply_fusion.22) | copy-start | bytes 3076
  251.7 35.7 %copy-start.101 = (f32[256,32]{0,1:T(8,128)S(1)}, f32[256,32]{0,1:T(8,128)}, u32[]{:S(2)}) copy-start(f32[256,32]{0,1:T(8,128)} %copy-done.100) | copy-start | bytes 98308
  251.7 35.7 %copy-start.104 = (f32[256,32]{0,1:T(8,128)S(1)}, f32[256,32]{0,1:T(8,128)}, u32[]{:S(2)}) copy-start(f32[256,32]{0,1:T(8,128)} %copy-done.103) | copy-start | bytes 98308
  291.7 153.6 %reduce-scatter.13.cloned.1.call-start = ((), (), s32[]{:S(2)}) async-start(), calls=%async_computation.24 | async-start | bytes 3538944 | tf_op jit(solution)/shard_map/reduce_scatter | solution.py:288
  327.7 43.5 %copy-start.133 = (f32[1152]{0:T(1024)S(1)}, f32[1152]{0:T(1024)}, u32[]{:S(2)}) copy-start(f32[1152]{0:T(1024)} %pad_maximum_fusion.35) | copy-start | bytes 13828
  327.7 43.5 %copy-start.171 = (f32[256]{0:T(256)S(1)}, f32[256]{0:T(256)}, u32[]{:S(2)}) copy-start(f32[256]{0:T(256)} %copy-done.170) | copy-start | bytes 3076
  327.7 166.0 %all-gather.36.cloned.1.call-start = ((), (), s32[]{:S(2)}) async-start(), calls=%async_computation.21 | async-start | bytes 1769472 | tf_op jit(solution)/shard_map/all_gather | solution.py:234
  395.5 55.6 %copy-start.180 = (f32[3,4,256]{2,1,0:T(4,128)}, f32[3,4,256]{2,1,0:T(4,128)S(1)}, u32[]{:S(2)}) copy-start(f32[3,4,256]{2,1,0:T(4,128)S(1)} %get-tuple-element.2237) | copy-start | bytes 36868
  395.5 53.7 %copy-start.15 = (f32[128,768]{1,0:T(8,128)S(1)}, f32[128,768]{1,0:T(8,128)}, u32[]{:S(2)}) copy-start(f32[128,768]{1,0:T(8,128)} %copy-done.14) | copy-start | bytes 1179652
  449.2 209.6 %reduce-scatter.17.cloned.1.call-start = ((), (), s32[]{:S(2)}) async-start(), calls=%async_computation.26 | async-start | bytes 3538944 | tf_op jit(solution)/shard_map/reduce_scatter | solution.py:288
  524.8 262.6 %copy-start.201 = (f32[256]{0:T(256)}, f32[256]{0:T(256)S(1)}, u32[]{:S(2)}) copy-start(f32[256]{0:T(256)S(1)} %broadcast_multiply_fusion.18) | copy-start | bytes 3076
  585.3 73.4 %copy-start.105 = (f32[256,32]{0,1:T(8,128)S(1)}, f32[256,32]{0,1:T(8,128)}, u32[]{:S(2)}) copy-start(f32[256,32]{0,1:T(8,128)} %copy-done.103) | copy-start | bytes 98308
  585.3 119.2 %all-gather.38.cloned.1.call-start = ((), (), s32[]{:S(2)}) async-start(), calls=%async_computation.22 | async-start | bytes 1769472 | tf_op jit(solution)/shard_map/all_gather | solution.py:235
  587.2 163.4 %all-gather.40.cloned.1.call-start = ((), (), s32[]{:S(2)}) async-start(), calls=%async_computation.23 | async-start | bytes 1769472 | tf_op jit(solution)/shard_map/all_gather | solution.py:234
  662.0 292.1 %reduce-scatter.15.cloned.1.call-start = ((), (), s32[]{:S(2)}) async-start(), calls=%async_computation.25 | async-start | bytes 3538944 | tf_op jit(solution)/shard_map/reduce_scatter | solution.py:289
  666.0 295.4 %reduce-scatter.19.cloned.1.call-start = ((), (), s32[]{:S(2)}) async-start(), calls=%async_computation.27 | async-start | bytes 3538944 | tf_op jit(solution)/shard_map/reduce_scatter | solution.py:289
  716.1 266.3 %reduce-scatter.23.cloned.1.call-start = ((), (), s32[]{:S(2)}) async-start(), calls=%async_computation.29 | async-start | bytes 3538944 | tf_op jit(solution)/shard_map/reduce_scatter | solution.py:289
  778.9 65.9 %copy-start.194 = (f32[256]{0:T(256)}, f32[256]{0:T(256)S(1)}, u32[]{:S(2)}) copy-start(f32[256]{0:T(256)S(1)} %broadcast_multiply_fusion.16) | copy-start | bytes 3076
  779.1 65.6 %copy-start.210 = (f32[256]{0:T(256)}, f32[256]{0:T(256)S(1)}, u32[]{:S(2)}) copy-start(f32[256]{0:T(256)S(1)} %add_rsqrt_fusion) | copy-start | bytes 3076
  846.7 213.4 %reduce-scatter.27.cloned.1.call-start = ((), (), s32[]{:S(2)}) async-start(), calls=%async_computation.31 | async-start | bytes 3538944 | tf_op jit(solution)/shard_map/reduce_scatter | solution.py:289
  886.6 251.4 %reduce-scatter.21.cloned.1.call-start = ((), (), s32[]{:S(2)}) async-start(), calls=%async_computation.28 | async-start | bytes 3538944 | tf_op jit(solution)/shard_map/reduce_scatter | solution.py:288
  891.1 324.6 %reduce-scatter.25.cloned.1.call-start = ((), (), s32[]{:S(2)}) async-start(), calls=%async_computation.30 | async-start | bytes 3538944 | tf_op jit(solution)/shard_map/reduce_scatter | solution.py:288
  893.4 357.7 %reduce-scatter.31.cloned.1.call-start = ((), (), s32[]{:S(2)}) async-start(), calls=%async_computation.33 | async-start | bytes 2949120 | tf_op jit(solution)/shard_map/reduce_scatter | solution.py:132
  899.2 433.1 %reduce-scatter.33.cloned.1.call-start = ((), (), s32[]{:S(2)}) async-start(), calls=%async_computation.34 | async-start | bytes 11796480 | tf_op jit(solution)/shard_map/reduce_scatter | solution.py:134
  925.1 488.4 %reduce-scatter.35.cloned.1.call-start = ((), (), s32[]{:S(2)}) async-start(), calls=%async_computation.35 | async-start | bytes 11796480 | tf_op jit(solution)/shard_map/reduce_scatter | solution.py:136
  952.4 527.3 %reduce-scatter.29.cloned.1.call-start = ((), (), s32[]{:S(2)}) async-start(), calls=%async_computation.32 | async-start | bytes 8847360 | tf_op jit(solution)/shard_map/reduce_scatter | solution.py:131
  968.5 169.5 %copy-start.90 = (f32[3,256,256]{1,2,0:T(8,128)S(1)}, f32[3,256,256]{1,2,0:T(8,128)}, u32[]{:S(2)}) copy-start(f32[3,256,256]{1,2,0:T(8,128)} %copy-done.89) | copy-start | bytes 2359300
  968.5 169.5 %copy-start.91 = (f32[3,256,256]{1,2,0:T(8,128)S(1)}, f32[3,256,256]{1,2,0:T(8,128)}, u32[]{:S(2)}) copy-start(f32[3,256,256]{1,2,0:T(8,128)} %get-tuple-element.392) | copy-start | bytes 2359300
  968.5 169.5 %copy-start.102 = (f32[256,32]{0,1:T(8,128)S(1)}, f32[256,32]{0,1:T(8,128)}, u32[]{:S(2)}) copy-start(f32[256,32]{0,1:T(8,128)} %copy-done.100) | copy-start | bytes 98308
  968.5 169.5 %copy-start.106 = (f32[256,32]{0,1:T(8,128)S(1)}, f32[256,32]{0,1:T(8,128)}, u32[]{:S(2)}) copy-start(f32[256,32]{0,1:T(8,128)} %copy-done.103) | copy-start | bytes 98308
  1138.0 80.3 %copy-start.176 = (f32[256]{0:T(256)S(1)}, f32[256]{0:T(256)}, u32[]{:S(2)}) copy-start(f32[256]{0:T(256)} %copy-done.175) | copy-start | bytes 3076
  1138.1 80.3 %copy-start.183 = (f32[256]{0:T(256)S(1)}, f32[256]{0:T(256)}, u32[]{:S(2)}) copy-start(f32[256]{0:T(256)} %add_rsqrt_fusion.3) | copy-start | bytes 3076
  1140.2 81.2 %slice-start.4 = ((s8[7077888]{0:T(1024)(128)(4,1)}), s8[2883584]{0:T(1024)(128)(4,1)S(1)}, s32[]{:S(2)}) async-start(s8[7077888]{0:T(1024)(128)(4,1)} %bitcast.625), calls=%async_computation.41 | async-start | bytes 5767168
  1230.0 490.7 %all-reduce.15.cloned.1.call-start = ((), (), s32[]{:S(2)}) async-start(), calls=%async_computation.36 | async-start | bytes 14155776 | tf_op jit(solution)/shard_map/psum | solution.py:139
  (224 other events, 1199.5 us)
Sparse Core Ops, SparseCore 0:
  9.6 33.4 all-gather.17
  44.6 37.5 all-gather.27
  84.4 43.9 all-gather.19
  130.3 44.1 all-gather.21
  175.9 15.6 all-gather.23
  193.0 37.4 all-gather.25
  232.7 44.2 all-gather.29
  279.1 43.0 all-gather.33
  324.2 44.0 all-gather.31
  371.8 73.4 reduce-scatter.12
  449.3 44.4 all-gather.35
  585.5 73.2 reduce-scatter.16
  661.5 43.0 all-gather.37
  706.4 44.0 all-gather.39
  754.0 73.3 reduce-scatter.14
  830.8 74.0 reduce-scatter.18
  908.4 74.0 reduce-scatter.22
  985.9 74.1 reduce-scatter.26
  1063.7 74.2 reduce-scatter.20
  1141.5 74.2 reduce-scatter.24
  1218.9 32.1 reduce-scatter.30
  1253.8 78.4 reduce-scatter.32
  1335.1 78.4 reduce-scatter.34
  1416.1 63.6 reduce-scatter.28
  1484.2 236.4 all-reduce.14
where the time goes:
time: 1750 us; the launch traced here: 1730 us
  waiting for transfers between devices  933 us (53%)
  matrix products  280 us (16%)
  local copies, waits for them, and re-layouts  230 us (13%)
  other arithmetic  144 us (8%)
  blocking collectives  123 us (7%)
  between operations  19.6 us (1%)
    reduce_scatter x4, waiting for transfers between devices, body(): lax.psum_scatter(key_grad_all[:seq_len], 'ctx', scatter_dimension=0, tile...  269 us
    psum x1, waiting for transfers between devices, reduce_grads(): lax.psum((shards[0], shards[1], shards[2], shards[3], shards[4], shards[5...  186 us
    all_gather x4, waiting for transfers between devices, body(): lax.all_gather(keys[local_rows:], 'ctx', axis=0, tiled=True)  99.5 us
    reduce_scatter x4, waiting for transfers between devices, body(): lax.psum_scatter(value_grad_all[:seq_len], 'ctx', scatter_dimension=0, ti...  84.3 us
    reduce_scatter x1, waiting for transfers between devices, reduce_grads(): lax.psum_scatter(grads[7], 'fsdp', scatter_dimension=0, tiled=True)  81.3 us
    reduce_scatter x1, waiting for transfers between devices, reduce_grads(): lax.psum_scatter(grads[5], 'fsdp', scatter_dimension=0, tiled=True)  81.3 us
    all_gather x4, blocking collectives, body(): lax.all_gather(doc_local.astype(jnp.bfloat16), 'ctx', axis=0, tiled=True)  73.6 us
    reduce_scatter x1, waiting for transfers between devices, reduce_grads(): lax.psum_scatter(grads[2], 'fsdp', scatter_dimension=0, tiled=True)  66.2 us
  transfers between devices with their start and end apart: 25, of which 18 were waited for; matrix products, arithmetic and copies ran while one was open for 31% of the time, Pallas kernels for 0%

commit v1 on v0

--- a/solution.py
+++ b/solution.py
@@ -3,6 +3,8 @@
 import jax
 import jax.numpy as jnp
 from jax import lax
+from jax.experimental import pallas as pl
+from jax.experimental.pallas import tpu as pltpu
 from jax.sharding import PartitionSpec as P
 
 D = 768
@@ -156,7 +158,7 @@
     return tuple((left_item + right_item for left_item, right_item in zip(left_items, right_items)))
 
 
-def body(
+def general_body(
     clean_in,
     segments,
     noise,
@@ -339,6 +341,392 @@
     )
 
 
+PAIR=2*HEAD; PAIRS=D//PAIR
+NEG=-1e30
+VMEM_LIMIT=60<<20
+F32=jnp.float32; BF=jnp.bfloat16
+
+def dot_nn(a,b): return lax.dot_general(a,b,(((1,),(0,)),((),())),preferred_element_type=F32)
+def dot_nt(a,b): return lax.dot_general(a,b,(((1,),(1,)),((),())),preferred_element_type=F32)
+def dot_tn(a,b): return lax.dot_general(a,b,(((0,),(0,)),((),())),preferred_element_type=F32)
+
+def tiles_of(half):
+    return [(s,min(128,half-s)) for s in range(0,half,128)]
+
+def norm_rows(rows):
+    centre=rows-jnp.mean(rows,axis=-1,keepdims=True)
+    scale=lax.rsqrt(jnp.mean(centre*centre,axis=-1,keepdims=True)+EPS)
+    return centre*scale, scale
+
+def swap_halves(z):
+    lane=lax.broadcasted_iota(jnp.int32,z.shape,1)
+    low=(lane & (HEAD-1)) < HEAD//2
+    return jnp.where(low,pltpu.roll(z,PAIR-HEAD//2,1),pltpu.roll(z,HEAD//2,1))
+
+def head_stack(z):
+    lane=lax.broadcasted_iota(jnp.int32,z.shape,1)
+    first=lane<HEAD
+    zero=jnp.zeros_like(z)
+    return jnp.concatenate([jnp.where(first,z,zero),jnp.where(first,zero,z)],axis=0)
+
+def head_merge(z):
+    n=z.shape[0]//2
+    lane=lax.broadcasted_iota(jnp.int32,(n,z.shape[1]),1)
+    return jnp.where(lane<HEAD,z[:n],z[n:])
+
+def layer_rows(xc_ref,noise_ref,emb_ref):
+    clean=xc_ref[...].astype(F32)
+    noisy=jnp.where(noise_ref[...]==1,emb_ref[...].astype(F32),clean)
+    return noisy,clean
+
+def fwd_attn_kernel(half,xc,noise,segc,segr,emb,gain,wq,wk,wv,wout,cos,sin,
+                    q_o,k_o,v_o,mix_o,lse_o,x1_o,h_s,bias_s,self_s,mix_s):
+    p=pl.program_id(0)
+    tiles=tiles_of(half)
+    @pl.when(p==0)
+    def _():
+        g=gain[...].astype(F32)
+        for c,rows in enumerate(layer_rows(xc,noise,emb)):
+            x1_o[c*half:(c+1)*half]=rows
+            n,_=norm_rows(rows)
+            h_s[c*half:(c+1)*half]=(n*g).astype(BF)
+        for s,m in tiles:
+            n=s+m
+            qb=(lax.broadcasted_iota(jnp.int32,(m,n),0)+s)//BLK
+            kb=lax.broadcasted_iota(jnp.int32,(m,n),1)//BLK
+            same=segc[s:n]==segr[:,:n]
+            bias_s[0,s:n,:n]=jnp.where(same&(kb<qb),0.0,NEG)
+            bias_s[1,s:n,:n]=jnp.where(same&(kb<=qb),0.0,NEG)
+            qb=lax.broadcasted_iota(jnp.int32,(m,m),0)//BLK
+            kb=lax.broadcasted_iota(jnp.int32,(m,m),1)//BLK
+            same=segc[s:n]==segr[:,s:n]
+            self_s[s:n,:m]=jnp.where(same&(kb==qb),0.0,NEG)
+    h=h_s[...]
+    cs=jnp.concatenate([cos[...],cos[...]],axis=0)
+    sn=jnp.concatenate([sin[...],sin[...]],axis=0)
+    z=dot_nn(h,wq[...]); q_o[...]=((z*cs+swap_halves(z)*sn).astype(BF)*BF(HEAD**-0.5)).astype(BF)
+    z=dot_nn(h,wk[...]); k_o[...]=(z*cs+swap_halves(z)*sn).astype(BF)
+    v_o[...]=dot_nn(h,wv[...]).astype(BF)
+    idx=0
+    for s,m in tiles:
+        n=s+m
+        for c in (0,1):
+            qs=head_stack(q_o[c*half+s:c*half+n])
+            kc=k_o[half:half+n]; vc=v_o[half:half+n]
+            sc=dot_nt(qs,kc).reshape(2,m,n)+bias_s[c,s:n,:n][None]
+            top=jnp.max(sc,axis=-1,keepdims=True)
+            if c==0:
+                ss=dot_nt(qs,k_o[s:n]).reshape(2,m,m)+self_s[s:n,:m][None]
+                top=jnp.maximum(top,jnp.max(ss,axis=-1,keepdims=True))
+            w=jnp.exp(sc-top); tot=jnp.sum(w,axis=-1,keepdims=True)
+            o=dot_nn(w.astype(BF).reshape(2*m,n),vc)
+            if c==0:
+                w2=jnp.exp(ss-top); tot=tot+jnp.sum(w2,axis=-1,keepdims=True)
+                o=o+dot_nn(w2.astype(BF).reshape(2*m,m),v_o[s:n])
+            tot=tot.reshape(2*m,1)
+            o=o*(1.0/tot)
+            mx=head_merge(o).astype(BF)
+            mix_o[c*half+s:c*half+n]=mx
+            mix_s[p,c*half+s:c*half+n]=mx
+            lse=top.reshape(2*m,1)+jnp.log(tot)
+            lse_o[0,idx:idx+1,:2*m]=jnp.broadcast_to(lse,(2*m,128)).T[0:1]
+            idx+=1
+    @pl.when(p==pl.num_programs(0)-1)
+    def _():
+        full=jnp.concatenate([mix_s[i] for i in range(PAIRS)],axis=1)
+        x1_o[...]=x1_o[...]+dot_nn(full,wout[...])
+
+def whole(shape): return pl.BlockSpec(shape,lambda *i:(0,)*len(shape))
+
+def fwd_attn(xc,noise,segc,segr,emb,gain,wqkv,wout,cos,sin):
+    half=xc.shape[0]; R=2*half
+    nt=len(tiles_of(half))*2; ntp=-(-nt//8)*8
+    ws=[pl.BlockSpec((D,PAIR),(lambda off:(lambda p:(0,off+p)))(o*PAIRS)) for o in range(3)]
+    rows=pl.BlockSpec((R,PAIR),lambda p:(0,p))
+    return pl.pallas_call(partial(fwd_attn_kernel,half),grid=(PAIRS,),
+        in_specs=[whole((half,D)),whole((half,1)),whole((half,1)),whole((1,half)),whole((1,D)),whole((1,D)),*ws,whole((D,D)),whole((half,PAIR)),whole((half,PAIR))],
+        out_specs=[rows,rows,rows,rows,pl.BlockSpec((1,ntp,256),lambda p:(p,0,0)),whole((R,D))],
+        out_shape=[jax.ShapeDtypeStruct((R,D),BF)]*4+[jax.ShapeDtypeStruct((PAIRS,ntp,256),F32),jax.ShapeDtypeStruct((R,D),F32)],
+        scratch_shapes=[pltpu.VMEM((R,D),BF),pltpu.VMEM((2,half,half),F32),pltpu.VMEM((half,128),F32),pltpu.VMEM((PAIRS,R,PAIR),BF)],
+        compiler_params=pltpu.CompilerParams(vmem_limit_bytes=VMEM_LIMIT,dimension_semantics=("arbitrary",)),
+        cost_estimate=pl.CostEstimate(flops=2*R*D*(3*D+D)+24*R*half*D//2*2,bytes_accessed=16<<20,transcendentals=R*half*HEADS),
+        name="fwd_attn")(xc,noise,segc,segr,emb,gain,wqkv,wqkv,wqkv,wout,cos,sin)
+
+GC=(2.0/3.141592653589793)**0.5
+def ffn_fwd_kernel(x1,gain,wup,bup,wdn,bdn,out_o,act_o,dg_o,h_s,acc):
+    j=pl.program_id(0)
+    @pl.when(j==0)
+    def _():
+        n,_=norm_rows(x1[...])
+        h_s[...]=(n*gain[...].astype(F32)).astype(BF)
+        acc[...]=x1[...]+bdn[...].astype(F32)
+    R=h_s.shape[0]; ch=R//3
+    for i in range(3):
+        r=slice(i*ch,(i+1)*ch)
+        u=dot_nn(h_s[r],wup[...])+bup[...].astype(F32)
+        u2=u*u
+        t=jnp.tanh(GC*(u+0.044715*u*u2))
+        a=0.5*(1.0+t)
+        act=(u*a).astype(BF)
+        act_o[r]=act
+        dg_o[r]=(a+0.5*u*(1.0-t*t)*(GC*(1.0+3*0.044715*u2))).astype(BF)
+        acc[r]+=dot_nn(act,wdn[...])
+    @pl.when(j==pl.num_programs(0)-1)
+    def _(): out_o[...]=acc[...].astype(BF)
+
+def ffn_fwd(x1,gain,wup,bup,wdn,bdn,tile=512):
+    R=x1.shape[0]
+    return pl.pallas_call(ffn_fwd_kernel,grid=(FF//tile,),
+        in_specs=[whole((R,D)),whole((1,D)),pl.BlockSpec((D,tile),lambda j:(0,j)),pl.BlockSpec((1,tile),lambda j:(0,j)),pl.BlockSpec((tile,D),lambda j:(j,0)),whole((1,D))],
+        out_specs=[whole((R,D)),pl.BlockSpec((R,tile),lambda j:(0,j)),pl.BlockSpec((R,tile),lambda j:(0,j))],
+        out_shape=[jax.ShapeDtypeStruct((R,D),BF),jax.ShapeDtypeStruct((R,FF),BF),jax.ShapeDtypeStruct((R,FF),BF)],
+        scratch_shapes=[pltpu.VMEM((R,D),BF),pltpu.VMEM((R,D),F32)],
+        compiler_params=pltpu.CompilerParams(vmem_limit_bytes=VMEM_LIMIT,dimension_semantics=("arbitrary",)),
+        cost_estimate=pl.CostEstimate(flops=4*R*D*FF,bytes_accessed=30<<20,transcendentals=R*FF),
+        name="ffn_fwd")(x1,gain,wup,bup,wdn,bdn)
+
+def ffn_bwd_kernel(x1,gain,gy,act,dg,wup,wdn,dwup_o,dwdn_o,dbup_o,dbdn_o,dgain_o,gx1_o,ga_o,hT_s,gh):
+    j=pl.program_id(0)
+    @pl.when(j==0)
+    def _():
+        n,_=norm_rows(x1[...])
+        hT_s[...]=(n*gain[...].astype(F32)).astype(BF).T
+        gh[...]=jnp.zeros_like(gh)
+        dbdn_o[...]=jnp.sum(gy[...].astype(F32),axis=0,keepdims=True)
+    ga=dot_nt(gy[...],wdn[...])
+    gu=(dg[...].astype(F32)*ga).astype(BF)
+    dwdn_o[...]=dot_tn(act[...],gy[...]).astype(BF)
+    dwup_o[...]=dot_nn(hT_s[...],gu).astype(BF)
+    dbup_o[...]=jnp.sum(gu.astype(F32),axis=0,keepdims=True)
+    gh[...]+=dot_nt(gu,wup[...])
+    @pl.when(j==pl.num_programs(0)-1)
+    def _():
+        n,scale=norm_rows(x1[...])
+        g2=gh[...]
+        dgain_o[...]=jnp.sum(g2*n,axis=0,keepdims=True)
+        e=g2*gain[...].astype(F32)
+        gx=gy[...].astype(F32)+scale*(e-jnp.mean(e,axis=-1,keepdims=True)-n*jnp.mean(e*n,axis=-1,keepdims=True))
+        gx1_o[...]=gx
+        ga_o[...]=gx.astype(BF)
+
+def ffn_bwd(x1,gain,gy,act,dg,wup,wdn,tile=512):
+    R=x1.shape[0]
+    col=pl.BlockSpec((R,tile),lambda j:(0,j))
+    return pl.pallas_call(ffn_bwd_kernel,grid=(FF//tile,),
+        in_specs=[whole((R,D)),whole((1,D)),whole((R,D)),col,col,pl.BlockSpec((D,tile),lambda j:(0,j)),pl.BlockSpec((tile,D),lambda j:(j,0))],
+        out_specs=[pl.BlockSpec((D,tile),lambda j:(0,j)),pl.BlockSpec((tile,D),lambda j:(j,0)),pl.BlockSpec((1,tile),lambda j:(0,j)),whole((1,D)),whole((1,D)),whole((R,D)),whole((R,D))],
+        out_shape=[jax.ShapeDtypeStruct((D,FF),BF),jax.ShapeDtypeStruct((FF,D),BF),jax.ShapeDtypeStruct((1,FF),F32),jax.ShapeDtypeStruct((1,D),F32),jax.ShapeDtypeStruct((1,D),F32),jax.ShapeDtypeStruct((R,D),F32),jax.ShapeDtypeStruct((R,D),BF)],
+        scratch_shapes=[pltpu.VMEM((D,R),BF),pltpu.VMEM((R,D),F32)],
+        compiler_params=pltpu.CompilerParams(vmem_limit_bytes=VMEM_LIMIT,dimension_semantics=("arbitrary",)),
+        cost_estimate=pl.CostEstimate(flops=8*R*D*FF,bytes_accessed=40<<20,transcendentals=0),
+        name="ffn_bwd")(x1,gain,gy,act,dg,wup,wdn)
+
+def bwd_attn_kernel(half,xc,noise,segc,segr,emb,gain,gx1,ga,q,k,v,mix,lse,wq,wk,wv,wout,cos,sin,
+                    dw_o,dwout_o,gin_o,demb_o,dgain_o,hT_s,gh,biasT_s,selfT_s,dq_s,dk_s,dv_s):
+    p=pl.program_id(0)
+    R=2*half
+    tiles=tiles_of(half)
+    @pl.when(p==0)
+    def _():
+        g=gain[...].astype(F32)
+        for c,rows in enumerate(layer_rows(xc,noise,emb)):
+            n,_=norm_rows(rows)
+            hT_s[:,c*half:(c+1)*half]=(n*g).astype(BF).T
+        gh[...]=jnp.zeros_like(gh)
+        for s,m in tiles:
+            n=s+m
+            qb=(lax.broadcasted_iota(jnp.int32,(n,m),1)+s)//BLK
+            kb=lax.broadcasted_iota(jnp.int32,(n,m),0)//BLK
+            same=segc[:n]==segr[:,s:n]
+            biasT_s[0,:n,s:n]=jnp.where(same&(kb<qb),0.0,NEG)
+            biasT_s[1,:n,s:n]=jnp.where(same&(kb<=qb),0.0,NEG)
+            qb=lax.broadcasted_iota(jnp.int32,(m,m),1)//BLK
+            kb=lax.broadcasted_iota(jnp.int32,(m,m),0)//BLK
+            same=segc[s:n]==segr[:,s:n]
+            selfT_s[s:n,:m]=jnp.where(same&(kb==qb),0.0,NEG)
+    gm=dot_nt(ga[...],wout[...]).astype(BF)
+    dwout_o[...]=dot_tn(mix[...],ga[...]).astype(BF)
+    gd=gm.astype(F32)*mix[...].astype(F32)
+    dk_s[...]=jnp.zeros_like(dk_s); dv_s[...]=jnp.zeros_like(dv_s)
+    idx=0
+    for s,m in tiles:
+        n=s+m
+        for c in (0,1):
+            rs=slice(c*half+s,c*half+n)
+            qs=head_stack(q[rs]); gs=head_stack(gm[rs])
+            delta=jnp.sum(head_stack(gd[rs]).T,axis=0,keepdims=True)
+            row=lse[0,idx:idx+1,:2*m]
+            def part(krows,bias):
+                kc=k[krows]; vc=v[krows]
+                st=dot_nt(kc,qs)+jnp.concatenate([bias,bias],axis=1)
+                pt=jnp.exp(st-row)
+                dp=dot_nt(vc,gs)
+                ds=(pt*(dp-delta)).astype(BF)
+                dv_s[krows]+=dot_nn(pt.astype(BF),gs)
+                dk_s[krows]+=dot_nn(ds,qs)
+                return dot_tn(ds,kc)
+            dq=part(slice(half,half+n),biasT_s[c,:n,s:n])
+            if c==0: dq=dq+part(slice(s,n),selfT_s[s:n,:m])
+            dq_s[rs]=head_merge(dq)*HEAD**-0.5
+            idx+=1
+    cs=jnp.concatenate([cos[...],cos[...]],axis=0)
+    sn=jnp.concatenate([sin[...],sin[...]],axis=0)
+    total=None
+    for i,(g,w) in enumerate(((dq_s,wq),(dk_s,wk),(dv_s,wv))):
+        z=g[...]
+        if i<2: z=z*cs-swap_halves(z)*sn
+        z=z.astype(BF)
+        dw_o[i]=dot_nn(hT_s[...],z).astype(BF)
+        gh[...]+=dot_nt(z,w[...])
+    @pl.when(p==pl.num_programs(0)-1)
+    def _():
+        g=gain[...].astype(F32)
+        outs=[]; dg=0.0
+        for c,rows in enumerate(layer_rows(xc,noise,emb)):
+            n,scale=norm_rows(rows)
+            g1=gh[c*half:(c+1)*half]
+            dg=dg+jnp.sum(g1*n,axis=0,keepdims=True)
+            e=g1*g
+            outs.append(gx1[c*half:(c+1)*half]+scale*(e-jnp.mean(e,axis=-1,keepdims=True)-n*jnp.mean(e*n,axis=-1,keepdims=True)))
+        masked=noise[...]==1
+        gin_o[...]=(outs[1]+jnp.where(masked,0.0,outs[0])).astype(gin_o.dtype)
+        demb_o[...]=jnp.sum(jnp.where(masked,outs[0],0.0),axis=0,keepdims=True)
+        dgain_o[...]=dg
+
+def bwd_attn(xc,noise,segc,segr,emb,gain,gx1,ga,q,k,v,mix,lse,wqkv,wout,cos,sin):
+    half=xc.shape[0]; R=2*half
+    ntp=lse.shape[1]
+    ws=[pl.BlockSpec((D,PAIR),(lambda off:(lambda p:(0,off+p)))(o*PAIRS)) for o in range(3)]
+    rows=pl.BlockSpec((R,PAIR),lambda p:(0,p))
+    return pl.pallas_call(partial(bwd_attn_kernel,half),grid=(PAIRS,),
+        in_specs=[whole((half,D)),whole((half,1)),whole((half,1)),whole((1,half)),whole((1,D)),whole((1,D)),whole((R,D)),whole((R,D)),rows,rows,rows,rows,
+                  pl.BlockSpec((1,ntp,256),lambda p:(p,0,0)),*ws,pl.BlockSpec((PAIR,D),lambda p:(p,0)),whole((half,PAIR)),whole((half,PAIR))],
+        out_specs=[pl.BlockSpec((3,D,PAIR),lambda p:(0,0,p)),pl.BlockSpec((PAIR,D),lambda p:(p,0)),whole((half,D)),whole((1,D)),whole((1,D))],
+        out_shape=[jax.ShapeDtypeStruct((3,D,D),BF),jax.ShapeDtypeStruct((D,D),BF),jax.ShapeDtypeStruct((half,D),BF),jax.ShapeDtypeStruct((1,D),F32),jax.ShapeDtypeStruct((1,D),F32)],
+        scratch_shapes=[pltpu.VMEM((D,R),BF),pltpu.VMEM((R,D),F32),pltpu.VMEM((2,half,-(-half//128)*128),F32),pltpu.VMEM((half,128),F32)]+[pltpu.VMEM((R,PAIR),F32)]*3,
+        compiler_params=pltpu.CompilerParams(vmem_limit_bytes=VMEM_LIMIT,dimension_semantics=("arbitrary",)),
+        cost_estimate=pl.CostEstimate(flops=4*R*D*(3*D+D)+60*R*half*D//2*2,bytes_accessed=30<<20,transcendentals=R*half*HEADS),
+        name="bwd_attn")(xc,noise,segc,segr,emb,gain,gx1,ga,q,k,v,mix,lse,wqkv,wqkv,wqkv,wout,cos,sin)
+
+
+def flip(values, axis, count, bit):
+    return lax.ppermute(values, axis, [(i, i ^ bit) for i in range(count)])
+
+
+def pick(values, index, axis):
+    return lax.dynamic_index_in_dim(values, index, axis, keepdims=False)
+
+
+def order_two(mine, other, index, axis):
+    return jnp.where(index == 0, jnp.stack([mine, other], axis), jnp.stack([other, mine], axis))
+
+
+def gather_rows(shard, core, chip):
+    near = order_two(shard, flip(shard, "fsdp", 4, 2), chip, 0)
+    full = order_two(near, flip(near, "fsdp", 4, 1), core, 1)
+    return full.reshape((4 * shard.shape[0],) + shard.shape[1:])
+
+
+def halve(values, index, axis, mesh_axis, count, bit):
+    received = flip(pick(values, 1 - index, axis), mesh_axis, count, bit)
+    kept = pick(values, index, axis)
+    return (kept.astype(F32) + received.astype(F32)).astype(BF)
+
+
+def reduce_shard(grad, lead, core, chip, ranks):
+    rows, cols = grad.shape[-2] // 4, grad.shape[-1]
+    axis = len(lead)
+    part = grad.reshape(lead + (2, 2, rows, cols))
+    part = halve(part, core, axis + 1, "fsdp", 4, 1)
+    part = halve(part, chip, axis, "fsdp", 4, 2)
+    shape = part.shape
+    for level in range(3):
+        size = part.shape[-2] // 2
+        part = halve(part.reshape(lead + (2, size, cols)), ranks[level], axis, "ctx", 8, 1 << level)
+    for level in (2, 1, 0):
+        size = part.shape[-2]
+        other = flip(part, "ctx", 8, 1 << level)
+        part = order_two(part, other, ranks[level], axis).reshape(lead + (2 * size, cols))
+    return part.reshape(shape).astype(F32)
+
+
+def to_unit(blocks, part, fill):
+    extra = flip(blocks[7], "ctx", 8, 1)[None]
+    pads = jnp.full((2,) + blocks.shape[1:], fill, blocks.dtype)
+    first = jnp.concatenate([blocks, extra], axis=0)
+    second = jnp.concatenate([blocks[6::-1], pads], axis=0)
+    return jnp.where(part == 0, first, second)
+
+
+def from_unit(pieces, part):
+    extra = flip(pieces[8], "ctx", 8, 1)[None]
+    second = jnp.concatenate([pieces[6::-1], extra], axis=0)
+    return jnp.where(part == 0, pieces[:8], second)
+
+
+def exchange(blocks):
+    return lax.all_to_all(blocks, "ctx", 0, 0)
+
+
+def even_body(clean_in, segments, noise, mask_embed, norm1_gain, qkv_weight, out_weight, norm2_gain, up_weight, up_bias,
+              down_weight, down_bias, out_grad):
+    rank = lax.axis_index("ctx")
+    place = lax.axis_index("fsdp")
+    core, chip = place & 1, place >> 1
+    part = rank & 1
+    ranks = (rank & 1, (rank >> 1) & 1, rank >> 2)
+    piece = clean_in.shape[2]
+    half = 9 * piece
+    meta = jnp.concatenate([segments.reshape(8, piece), noise.reshape(8, piece)], axis=1)
+    clean = to_unit(exchange(clean_in.reshape(8, piece, D)), part, 0).reshape(half, D)
+    meta = exchange(meta)
+    seg = to_unit(meta[:, :piece], part, -1).reshape(half)
+    mask = to_unit(meta[:, piece:], part, 0).reshape(half, 1)
+    qkv_full = gather_rows(qkv_weight, core, chip)
+    out_full = gather_rows(out_weight, core, chip)
+    small = jnp.concatenate([mask_embed, norm1_gain, norm2_gain, down_bias, up_bias])
+    small = lax.all_gather(small, "fsdp", axis=0).reshape(4, -1)
+    width = mask_embed.shape[0]
+    embed, gain_one, gain_two, down_shift = (small[:, i * width:(i + 1) * width].reshape(1, D) for i in range(4))
+    up_shift = small[:, 4 * width:].reshape(1, FF)
+    up_full = gather_rows(up_weight, core, chip)
+    down_full = gather_rows(down_weight, core, chip)
+    cotangent = exchange(out_grad.transpose(0, 2, 1, 3, 4).reshape(8, 2, piece, D))
+    cotangent = to_unit(cotangent, part, 0).transpose(1, 0, 2, 3).reshape(2 * half, D)
+
+    cos_part, sin_part = rope_tables(part * half + jnp.arange(half, dtype=jnp.int32))
+    cosine = jnp.tile(cos_part, (1, 4))
+    sine = jnp.tile(jnp.concatenate([-sin_part, sin_part], axis=1), (1, 2))
+    seg_col, seg_row = seg[:, None], seg[None, :]
+
+    q, k, v, mixed, lse, resid = fwd_attn(clean, mask, seg_col, seg_row, embed, gain_one, qkv_full, out_full, cosine, sine)
+    result, active, slope = ffn_fwd(resid, gain_two, up_full, up_shift, down_full, down_shift)
+    up_grad, down_grad, up_shift_grad, down_shift_grad, gain_two_grad, grad_resid, grad_attn = ffn_bwd(
+        resid, gain_two, cotangent, active, slope, up_full, down_full)
+    block_out = from_unit(result.reshape(2, 9, piece, D).transpose(1, 0, 2, 3), part)
+    block_out = exchange(block_out).reshape(4, 2, 2, piece, D).transpose(0, 2, 1, 3, 4)
+    qkv_grad, out_weight_grad, grad_in, embed_grad, gain_one_grad = bwd_attn(
+        clean, mask, seg_col, seg_row, embed, gain_one, grad_resid, grad_attn, q, k, v, mixed, lse, qkv_full, out_full,
+        cosine, sine)
+    input_grad = exchange(from_unit(grad_in.reshape(9, piece, D), part)).reshape(4, 2, piece, D).astype(F32)
+
+    down_sum = reduce_shard(down_grad, (), core, chip, ranks)
+    up_sum = reduce_shard(up_grad, (), core, chip, ranks)
+    out_sum = reduce_shard(out_weight_grad, (), core, chip, ranks)
+    qkv_sum = reduce_shard(qkv_grad, (3,), core, chip, ranks)
+    qkv_sum = jnp.concatenate([qkv_sum[0], qkv_sum[1], qkv_sum[2]], axis=1)
+    sums = jnp.concatenate([x.reshape(-1) for x in (embed_grad, gain_one_grad, gain_two_grad, down_shift_grad, up_shift_grad)])
+    sums = lax.psum(sums, ("ctx", "fsdp"))
+    own = [lax.dynamic_slice_in_dim(sums, i * D + place * width, width) for i in range(4)]
+    own_up = lax.dynamic_slice_in_dim(sums, 4 * D + place * (FF // 4), FF // 4)
+    return (block_out, input_grad, own[0], own[1], qkv_sum, out_sum, own[2], up_sum, own_up, down_sum, own[3])
+
+
+def choose_body(axes, *arrays):
+    even = axes["ctx"] == 8 and axes["fsdp"] == 4 and arrays[0].shape[0] == 4
+    return (even_body if even else general_body)(*arrays)
+
+
 def solution(mesh):
     placed = (
         P("fsdp", None, "ctx", None),
@@ -356,7 +744,7 @@
         P("fsdp", None, None, "ctx", None),
     )
     return jax.shard_map(
-        body,
+        partial(choose_body, dict(mesh.shape)),
         mesh=mesh,
         in_specs=placed,
         out_specs=(

time: 1750 us -> 600 us (0.34)
  waiting for transfers between devices: 933 us -> 132 us
  matrix products: 280 us -> 0 us
  local copies, waits for them, and re-layouts: 230 us -> 47.5 us
  Pallas kernels: 0 us -> 161 us
  other arithmetic: 144 us -> 71.5 us
  starting transfers between devices: 2.13 us -> 65.2 us
  between operations: 19.6 us -> 1.82 us
    reduce_scatter x12 -> x0, waiting for transfers between devices: 589 us -> none  [the longest x4 269 us: body(): lax.psum_scatter(key_grad_all[:seq_len], 'ctx', scatter_dimension=0, tile...]
    dot_general x132 -> x0, matrix products: 280 us -> none  [the longest x24 35.2 us: masked_scores(): jnp.einsum('qhd,khd->hqk', query_heads, key_heads, preferred_element_type...]
    psum x1 -> x0, waiting for transfers between devices: 186 us -> none  [reduce_grads(): lax.psum((shards[0], shards[1], shards[2], shards[3], shards[4], shards[5...]
    pallas_call x0 -> x4, Pallas kernels: none -> 161 us  [the longest x1 59.2 us: bwd_attn(): pl.pallas_call(partial(bwd_attn_kernel, half), grid=(PAIRS,), in_specs=[w...]
    all_gather x12 -> x0, waiting for transfers between devices: 155 us -> none  [the longest x4 99.5 us: body(): lax.all_gather(keys[local_rows:], 'ctx', axis=0, tiled=True)]
    ppermute x0 -> x46, waiting for transfers between devices: none -> 121 us  [flip(): return lax.ppermute(values, axis, [(i, i ^ bit) for i in range(count)])]
    slice x34 -> x10, local copies, waits for them, and re-layouts: 65.5 us -> 4.34 us  [the longest x3 2.15 us: to_unit(): second = jnp.concatenate([blocks[6::-1], pads], axis=0)]
    dynamic_slice x72 -> x2, local copies, waits for them, and re-layouts: 54.5 us -> 2.13 us  [the longest x1 1.46 us: even_body(): lax.dynamic_slice_in_dim(sums, i * D + place * width, width)]
  transfers between devices with their start and end apart: 25 -> 51, of which waited for: 18 -> 23; matrix products, arithmetic and copies ran while one was open for 31% -> 17% of each run, Pallas kernels for 0% -> 7%
where the time goes in v1:
time: 600 us; the launch traced here: 596 us
  Pallas kernels  161 us (27%)
  waiting for transfers between devices  132 us (22%)
  blocking collectives  116 us (19%)
  other arithmetic  71.5 us (12%)
  starting transfers between devices  65.2 us (11%)
  local copies, waits for them, and re-layouts  47.5 us (8%)
    ppermute x46, waiting for transfers between devices, flip(): return lax.ppermute(values, axis, [(i, i ^ bit) for i in range(count)])  121 us
    all_gather x1, blocking collectives, even_body(): small = lax.all_gather(small, 'fsdp', axis=0).reshape(4, -1)  71.7 us
    pallas_call x1, Pallas kernels, bwd_attn(): pl.pallas_call(partial(bwd_attn_kernel, half), grid=(PAIRS,), in_specs=[w...  59.2 us
    psum x1, blocking collectives, even_body(): sums = lax.psum(sums, ('ctx', 'fsdp'))  44.3 us
    pallas_call x1, Pallas kernels, fwd_attn(): pl.pallas_call(partial(fwd_attn_kernel, half), grid=(PAIRS,), in_specs=[w...  41.7 us
    ppermute x46, starting transfers between devices, flip(): return lax.ppermute(values, axis, [(i, i ^ bit) for i in range(count)])  39.9 us
    select_n x23, other arithmetic, order_two(): jnp.where(index == 0, jnp.stack([mine, other], axis), jnp.stack([other, m...  39.8 us
    pallas_call x1, Pallas kernels, ffn_bwd(): pl.pallas_call(ffn_bwd_kernel, grid=(FF // tile,), in_specs=[whole((R, D)...  36.1 us
  transfers between devices with their start and end apart: 51, of which 23 were waited for; matrix products, arithmetic and copies ran while one was open for 17% of the time, Pallas kernels for 7%

profile of v1, /device:TPU:0, one launch (start us, length us, event | category | flops | bytes accessed | tf_op | source)
XLA Modules:
  0.0 595.5 jit_solution(6446481361681116849)
XLA Ops:
  2.0 7.3 %all-to-all-start.1 = ((s32[8,1,128]{2,1,0:T(1,128)}), s32[8,1,128]{2,1,0:T(1,128)S(1)}, u32[]{:S(2)}, u32[]{:S(2)}) async-start(s32[8,1,128]{2,1,0:T(1,128)} %bitcast.6), calls=%async_computation.1 | async-start | bytes 8192 | tf_op jit(solution)/shard_map/all_to_all | solution.py:668
  13.3 3.4 concatenate.108
  16.8 71.7 %all-gather.1 = bf16[4,1,1536]{2,1,0:T(2,128)(2,1)S(1)} all-gather(bf16[1,1,1536]{2,1,0:T(2,128)(2,1)S(1)} %reshape.764), channel_id=2, replica_groups=mesh['ctx'=8,'fsdp'=4] {'fsdp'}, dimensions={0}, use_global_device_ids=true | all-gather | bytes 15360 | tf_op jit(solution)/shard_map/all_gather | solution.py:688
  92.8 5.7 all-to-all-start
  113.5 5.7 all-to-all-done
  120.1 3.8 all-to-all-start.3
  127.7 2.5 maximum_select_fusion.10
  130.2 3.5 maximum_select_fusion.4
  133.9 3.4 maximum_select_fusion.6
  137.6 3.5 maximum_select_fusion.3
  143.2 3.4 maximum_select_fusion.5
  151.8 4.0 maximum_select_fusion.2
  155.8 5.3 all-to-all-done.3
  162.6 41.7 %fwd_attn.1 = (bf16[1152,768]{1,0:T(8,128)(2,1)}, bf16[1152,768]{1,0:T(8,128)(2,1)}, bf16[1152,768]{1,0:T(8,128)(2,1)}, bf16[1152,768]{1,0:T(8,128)(2,1)}, f32[6,16,256]{2,1,0:T(8,128)}, /*index=5*/f32[1152,768]{1,0:T(8,128)}) custom-call(bf16[576,768]{1,0:T(8,128)(2,1)} %bitcast.313, s32[576,1]{1,0:T(8,128)} %reshape.767.noise, ...), custom_call_target="tpu_custom_call" | custom-call | flops 17666408448 | bytes 16777216 | tf_op jit(solution)/shard_map/fwd_attn/pallas_call | solution.py:446
  209.5 5.8 maximum_select_fusion
  215.4 5.6 maximum_select_fusion.1
  221.0 24.2 %ffn_fwd.1 = (bf16[1152,768]{1,0:T(8,128)(2,1)}, bf16[1152,3072]{1,0:T(8,128)(2,1)}, bf16[1152,3072]{1,0:T(8,128)(2,1)}) custom-call(f32[1152,768]{1,0:T(8,128)} %get-tuple-element.32.x1, bf16[1,768]{1,0:T(2,128)(2,1)} %reshape.711.gain, bf16[768,3072]{1,0:T(8,128)(2,1)} %bitcast.250, bf16[1,3072]{1,0:T(2,128)(2,1)} %bitcast.348, ...), custom_call_target="tpu_custom_call" | custom-call | flops 10871635968 | bytes 31457280 | tf_op jit(solution)/shard_map/ffn_fwd/pallas_call | solution.py:479
  246.8 36.1 %ffn_bwd.1 = (bf16[768,3072]{1,0:T(8,128)(2,1)}, bf16[3072,768]{1,0:T(8,128)(2,1)}, f32[1,3072]{1,0:T(1,128)}, f32[1,768]{1,0:T(1,128)}, f32[1,768]{1,0:T(1,128)...) custom-call(f32[1152,768]{1,0:T(8,128)} %get-tuple-element.32.x1, bf16[1,768]{1,0:T(2,128)(2,1)} %reshape.711.gain, ...), custom_call_target="tpu_custom_call" | custom-call | flops 21743271936 | bytes 41943040 | tf_op jit(solution)/shard_map/ffn_bwd/pallas_call | solution.py:515
  282.9 59.2 %bwd_attn.1 = (bf16[3,768,768]{2,1,0:T(8,128)(2,1)}, bf16[768,768]{1,0:T(8,128)(2,1)}, bf16[576,768]{1,0:T(8,128)(2,1)}, f32[1,768]{1,0:T(1,128)}, f32[1,768]{1,0:T(1,128)}) custom-call(bf16[576,768]{1,0:T(8,128)(2,1)} %bitcast.314, s32[576,1]{1,0:T(8,128)} %reshape.767.noise, s32[576,1]{1,0:T(8,128)} %broadcast_in_dim_reshape.8.segc, ...), custom_call_target="tpu_custom_call" | custom-call | flops 41448112128 | bytes 31457280 | tf_op jit(solution)/shard_map/bwd_attn/pallas_call | solution.py:601
  351.7 3.0 dynamic-slice_bitcast_fusion.2
  354.6 3.4 dynamic-slice_bitcast_fusion.1
  361.4 7.4 %collective-permute-done.23 = bf16[192,768]{1,0:T(8,128)(2,1)S(1)} collective-permute-done((bf16[192,768]{1,0:T(8,128)(2,1)S(1)}, bf16[192,768]{1,0:T(8,128)(2,1)S(1)}, u32[]{:S(2)}, u32[]{:S(2)}) %collective-permute-start.23) | collective-permute-done | bytes 294944 | tf_op jit(solution)/shard_map/ppermute | solution.py:613
  371.1 3.0 collective-permute-done.24
  374.2 4.3 collective-permute-done.25
  379.7 4.2 all-to-all-start.4
  384.0 2.9 collective-permute-start.27
  386.9 44.3 %psum.7 = f32[6144]{0:T(1024)S(1)} all-reduce(f32[6144]{0:T(1024)S(1)} %constant_dynamic-update-slice_fusion), channel_id=1, replica_groups=mesh['ctx'=8,'fsdp'=4] {'ctx','fsdp'}, use_global_device_ids=true, to_apply=%region_0.1 | all-reduce | flops 6144 | bytes 49152 | tf_op jit(solution)/shard_map/psum | solution.py:719
  432.0 2.4 fusion.2
  444.5 4.3 all-to-all-start.2
  452.1 4.3 collective-permute-done.15
  459.5 3.3 fusion.1
  464.3 11.8 %collective-permute-done.16 = bf16[3,96,768]{2,1,0:T(8,128)(2,1)S(1)} collective-permute-done((bf16[3,96,768]{2,1,0:T(8,128)(2,1)S(1)}, bf16[3,96,768]{2,1,0:T(8,128)(2,1)S(1)}, u32[]{:S(2)}, u32[]{:S(2)}) %collective-permute-start.16) | collective-permute-done | bytes 442400 | tf_op jit(solution)/shard_map/ppermute | solution.py:613
  478.5 7.5 %collective-permute-done.17 = bf16[3,48,768]{2,1,0:T(8,128)(2,1)S(1)} collective-permute-done((bf16[3,48,768]{2,1,0:T(8,128)(2,1)S(1)}, bf16[3,48,768]{2,1,0:T(8,128)(2,1)S(1)}, u32[]{:S(2)}, u32[]{:S(2)}) %collective-permute-start.17) | collective-permute-done | bytes 221216 | tf_op jit(solution)/shard_map/ppermute | solution.py:613
  490.6 2.7 copy.65
  498.8 5.2 collective-permute-done.19
  504.1 14.0 %collective-permute-done.39 = bf16[768,768]{1,0:T(8,128)(2,1)} collective-permute-done((bf16[768,768]{1,0:T(8,128)(2,1)}, bf16[768,768]{1,0:T(8,128)(2,1)}, u32[]{:S(2)}, u32[]{:S(2)}) %collective-permute-start.39) | collective-permute-done | bytes 1179680 | tf_op jit(solution)/shard_map/ppermute | solution.py:613
  522.1 2.7 collective-permute-start.33
  524.8 11.3 %collective-permute-done.40 = bf16[384,768]{1,0:T(8,128)(2,1)S(1)} collective-permute-done((bf16[384,768]{1,0:T(8,128)(2,1)S(1)}, bf16[384,768]{1,0:T(8,128)(2,1)S(1)}, u32[]{:S(2)}, u32[]{:S(2)}) %collective-permute-start.40) | collective-permute-done | bytes 589856 | tf_op jit(solution)/shard_map/ppermute | solution.py:613
  536.3 2.7 collective-permute-start.41
  539.4 4.0 collective-permute-done.21
  543.5 10.5 %collective-permute-done.34 = bf16[24,3072]{1,0:T(8,128)(2,1)S(1)} collective-permute-done((bf16[24,3072]{1,0:T(8,128)(2,1)S(1)}, bf16[24,3072]{1,0:T(8,128)(2,1)S(1)}, u32[]{:S(2)}, u32[]{:S(2)}) %collective-permute-start.34) | collective-permute-done | bytes 147488 | tf_op jit(solution)/shard_map/ppermute | solution.py:613
  554.2 3.0 collective-permute-start.42
  557.2 5.2 collective-permute-done.35
  565.1 4.1 collective-permute-done.36
  569.4 2.5 collective-permute-done.43
  573.3 5.4 collective-permute-done.44
  578.9 5.3 collective-permute-done.37
  586.2 7.3 %collective-permute-done.45 = bf16[384,768]{1,0:T(8,128)(2,1)S(1)} collective-permute-done((bf16[384,768]{1,0:T(8,128)(2,1)S(1)}, bf16[384,768]{1,0:T(8,128)(2,1)S(1)}, u32[]{:S(2)}, u32[]{:S(2)}) %collective-permute-start.45) | collective-permute-done | bytes 589856 | tf_op jit(solution)/shard_map/ppermute | solution.py:613
  (256 shorter events, 106.1 us)
Async XLA Ops:
  2.0 90.8 %all-to-all-start.1 = ((s32[8,1,128]{2,1,0:T(1,128)}), s32[8,1,128]{2,1,0:T(1,128)S(1)}, u32[]{:S(2)}, u32[]{:S(2)}) async-start(s32[8,1,128]{2,1,0:T(1,128)} %bitcast.6), calls=%async_computation.1 | async-start | bytes 8192 | tf_op jit(solution)/shard_map/all_to_all | solution.py:668
  9.3 114.7 %collective-permute-start.3 = (bf16[192,2304]{1,0:T(8,128)(2,1)}, bf16[192,2304]{1,0:T(8,128)(2,1)S(1)}, u32[]{:S(2)}, u32[]{:S(2)}) collective-permute-start(bf16[192,2304]{1,0:T(8,128)(2,1)} %param.18), channel_id=1, source_target_pairs={{0,2},{1,3},{2,0},{3,1},{4,6},{5,7},{6,4},{7,5},{8,10},{9,11},{10,... | collective-permute-start | bytes 2654216 | tf_op jit(solution)/shard_map/ppermute | solution.py:613
  10.8 98.6 %collective-permute-start.5 = (bf16[192,768]{1,0:T(8,128)(2,1)}, bf16[192,768]{1,0:T(8,128)(2,1)}, u32[]{:S(2)}, u32[]{:S(2)}) collective-permute-start(bf16[192,768]{1,0:T(8,128)(2,1)} %param.19), channel_id=1, source_target_pairs={{0,2},{1,3},{2,0},{3,1},{4,6},{5,7},{6,4},{7,5},{8,10},{9,11},{10,... | collective-permute-start | bytes 884744 | tf_op jit(solution)/shard_map/ppermute | solution.py:613
  11.3 118.9 %collective-permute-start.7 = (bf16[192,3072]{1,0:T(8,128)(2,1)}, bf16[192,3072]{1,0:T(8,128)(2,1)}, u32[]{:S(2)}, u32[]{:S(2)}) collective-permute-start(bf16[192,3072]{1,0:T(8,128)(2,1)} %param.21), channel_id=1, source_target_pairs={{0,2},{1,3},{2,0},{3,1},{4,6},{5,7},{6,4},{7,5},{8,10},{9,11},{10,... | collective-permute-start | bytes 3538952 | tf_op jit(solution)/shard_map/ppermute | solution.py:613
  12.8 121.1 %collective-permute-start.9 = (bf16[768,768]{1,0:T(8,128)(2,1)}, bf16[768,768]{1,0:T(8,128)(2,1)}, u32[]{:S(2)}, u32[]{:S(2)}) collective-permute-start(bf16[768,768]{1,0:T(8,128)(2,1)} %param.23), channel_id=1, source_target_pairs={{0,2},{1,3},{2,0},{3,1},{4,6},{5,7},{6,4},{7,5},{8,10},{9,11},{10,... | collective-permute-start | bytes 3538952 | tf_op jit(solution)/shard_map/ppermute | solution.py:613
  92.8 26.3 %all-to-all-start = ((bf16[8,64,768]{2,1,0:T(8,128)(2,1)}), bf16[8,64,768]{2,1,0:T(8,128)(2,1)S(1)}, u32[]{:S(2)}, u32[]{:S(2)}) async-start(bf16[8,64,768]{2,1,0:T(8,128)(2,1)} %bitcast.315), calls=%async_computation | async-start | bytes 1572864 | tf_op jit(solution)/shard_map/all_to_all | solution.py:668
  111.5 16.1 %collective-permute-start.6 = (bf16[2,192,768]{2,1,0:T(8,128)(2,1)}, bf16[2,192,768]{2,1,0:T(8,128)(2,1)}, u32[]{:S(2)}, u32[]{:S(2)}) collective-permute-start(bf16[2,192,768]{2,1,0:T(8,128)(2,1)} %maximum_select_fusion.17), channel_id=1, source_target_pairs={{0,1},{1,0},{2,3},{3,2},{4,5},{5,4},{6,7},{7,6},{8,9},{9,8},{10,11... | collective-permute-start | bytes 1769480 | tf_op jit(solution)/shard_map/ppermute | solution.py:613
  120.1 41.0 %all-to-all-start.3 = ((bf16[8,2,64,768]{3,2,1,0:T(8,128)(2,1)}), bf16[8,2,64,768]{3,2,1,0:T(8,128)(2,1)S(1)}, u32[]{:S(2)}, u32[]{:S(2)}) async-start(bf16[8,2,64,768]{3,2,1,0:T(8,128)(2,1)} %bitcast.45), calls=%async_computation.3 | async-start | bytes 3145728 | tf_op jit(solution)/shard_map/all_to_all | solution.py:668
  125.5 26.4 %collective-permute-start.4 = (bf16[2,192,2304]{2,1,0:T(8,128)(2,1)}, bf16[2,192,2304]{2,1,0:T(8,128)(2,1)}, u32[]{:S(2)}, u32[]{:S(2)}) collective-permute-start(bf16[2,192,2304]{2,1,0:T(8,128)(2,1)} %maximum_select_fusion.8), channel_id=1, source_target_pairs={{0,1},{1,0},{2,3},{3,2},{4,5},{5,4},{6,7},{7,6},{8,9},{9,8},{10,11... | collective-permute-start | bytes 5308424 | tf_op jit(solution)/shard_map/ppermute | solution.py:613
  133.7 74.8 %collective-permute-start.8 = (bf16[2,192,3072]{2,1,0:T(8,128)(2,1)}, bf16[2,192,3072]{2,1,0:T(8,128)(2,1)}, u32[]{:S(2)}, u32[]{:S(2)}) collective-permute-start(bf16[2,192,3072]{2,1,0:T(8,128)(2,1)} %maximum_select_fusion.4), channel_id=1, source_target_pairs={{0,1},{1,0},{2,3},{3,2},{4,5},{5,4},{6,7},{7,6},{8,9},{9,8},{10,11... | collective-permute-start | bytes 7077896 | tf_op jit(solution)/shard_map/ppermute | solution.py:613
  137.3 78.1 %collective-permute-start.10 = (bf16[2,768,768]{2,1,0:T(8,128)(2,1)}, bf16[2,768,768]{2,1,0:T(8,128)(2,1)}, u32[]{:S(2)}, u32[]{:S(2)}) collective-permute-start(bf16[2,768,768]{2,1,0:T(8,128)(2,1)} %maximum_select_fusion.6), channel_id=1, source_target_pairs={{0,1},{1,0},{2,3},{3,2},{4,5},{5,4},{6,7},{7,6},{8,9},{9,8},{10,11... | collective-permute-start | bytes 7077896 | tf_op jit(solution)/shard_map/ppermute | solution.py:613
  141.1 8.3 %collective-permute-start = (bf16[64,768]{1,0:T(8,128)(2,1)S(1)}, bf16[64,768]{1,0:T(8,128)(2,1)S(1)}, u32[]{:S(2)}, u32[]{:S(2)}) collective-permute-start(bf16[64,768]{1,0:T(8,128)(2,1)S(1)} %slice_bitcast_fusion.2), channel_id=1, source_target_pairs={{0,4},{4,0},{8,12},{12,8},{16,20},{20,16},{24,28},{28,24},{1,5},{5... | collective-permute-start | bytes 294920 | tf_op jit(solution)/shard_map/ppermute | solution.py:613
  161.1 45.9 %collective-permute-start.12 = (bf16[2,64,768]{2,1,0:T(8,128)(2,1)S(1)}, bf16[2,64,768]{2,1,0:T(8,128)(2,1)S(1)}, u32[]{:S(2)}, u32[]{:S(2)}) collective-permute-start(bf16[2,64,768]{2,1,0:T(8,128)(2,1)S(1)} %slice_bitcast_fusion), channel_id=1, source_target_pairs={{0,4},{4,0},{8,12},{12,8},{16,20},{20,16},{24,28},{28,24},{1,5},{5... | collective-permute-start | bytes 589832 | tf_op jit(solution)/shard_map/ppermute | solution.py:613
  344.0 14.5 %collective-permute-start.22 = (bf16[2,192,768]{2,1,0:T(8,128)(2,1)}, bf16[2,192,768]{2,1,0:T(8,128)(2,1)}, u32[]{:S(2)}, u32[]{:S(2)}) collective-permute-start(bf16[2,192,768]{2,1,0:T(8,128)(2,1)} %dynamic-slice_bitcast_fusion.8), channel_id=1, source_target_pairs={{0,1},{1,0},{2,3},{3,2},{4,5},{5,4},{6,7},{7,6},{8,9},{9,8},{10,11... | collective-permute-start | bytes 1769480 | tf_op jit(solution)/shard_map/ppermute | solution.py:613
  347.1 93.0 %collective-permute-start.11 = (bf16[2,64,768]{2,1,0:T(8,128)(2,1)}, bf16[2,64,768]{2,1,0:T(8,128)(2,1)}, u32[]{:S(2)}, u32[]{:S(2)}) collective-permute-start(bf16[2,64,768]{2,1,0:T(8,128)(2,1)} %slice_bitcast_fusion.1), channel_id=1, source_target_pairs={{0,4},{4,0},{8,12},{12,8},{16,20},{20,16},{24,28},{28,24},{1,5},{5... | collective-permute-start | bytes 589832 | tf_op jit(solution)/shard_map/ppermute | solution.py:613
  348.9 29.7 %collective-permute-start.13 = (bf16[64,768]{1,0:T(8,128)(2,1)S(1)}, bf16[64,768]{1,0:T(8,128)(2,1)S(1)}, u32[]{:S(2)}, u32[]{:S(2)}) collective-permute-start(bf16[64,768]{1,0:T(8,128)(2,1)S(1)} %slice.108), channel_id=1, source_target_pairs={{0,4},{4,0},{8,12},{12,8},{16,20},{20,16},{24,28},{28,24},{1,5},{5... | collective-permute-start | bytes 294920 | tf_op jit(solution)/shard_map/ppermute | solution.py:613
  354.6 77.4 %collective-permute-start.14 = (bf16[3,2,192,768]{3,2,1,0:T(8,128)(2,1)}, bf16[3,2,192,768]{3,2,1,0:T(8,128)(2,1)}, u32[]{:S(2)}, u32[]{:S(2)}) collective-permute-start(bf16[3,2,192,768]{3,2,1,0:T(8,128)(2,1)} %dynamic-slice_bitcast_fusion.2), channel_id=1, source_target_pairs={{0,1},{1,0},{2,3},{3,2},{4,5},{5,4},{6,7},{7,6},{8,9},{9,8},{10,11... | collective-permute-start | bytes 5308424 | tf_op jit(solution)/shard_map/ppermute | solution.py:613
  358.0 101.5 %collective-permute-start.30 = (bf16[2,192,3072]{2,1,0:T(8,128)(2,1)}, bf16[2,192,3072]{2,1,0:T(8,128)(2,1)}, u32[]{:S(2)}, u32[]{:S(2)}) collective-permute-start(bf16[2,192,3072]{2,1,0:T(8,128)(2,1)} %dynamic-slice_bitcast_fusion.1), channel_id=1, source_target_pairs={{0,1},{1,0},{2,3},{3,2},{4,5},{5,4},{6,7},{7,6},{8,9},{9,8},{10,11... | collective-permute-start | bytes 7077896 | tf_op jit(solution)/shard_map/ppermute | solution.py:613
  359.8 9.0 %collective-permute-start.23 = (bf16[192,768]{1,0:T(8,128)(2,1)S(1)}, bf16[192,768]{1,0:T(8,128)(2,1)S(1)}, u32[]{:S(2)}, u32[]{:S(2)}) collective-permute-start(bf16[192,768]{1,0:T(8,128)(2,1)S(1)} %dynamic-slice_bitcast_fusion.12), channel_id=1, source_target_pairs={{0,2},{1,3},{2,0},{3,1},{4,6},{5,7},{6,4},{7,5},{8,10},{9,11},{10,... | collective-permute-start | bytes 884744 | tf_op jit(solution)/shard_map/ppermute | solution.py:613
  368.9 5.2 collective-permute-start.24
  378.6 97.7 %collective-permute-start.38 = (bf16[2,768,768]{2,1,0:T(8,128)(2,1)}, bf16[2,768,768]{2,1,0:T(8,128)(2,1)}, u32[]{:S(2)}, u32[]{:S(2)}) collective-permute-start(bf16[2,768,768]{2,1,0:T(8,128)(2,1)} %dynamic-slice_bitcast_fusion), channel_id=1, source_target_pairs={{0,1},{1,0},{2,3},{3,2},{4,5},{5,4},{6,7},{7,6},{8,9},{9,8},{10,11... | collective-permute-start | bytes 7077896 | tf_op jit(solution)/shard_map/ppermute | solution.py:613
  378.6 5.3 collective-permute-start.26
  379.7 64.8 %all-to-all-start.4 = ((bf16[8,64,768]{2,1,0:T(8,128)(2,1)}), bf16[8,64,768]{2,1,0:T(8,128)(2,1)}, u32[]{:S(2)}, u32[]{:S(2)}) async-start(bf16[8,64,768]{2,1,0:T(8,128)(2,1)} %maximum_select_fusion.15), calls=%async_computation.4 | async-start | bytes 1572864 | tf_op jit(solution)/shard_map/all_to_all | solution.py:668
  384.0 47.9 %collective-permute-start.27 = (bf16[24,768]{1,0:T(8,128)(2,1)S(1)}, bf16[24,768]{1,0:T(8,128)(2,1)S(1)}, u32[]{:S(2)}, u32[]{:S(2)}) collective-permute-start(bf16[24,768]{1,0:T(8,128)(2,1)S(1)} %fusion.21), channel_id=1, source_target_pairs={{0,16},{4,20},{8,24},{12,28},{16,0},{20,4},{24,8},{28,12},{1,17},{... | collective-permute-start | bytes 110600 | tf_op jit(solution)/shard_map/ppermute | solution.py:613
  431.9 7.3 %collective-permute-start.28 = (bf16[48,768]{1,0:T(8,128)(2,1)S(1)}, bf16[48,768]{1,0:T(8,128)(2,1)S(1)}, u32[]{:S(2)}, u32[]{:S(2)}) collective-permute-start(bf16[48,768]{1,0:T(8,128)(2,1)S(1)} %bitcast.328), channel_id=1, source_target_pairs={{0,8},{4,12},{8,0},{12,4},{16,24},{20,28},{24,16},{28,20},{1,9},{5... | collective-permute-start | bytes 221192 | tf_op jit(solution)/shard_map/ppermute | solution.py:613
  435.5 21.0 %collective-permute-start.15 = (bf16[3,192,768]{2,1,0:T(8,128)(2,1)}, bf16[3,192,768]{2,1,0:T(8,128)(2,1)}, u32[]{:S(2)}, u32[]{:S(2)}) collective-permute-start(bf16[3,192,768]{2,1,0:T(8,128)(2,1)} %dynamic-slice_bitcast_fusion.5), channel_id=1, source_target_pairs={{0,2},{1,3},{2,0},{3,1},{4,6},{5,7},{6,4},{7,5},{8,10},{9,11},{10,... | collective-permute-start | bytes 2654216 | tf_op jit(solution)/shard_map/ppermute | solution.py:613
  439.3 5.2 collective-permute-start.29
  444.5 46.1 %all-to-all-start.2 = ((bf16[8,2,64,768]{3,2,1,0:T(8,128)(2,1)}), bf16[8,2,64,768]{3,2,1,0:T(8,128)(2,1)}, u32[]{:S(2)}, u32[]{:S(2)}) async-start(bf16[8,2,64,768]{3,2,1,0:T(8,128)(2,1)} %slice_select_fusion), calls=%async_computation.2 | async-start | bytes 3145728 | tf_op jit(solution)/shard_map/all_to_all | solution.py:668
  457.9 18.1 %collective-permute-start.16 = (bf16[3,96,768]{2,1,0:T(8,128)(2,1)S(1)}, bf16[3,96,768]{2,1,0:T(8,128)(2,1)S(1)}, u32[]{:S(2)}, u32[]{:S(2)}) collective-permute-start(bf16[3,96,768]{2,1,0:T(8,128)(2,1)S(1)} %dynamic-slice_bitcast_fusion.9), channel_id=1, source_target_pairs={{0,4},{4,0},{8,12},{12,8},{16,20},{20,16},{24,28},{28,24},{1,5},{5... | collective-permute-start | bytes 1327112 | tf_op jit(solution)/shard_map/ppermute | solution.py:613
  462.8 34.0 %collective-permute-start.31 = (bf16[192,3072]{1,0:T(8,128)(2,1)S(1)}, bf16[192,3072]{1,0:T(8,128)(2,1)}, u32[]{:S(2)}, u32[]{:S(2)}) collective-permute-start(bf16[192,3072]{1,0:T(8,128)(2,1)S(1)} %dynamic-slice_bitcast_fusion.4), channel_id=1, source_target_pairs={{0,2},{1,3},{2,0},{3,1},{4,6},{5,7},{6,4},{7,5},{8,10},{9,11},{10,... | collective-permute-start | bytes 3538952 | tf_op jit(solution)/shard_map/ppermute | solution.py:613
  476.2 9.9 %collective-permute-start.17 = (bf16[3,48,768]{2,1,0:T(8,128)(2,1)S(1)}, bf16[3,48,768]{2,1,0:T(8,128)(2,1)S(1)}, u32[]{:S(2)}, u32[]{:S(2)}) collective-permute-start(bf16[3,48,768]{2,1,0:T(8,128)(2,1)S(1)} %dynamic-slice_bitcast_fusion.13), channel_id=1, source_target_pairs={{0,8},{4,12},{8,0},{12,4},{16,24},{20,28},{24,16},{28,20},{1,9},{5... | collective-permute-start | bytes 663560 | tf_op jit(solution)/shard_map/ppermute | solution.py:613
  487.5 8.3 %collective-permute-start.18 = (bf16[3,24,768]{2,1,0:T(8,128)(2,1)}, bf16[3,24,768]{2,1,0:T(8,128)(2,1)}, u32[]{:S(2)}, u32[]{:S(2)}) collective-permute-start(bf16[3,24,768]{2,1,0:T(8,128)(2,1)} %dynamic-slice_bitcast_fusion.17), channel_id=1, source_target_pairs={{0,16},{4,20},{8,24},{12,28},{16,0},{20,4},{24,8},{28,12},{1,17},{... | collective-permute-start | bytes 331784 | tf_op jit(solution)/shard_map/ppermute | solution.py:613
  490.1 27.9 %collective-permute-start.39 = (bf16[768,768]{1,0:T(8,128)(2,1)}, bf16[768,768]{1,0:T(8,128)(2,1)}, u32[]{:S(2)}, u32[]{:S(2)}) collective-permute-start(bf16[768,768]{1,0:T(8,128)(2,1)} %dynamic-slice_bitcast_fusion.3), channel_id=1, source_target_pairs={{0,2},{1,3},{2,0},{3,1},{4,6},{5,7},{6,4},{7,5},{8,10},{9,11},{10,... | collective-permute-start | bytes 3538952 | tf_op jit(solution)/shard_map/ppermute | solution.py:613
  496.7 7.2 %collective-permute-start.19 = (bf16[3,24,768]{2,1,0:T(8,128)(2,1)S(1)}, bf16[3,24,768]{2,1,0:T(8,128)(2,1)S(1)}, u32[]{:S(2)}, u32[]{:S(2)}) collective-permute-start(bf16[3,24,768]{2,1,0:T(8,128)(2,1)S(1)} %fusion.19), channel_id=1, source_target_pairs={{0,16},{4,20},{8,24},{12,28},{16,0},{20,4},{24,8},{28,12},{1,17},{... | collective-permute-start | bytes 331784 | tf_op jit(solution)/shard_map/ppermute | solution.py:613
  498.7 23.2 %collective-permute-start.32 = (bf16[96,3072]{1,0:T(8,128)(2,1)S(1)}, bf16[96,3072]{1,0:T(8,128)(2,1)S(1)}, u32[]{:S(2)}, u32[]{:S(2)}) collective-permute-start(bf16[96,3072]{1,0:T(8,128)(2,1)S(1)} %dynamic-slice_bitcast_fusion.7), channel_id=1, source_target_pairs={{0,4},{4,0},{8,12},{12,8},{16,20},{20,16},{24,28},{28,24},{1,5},{5... | collective-permute-start | bytes 1769480 | tf_op jit(solution)/shard_map/ppermute | solution.py:613
  504.0 15.8 %collective-permute-start.20 = (bf16[3,48,768]{2,1,0:T(8,128)(2,1)S(1)}, bf16[3,48,768]{2,1,0:T(8,128)(2,1)S(1)}, u32[]{:S(2)}, u32[]{:S(2)}) collective-permute-start(bf16[3,48,768]{2,1,0:T(8,128)(2,1)S(1)} %bitcast.311), channel_id=1, source_target_pairs={{0,8},{4,12},{8,0},{12,4},{16,24},{20,28},{24,16},{28,20},{1,9},{5... | collective-permute-start | bytes 663560 | tf_op jit(solution)/shard_map/ppermute | solution.py:613
  519.7 16.3 %collective-permute-start.40 = (bf16[384,768]{1,0:T(8,128)(2,1)S(1)}, bf16[384,768]{1,0:T(8,128)(2,1)S(1)}, u32[]{:S(2)}, u32[]{:S(2)}) collective-permute-start(bf16[384,768]{1,0:T(8,128)(2,1)S(1)} %dynamic-slice_bitcast_fusion.6), channel_id=1, source_target_pairs={{0,4},{4,0},{8,12},{12,8},{16,20},{20,16},{24,28},{28,24},{1,5},{5... | collective-permute-start | bytes 1769480 | tf_op jit(solution)/shard_map/ppermute | solution.py:613
  519.9 23.5 %collective-permute-start.21 = (bf16[3,96,768]{2,1,0:T(8,128)(2,1)S(1)}, bf16[3,96,768]{2,1,0:T(8,128)(2,1)S(1)}, u32[]{:S(2)}, u32[]{:S(2)}) collective-permute-start(bf16[3,96,768]{2,1,0:T(8,128)(2,1)S(1)} %bitcast.289), channel_id=1, source_target_pairs={{0,4},{4,0},{8,12},{12,8},{16,20},{20,16},{24,28},{28,24},{1,5},{5... | collective-permute-start | bytes 1327112 | tf_op jit(solution)/shard_map/ppermute | solution.py:613
  522.1 16.8 %collective-permute-start.33 = (bf16[48,3072]{1,0:T(8,128)(2,1)S(1)}, bf16[48,3072]{1,0:T(8,128)(2,1)S(1)}, u32[]{:S(2)}, u32[]{:S(2)}) collective-permute-start(bf16[48,3072]{1,0:T(8,128)(2,1)S(1)} %dynamic-slice_bitcast_fusion.11), channel_id=1, source_target_pairs={{0,8},{4,12},{8,0},{12,4},{16,24},{20,28},{24,16},{28,20},{1,9},{5... | collective-permute-start | bytes 884744 | tf_op jit(solution)/shard_map/ppermute | solution.py:613
  536.3 17.8 %collective-permute-start.41 = (bf16[192,768]{1,0:T(8,128)(2,1)S(1)}, bf16[192,768]{1,0:T(8,128)(2,1)S(1)}, u32[]{:S(2)}, u32[]{:S(2)}) collective-permute-start(bf16[192,768]{1,0:T(8,128)(2,1)S(1)} %dynamic-slice_bitcast_fusion.10), channel_id=1, source_target_pairs={{0,8},{4,12},{8,0},{12,4},{16,24},{20,28},{24,16},{28,20},{1,9},{5... | collective-permute-start | bytes 884744 | tf_op jit(solution)/shard_map/ppermute | solution.py:613
  539.0 14.9 %collective-permute-start.34 = (bf16[24,3072]{1,0:T(8,128)(2,1)S(1)}, bf16[24,3072]{1,0:T(8,128)(2,1)S(1)}, u32[]{:S(2)}, u32[]{:S(2)}) collective-permute-start(bf16[24,3072]{1,0:T(8,128)(2,1)S(1)} %dynamic-slice_bitcast_fusion.15), channel_id=1, source_target_pairs={{0,16},{4,20},{8,24},{12,28},{16,0},{20,4},{24,8},{28,12},{1,17},{... | collective-permute-start | bytes 442376 | tf_op jit(solution)/shard_map/ppermute | solution.py:613
  554.0 8.4 %collective-permute-start.35 = (bf16[24,3072]{1,0:T(8,128)(2,1)S(1)}, bf16[24,3072]{1,0:T(8,128)(2,1)S(1)}, u32[]{:S(2)}, u32[]{:S(2)}) collective-permute-start(bf16[24,3072]{1,0:T(8,128)(2,1)S(1)} %fusion.17), channel_id=1, source_target_pairs={{0,16},{4,20},{8,24},{12,28},{16,0},{20,4},{24,8},{28,12},{1,17},{... | collective-permute-start | bytes 442376 | tf_op jit(solution)/shard_map/ppermute | solution.py:613
  554.2 10.8 %collective-permute-start.42 = (bf16[96,768]{1,0:T(8,128)(2,1)S(1)}, bf16[96,768]{1,0:T(8,128)(2,1)S(1)}, u32[]{:S(2)}, u32[]{:S(2)}) collective-permute-start(bf16[96,768]{1,0:T(8,128)(2,1)S(1)} %dynamic-slice_bitcast_fusion.14), channel_id=1, source_target_pairs={{0,16},{4,20},{8,24},{12,28},{16,0},{20,4},{24,8},{28,12},{1,17},{... | collective-permute-start | bytes 442376 | tf_op jit(solution)/shard_map/ppermute | solution.py:613
  562.4 6.8 %collective-permute-start.36 = (bf16[48,3072]{1,0:T(8,128)(2,1)S(1)}, bf16[48,3072]{1,0:T(8,128)(2,1)S(1)}, u32[]{:S(2)}, u32[]{:S(2)}) collective-permute-start(bf16[48,3072]{1,0:T(8,128)(2,1)S(1)} %bitcast.303), channel_id=1, source_target_pairs={{0,8},{4,12},{8,0},{12,4},{16,24},{20,28},{24,16},{28,20},{1,9},{5... | collective-permute-start | bytes 884744 | tf_op jit(solution)/shard_map/ppermute | solution.py:613
  565.0 6.9 %collective-permute-start.43 = (bf16[96,768]{1,0:T(8,128)(2,1)S(1)}, bf16[96,768]{1,0:T(8,128)(2,1)S(1)}, u32[]{:S(2)}, u32[]{:S(2)}) collective-permute-start(bf16[96,768]{1,0:T(8,128)(2,1)S(1)} %fusion.16), channel_id=1, source_target_pairs={{0,16},{4,20},{8,24},{12,28},{16,0},{20,4},{24,8},{28,12},{1,17},{... | collective-permute-start | bytes 442376 | tf_op jit(solution)/shard_map/ppermute | solution.py:613
  569.3 14.9 %collective-permute-start.37 = (bf16[96,3072]{1,0:T(8,128)(2,1)S(1)}, bf16[96,3072]{1,0:T(8,128)(2,1)S(1)}, u32[]{:S(2)}, u32[]{:S(2)}) collective-permute-start(bf16[96,3072]{1,0:T(8,128)(2,1)S(1)} %bitcast.277), channel_id=1, source_target_pairs={{0,4},{4,0},{8,12},{12,8},{16,20},{20,16},{24,28},{28,24},{1,5},{5... | collective-permute-start | bytes 1769480 | tf_op jit(solution)/shard_map/ppermute | solution.py:613
  571.9 6.8 %collective-permute-start.44 = (bf16[192,768]{1,0:T(8,128)(2,1)S(1)}, bf16[192,768]{1,0:T(8,128)(2,1)S(1)}, u32[]{:S(2)}, u32[]{:S(2)}) collective-permute-start(bf16[192,768]{1,0:T(8,128)(2,1)S(1)} %bitcast.305), channel_id=1, source_target_pairs={{0,8},{4,12},{8,0},{12,4},{16,24},{20,28},{24,16},{28,20},{1,9},{5... | collective-permute-start | bytes 884744 | tf_op jit(solution)/shard_map/ppermute | solution.py:613
  578.8 14.6 %collective-permute-start.45 = (bf16[384,768]{1,0:T(8,128)(2,1)S(1)}, bf16[384,768]{1,0:T(8,128)(2,1)S(1)}, u32[]{:S(2)}, u32[]{:S(2)}) collective-permute-start(bf16[384,768]{1,0:T(8,128)(2,1)S(1)} %bitcast.279), channel_id=1, source_target_pairs={{0,4},{4,0},{8,12},{12,8},{16,20},{20,16},{24,28},{28,24},{1,5},{5... | collective-permute-start | bytes 1769480 | tf_op jit(solution)/shard_map/ppermute | solution.py:613
  (34 other events, 223.4 us)

commit v2 on v1

--- a/solution.py
+++ b/solution.py
@@ -438,19 +438,53 @@
 
 def whole(shape): return pl.BlockSpec(shape,lambda *i:(0,)*len(shape))
 
-def fwd_attn(xc,noise,segc,segr,emb,gain,wqkv,wout,cos,sin):
+def fwd_attn_comm_kernel(half,*refs):
+    ins,(up,down,gout,zeros),rest=refs[:12],refs[12:16],refs[16:]
+    outs,(up_o,down_o,cot_o),scratch=rest[:6],rest[6:9],rest[9:13]
+    a_send,a_recv,w_send,w_recv,local=rest[13:]
+    p=pl.program_id(0)
+    c,_=place_ids()
+    weights=[GatherRows(up,up_o,w_send.at[0],w_recv.at[0],local.at[0]),GatherRows(down,down_o,w_send.at[1],w_recv.at[1],local.at[1])]
+    rows=[ToUnit(lambda q,h,i=i:gout.at[q,i,h],lambda t,i=i:cot_o.at[i,t],a_send.at[i],a_recv.at[i],local.at[2+i]) for i in range(2)]
+    pads=[pltpu.make_async_copy(zeros,cot_o.at[i,pl.ds(7,2)],local.at[4+i]) for i in range(2)]
+    @pl.when(p==0)
+    def _():
+        meet(True,(1,2))
+        for w in weights: w.begin()
+        for r in rows: r.begin()
+        @pl.when(c%2==1)
+        def _():
+            for d in pads: d.start()
+            for d in pads: d.wait()
+    fwd_attn_kernel(half,*ins,*outs,*scratch)
+    @pl.when(p==2)
+    def _():
+        for w in weights: w.relay_far()
+    @pl.when(p==3)
+    def _():
+        for w in weights: w.relay_x()
+    @pl.when(p==pl.num_programs(0)-1)
+    def _():
+        for w in weights: w.finish()
+        for r in rows: r.finish()
+
+def fwd_attn(xc,noise,segc,segr,emb,gain,wqkv,wout,cos,sin,up,down,gout):
     half=xc.shape[0]; R=2*half
+    piece=gout.shape[3]
+    zeros=jnp.zeros((2,piece,D),BF)
     nt=len(tiles_of(half))*2; ntp=-(-nt//8)*8
     ws=[pl.BlockSpec((D,PAIR),(lambda off:(lambda p:(0,off+p)))(o*PAIRS)) for o in range(3)]
     rows=pl.BlockSpec((R,PAIR),lambda p:(0,p))
-    return pl.pallas_call(partial(fwd_attn_kernel,half),grid=(PAIRS,),
-        in_specs=[whole((half,D)),whole((half,1)),whole((half,1)),whole((1,half)),whole((1,D)),whole((1,D)),*ws,whole((D,D)),whole((half,PAIR)),whole((half,PAIR))],
-        out_specs=[rows,rows,rows,rows,pl.BlockSpec((1,ntp,256),lambda p:(p,0,0)),whole((R,D))],
-        out_shape=[jax.ShapeDtypeStruct((R,D),BF)]*4+[jax.ShapeDtypeStruct((PAIRS,ntp,256),F32),jax.ShapeDtypeStruct((R,D),F32)],
-        scratch_shapes=[pltpu.VMEM((R,D),BF),pltpu.VMEM((2,half,half),F32),pltpu.VMEM((half,128),F32),pltpu.VMEM((PAIRS,R,PAIR),BF)],
-        compiler_params=pltpu.CompilerParams(vmem_limit_bytes=VMEM_LIMIT,dimension_semantics=("arbitrary",)),
+    return pl.pallas_call(partial(fwd_attn_comm_kernel,half),grid=(PAIRS,),
+        in_specs=[whole((half,D)),whole((half,1)),whole((half,1)),whole((1,half)),whole((1,D)),whole((1,D)),*ws,whole((D,D)),whole((half,PAIR)),whole((half,PAIR)),whole(up.shape),whole(down.shape),ANYSPACE,whole(zeros.shape)],
+        out_specs=[rows,rows,rows,rows,pl.BlockSpec((1,ntp,256),lambda p:(p,0,0)),whole((R,D))]+[ANYSPACE]*3,
+        out_shape=[jax.ShapeDtypeStruct((R,D),BF)]*4+[jax.ShapeDtypeStruct((PAIRS,ntp,256),F32),jax.ShapeDtypeStruct((R,D),F32)]
+            +[jax.ShapeDtypeStruct((D,FF),BF),jax.ShapeDtypeStruct((FF,D),BF),jax.ShapeDtypeStruct((2,9,piece,D),BF)],
+        scratch_shapes=[pltpu.VMEM((R,D),BF),pltpu.VMEM((2,half,half),F32),pltpu.VMEM((half,128),F32),pltpu.VMEM((PAIRS,R,PAIR),BF),
+            DMA((2,8)),DMA((2,9)),DMA((2,5)),DMA((2,5)),DMA((6,))],
+        compiler_params=pltpu.CompilerParams(vmem_limit_bytes=VMEM_LIMIT,dimension_semantics=("arbitrary",),collective_id=1,has_side_effects=True),
         cost_estimate=pl.CostEstimate(flops=2*R*D*(3*D+D)+24*R*half*D//2*2,bytes_accessed=16<<20,transcendentals=R*half*HEADS),
-        name="fwd_attn")(xc,noise,segc,segr,emb,gain,wqkv,wqkv,wqkv,wout,cos,sin)
+        name="fwd_attn")(xc,noise,segc,segr,emb,gain,wqkv,wqkv,wqkv,wout,cos,sin,up,down,gout,zeros)
 
 GC=(2.0/3.141592653589793)**0.5
 def ffn_fwd_kernel(x1,gain,wup,bup,wdn,bdn,out_o,act_o,dg_o,h_s,acc):
@@ -509,17 +543,31 @@
         gx1_o[...]=gx
         ga_o[...]=gx.astype(BF)
 
-def ffn_bwd(x1,gain,gy,act,dg,wup,wdn,tile=512):
+def ffn_bwd_comm_kernel(*refs):
+    ins,(res,),outs,(out_o,),scratch,(send,recv,local)=refs[:7],refs[7:8],refs[8:15],refs[15:16],refs[16:18],refs[18:]
+    j=pl.program_id(0)
+    rows=[FromUnit(lambda t,i=i:res.at[i,t],lambda q,h,i=i:out_o.at[q,i,h],send.at[i],recv.at[i],local.at[i]) for i in range(2)]
+    @pl.when(j==0)
+    def _():
+        meet(True,())
+        for r in rows: r.begin()
+    ffn_bwd_kernel(*ins,*outs,*scratch)
+    @pl.when(j==pl.num_programs(0)-1)
+    def _():
+        for r in rows: r.finish()
+
+def ffn_bwd(x1,gain,gy,act,dg,wup,wdn,res,tile=512):
     R=x1.shape[0]
+    piece=R//18
     col=pl.BlockSpec((R,tile),lambda j:(0,j))
-    return pl.pallas_call(ffn_bwd_kernel,grid=(FF//tile,),
-        in_specs=[whole((R,D)),whole((1,D)),whole((R,D)),col,col,pl.BlockSpec((D,tile),lambda j:(0,j)),pl.BlockSpec((tile,D),lambda j:(j,0))],
-        out_specs=[pl.BlockSpec((D,tile),lambda j:(0,j)),pl.BlockSpec((tile,D),lambda j:(j,0)),pl.BlockSpec((1,tile),lambda j:(0,j)),whole((1,D)),whole((1,D)),whole((R,D)),whole((R,D))],
-        out_shape=[jax.ShapeDtypeStruct((D,FF),BF),jax.ShapeDtypeStruct((FF,D),BF),jax.ShapeDtypeStruct((1,FF),F32),jax.ShapeDtypeStruct((1,D),F32),jax.ShapeDtypeStruct((1,D),F32),jax.ShapeDtypeStruct((R,D),F32),jax.ShapeDtypeStruct((R,D),BF)],
-        scratch_shapes=[pltpu.VMEM((D,R),BF),pltpu.VMEM((R,D),F32)],
-        compiler_params=pltpu.CompilerParams(vmem_limit_bytes=VMEM_LIMIT,dimension_semantics=("arbitrary",)),
+    return pl.pallas_call(ffn_bwd_comm_kernel,grid=(FF//tile,),
+        in_specs=[whole((R,D)),whole((1,D)),whole((R,D)),col,col,pl.BlockSpec((D,tile),lambda j:(0,j)),pl.BlockSpec((tile,D),lambda j:(j,0)),ANYSPACE],
+        out_specs=[pl.BlockSpec((D,tile),lambda j:(0,j)),pl.BlockSpec((tile,D),lambda j:(j,0)),pl.BlockSpec((1,tile),lambda j:(0,j)),whole((1,D)),whole((1,D)),whole((R,D)),whole((R,D)),ANYSPACE],
+        out_shape=[jax.ShapeDtypeStruct((D,FF),BF),jax.ShapeDtypeStruct((FF,D),BF),jax.ShapeDtypeStruct((1,FF),F32),jax.ShapeDtypeStruct((1,D),F32),jax.ShapeDtypeStruct((1,D),F32),jax.ShapeDtypeStruct((R,D),F32),jax.ShapeDtypeStruct((R,D),BF),jax.ShapeDtypeStruct((4,2,2,piece,D),BF)],
+        scratch_shapes=[pltpu.VMEM((D,R),BF),pltpu.VMEM((R,D),F32),DMA((2,8)),DMA((2,8)),DMA((2,))],
+        compiler_params=pltpu.CompilerParams(vmem_limit_bytes=VMEM_LIMIT,dimension_semantics=("arbitrary",),collective_id=2,has_side_effects=True),
         cost_estimate=pl.CostEstimate(flops=8*R*D*FF,bytes_accessed=40<<20,transcendentals=0),
-        name="ffn_bwd")(x1,gain,gy,act,dg,wup,wdn)
+        name="ffn_bwd")(x1,gain,gy,act,dg,wup,wdn,res)
 
 def bwd_attn_kernel(half,xc,noise,segc,segr,emb,gain,gx1,ga,q,k,v,mix,lse,wq,wk,wv,wout,cos,sin,
                     dw_o,dwout_o,gin_o,demb_o,dgain_o,hT_s,gh,biasT_s,selfT_s,dq_s,dk_s,dv_s):
@@ -609,6 +657,263 @@
         name="bwd_attn")(xc,noise,segc,segr,emb,gain,gx1,ga,q,k,v,mix,lse,wqkv,wqkv,wqkv,wout,cos,sin)
 
 
+MESH = pl.DeviceIdType.MESH
+INVMEM = pl.BlockSpec(memory_space=pltpu.VMEM)
+ANYSPACE = pl.BlockSpec(memory_space=pl.ANY)
+
+
+def place_ids():
+    return lax.axis_index("ctx"), lax.axis_index("fsdp")
+
+
+def meet(all_ranks, fsdp_partners):
+    c, f = place_ids()
+    sem = pltpu.get_barrier_semaphore()
+    count = 0
+    ranks = [(c + s) % 8 for s in range(1, 8)] if all_ranks else [c + 1 - 2 * (c % 2)]
+    for rank in ranks:
+        pl.semaphore_signal(sem, inc=1, device_id={"ctx": rank}, device_id_type=MESH)
+        count += 1
+    for s in fsdp_partners:
+        other = (f + 2) % 4 if s == 2 else f + 1 - 2 * (f % 2) if s == 1 else 3 - f
+        pl.semaphore_signal(sem, inc=1, device_id={"fsdp": other}, device_id_type=MESH)
+        count += 1
+    pl.semaphore_wait(sem, count)
+
+
+def remote(src, dst, send, recv, where):
+    return pltpu.make_async_remote_copy(src_ref=src, dst_ref=dst, send_sem=send, recv_sem=recv, device_id=where,
+                                        device_id_type=MESH)
+
+
+class ToUnit:
+    def __init__(self, source, target, send, recv, local):
+        self.source, self.target, self.send, self.recv, self.local = source, target, send, recv, local
+        self.c, _ = place_ids()
+
+    def message(self, s):
+        c = self.c
+        t = (c + s) % 8
+        odd, last = t % 2, c // 7
+        slot = (1 - odd) * c + odd * ((1 - last) * (6 - c) + last * 8)
+        return remote(self.source(t // 2, odd), self.target(slot), self.send.at[s], self.recv.at[slot],
+                      {"ctx": t - odd * last})
+
+    def begin(self):
+        for s in range(1, 8):
+            self.message(s).start()
+
+        @pl.when(self.c == 7)
+        def _():
+            self.message(0).start()
+
+        @pl.when(self.c != 7)
+        def _():
+            self.own_safe().start()
+
+    def own_safe(self):
+        c = self.c
+        part = c % 2
+        slot = (1 - part) * c + part * (6 - c + c // 7)
+        return pltpu.make_async_copy(self.source(c // 2, part), self.target(slot), self.local)
+
+    def finish(self):
+        c = self.c
+        part = c % 2
+
+        @pl.when(c == 7)
+        def _():
+            self.message(0).wait_send()
+
+        @pl.when(c != 7)
+        def _():
+            self.own_safe().wait()
+
+        for s in range(1, 8):
+            self.message(s).wait_send()
+        own = (1 - part) * c + part * (6 - c)
+        for slot in range(9):
+            take = slot != own
+            if slot > 6:
+                take = take & (part == 0)
+
+            @pl.when(take)
+            def _():
+                remote(self.target(slot), self.target(slot), self.send.at[0], self.recv.at[slot], {"ctx": c}).wait_recv()
+
+
+class FromUnit:
+    def __init__(self, source, target, send, recv, local):
+        self.source, self.target, self.send, self.recv, self.local = source, target, send, recv, local
+        self.c, _ = place_ids()
+
+    def message(self, s):
+        c = self.c
+        part = c % 2
+        rank = (c + s) % 8
+        slot = (1 - part) * rank + part * (6 - rank + rank // 7)
+        return remote(self.source(slot), self.target(c // 2, part), self.send.at[s], self.recv.at[c], {"ctx": rank})
+
+    def extra(self):
+        c = self.c
+        seq = c // 2
+        return remote(self.source(8), self.target(seq, 1), self.send.at[0], self.recv.at[2 * seq + 1], {"ctx": 7})
+
+    def own(self):
+        c = self.c
+        part = c % 2
+        slot = (1 - part) * c + part * (6 - c + c // 7)
+        return pltpu.make_async_copy(self.source(slot), self.target(c // 2, part), self.local)
+
+    def each(self, remote_op, own_op):
+        c = self.c
+        part = c % 2
+        for s in range(1, 8):
+            rank = (c + s) % 8
+
+            @pl.when((part == 0) | (rank != 7))
+            def _():
+                remote_op(self.message(s))
+
+        @pl.when(part == 0)
+        def _():
+            remote_op(self.extra())
+
+        @pl.when(c != 7)
+        def _():
+            own_op(self.own())
+
+    def begin(self):
+        self.each(lambda m: m.start(), lambda m: m.start())
+
+    def finish(self):
+        self.each(lambda m: m.wait_send(), lambda m: m.wait())
+        c = self.c
+        for block in range(8):
+            @pl.when((c == 7) | (c != block))
+            def _():
+                ref = self.target(block // 2, block % 2)
+                remote(ref, ref, self.send.at[0], self.recv.at[block], {"ctx": c}).wait_recv()
+
+
+class GatherRows:
+    def __init__(self, shard, full, send, recv, local, parts=1):
+        c, f = place_ids()
+        n = shard.shape[0]
+        n2 = n // 2
+        m = n2 // parts
+        h = c % 2
+        sib, far, xn = f + 1 - 2 * (f % 2), (f + 2) % 4, c + 1 - 2 * (c % 2)
+        diag = (sib + 2) % 4
+        rows = lambda start, size: full.at[pl.ds(pl.multiple_of(start, 16), size)]
+        same = lambda ref, i, where: remote(ref, ref, send.at[i], recv.at[i], where)
+        mine = rows(f * n, n)
+        self.copy = pltpu.make_async_copy(shard, mine, local)
+        self.to_core = remote(shard, mine, send.at[0], recv.at[0], {"fsdp": sib})
+        self.from_core = same(rows(sib * n, n), 0, {"fsdp": sib})
+        self.to_far, self.from_far, self.to_x, self.from_x = [], [], [], []
+        self.near_core, self.away_core, self.from_near, self.from_away = [], [], [], []
+        for i in range(parts):
+            a, b = h * n2 + i * m, (1 - h) * n2 + i * m
+            near, away = rows(far * n + a, m), rows(far * n + b, m)
+            k = 1 + 4 * i
+            self.to_far.append(remote(shard.at[pl.ds(pl.multiple_of(a, 16), m)], rows(f * n + a, m), send.at[k], recv.at[k],
+                                      {"fsdp": far}))
+            self.from_far.append(same(near, k, {"fsdp": far}))
+            self.to_x.append(same(near, k + 1, {"ctx": xn}))
+            self.from_x.append(same(away, k + 1, {"ctx": xn}))
+            self.near_core.append(same(near, k + 2, {"fsdp": sib}))
+            self.away_core.append(same(away, k + 3, {"fsdp": sib}))
+            self.from_near.append(same(rows(diag * n + a, m), k + 2, {"fsdp": sib}))
+            self.from_away.append(same(rows(diag * n + b, m), k + 3, {"fsdp": sib}))
+
+    def begin(self):
+        for copy in self.to_far:
+            copy.start()
+        self.to_core.start()
+        self.copy.start()
+
+    def relay_far(self, i=0):
+        self.from_far[i].wait_recv()
+        self.to_x[i].start()
+        self.near_core[i].start()
+
+    def relay_x(self, i=0):
+        self.from_x[i].wait_recv()
+        self.away_core[i].start()
+
+    def finish(self):
+        self.copy.wait()
+        for copy in [self.to_core] + self.to_far + self.to_x + self.near_core + self.away_core:
+            copy.wait_send()
+        for copy in [self.from_core] + self.from_near + self.from_away:
+            copy.wait_recv()
+
+
+def prologue_kernel(clean, meta, qkv, out, small, zeros, blank, clean_o, meta_o, qkv_o, out_o, small_o,
+                    a_send, a_recv, m_send, m_recv, w_send, w_recv, s_send, s_recv, local):
+    c, f = place_ids()
+    meet(True, (1, 2, 3))
+    rows = ToUnit(lambda q, h: clean.at[q, h], lambda i: clean_o.at[i], a_send, a_recv, local.at[0])
+    notes = ToUnit(lambda q, h: meta.at[2 * q + h], lambda i: meta_o.at[i], m_send, m_recv, local.at[1])
+    weights = [GatherRows(qkv, qkv_o, w_send.at[0], w_recv.at[0], local.at[2], 3),
+               GatherRows(out, out_o, w_send.at[1], w_recv.at[1], local.at[3], 3)]
+    weights[0].begin()
+    notes.begin()
+    rows.begin()
+    weights[1].begin()
+    others = [f + 1 - 2 * (f % 2), (f + 2) % 4, 3 - f]
+    sends = [remote(small, small_o.at[f], s_send.at[i], s_recv.at[i], {"fsdp": other}) for i, other in enumerate(others)]
+    for copy in sends:
+        copy.start()
+    own = pltpu.make_async_copy(small, small_o.at[f], local.at[4])
+    own.start()
+    pads = [pltpu.make_async_copy(zeros, clean_o.at[pl.ds(7, 2)], local.at[5]),
+            pltpu.make_async_copy(blank, meta_o.at[pl.ds(7, 2)], local.at[6])]
+
+    @pl.when(c % 2 == 1)
+    def _():
+        for copy in pads:
+            copy.start()
+        for copy in pads:
+            copy.wait()
+
+    for i in range(3):
+        weights[0].relay_far(i)
+    for i in range(3):
+        weights[0].relay_x(i)
+        weights[1].relay_far(i)
+    for i in range(3):
+        weights[1].relay_x(i)
+    own.wait()
+    for i, other in enumerate(others):
+        sends[i].wait_send()
+        remote(small_o.at[other], small_o.at[other], s_send.at[i], s_recv.at[i], {"fsdp": other}).wait_recv()
+    notes.finish()
+    rows.finish()
+    for weight in weights:
+        weight.finish()
+
+
+DMA = pltpu.SemaphoreType.DMA
+
+
+def prologue(clean, meta, qkv, out, small):
+    piece = clean.shape[2]
+    zeros = jnp.zeros((2, piece, D), BF)
+    blank = jnp.concatenate([jnp.full((2, 8, piece), -1, jnp.int32), jnp.zeros((2, 8, 128 - piece), jnp.int32)], axis=2)
+    return pl.pallas_call(
+        prologue_kernel,
+        in_specs=[ANYSPACE] * 2 + [INVMEM] * 5,
+        out_specs=[ANYSPACE] * 5,
+        out_shape=[jax.ShapeDtypeStruct((9, piece, D), BF), jax.ShapeDtypeStruct((9, 8, 128), jnp.int32),
+                   jax.ShapeDtypeStruct((D, 3 * D), BF), jax.ShapeDtypeStruct((D, D), BF),
+                   jax.ShapeDtypeStruct((4,) + small.shape, BF)],
+        scratch_shapes=[DMA((8,)), DMA((9,)), DMA((8,)), DMA((9,)), DMA((2, 13)), DMA((2, 13)), DMA((3,)), DMA((3,)), DMA((7,))],
+        compiler_params=pltpu.CompilerParams(collective_id=0, has_side_effects=True),
+        name="prologue")(clean, meta, qkv, out, small, zeros, blank)
+
+
 def flip(values, axis, count, bit):
     return lax.ppermute(values, axis, [(i, i ^ bit) for i in range(count)])
 
@@ -677,34 +982,30 @@
     ranks = (rank & 1, (rank >> 1) & 1, rank >> 2)
     piece = clean_in.shape[2]
     half = 9 * piece
-    meta = jnp.concatenate([segments.reshape(8, piece), noise.reshape(8, piece)], axis=1)
-    clean = to_unit(exchange(clean_in.reshape(8, piece, D)), part, 0).reshape(half, D)
-    meta = exchange(meta)
-    seg = to_unit(meta[:, :piece], part, -1).reshape(half)
-    mask = to_unit(meta[:, piece:], part, 0).reshape(half, 1)
-    qkv_full = gather_rows(qkv_weight, core, chip)
-    out_full = gather_rows(out_weight, core, chip)
-    small = jnp.concatenate([mask_embed, norm1_gain, norm2_gain, down_bias, up_bias])
-    small = lax.all_gather(small, "fsdp", axis=0).reshape(4, -1)
+    meta = jnp.concatenate([segments.reshape(8, 1, piece), noise.reshape(8, 1, piece)], axis=2)
+    meta = jnp.broadcast_to(meta, (8, 8, 2 * piece))
+    small = jnp.concatenate([mask_embed, norm1_gain, norm2_gain, down_bias, up_bias]).reshape(-1, 128)
+    small = jnp.pad(small, ((0, 16 - small.shape[0]), (0, 0)))
+    clean, meta, qkv_full, out_full, small = prologue(clean_in, meta, qkv_weight, out_weight, small)
+    clean = clean.reshape(half, D)
+    seg = meta[:, 0, :piece].reshape(half)
+    mask = meta[:, 0, piece:].reshape(half, 1)
+    small = small.reshape(4, -1)
     width = mask_embed.shape[0]
     embed, gain_one, gain_two, down_shift = (small[:, i * width:(i + 1) * width].reshape(1, D) for i in range(4))
-    up_shift = small[:, 4 * width:].reshape(1, FF)
-    up_full = gather_rows(up_weight, core, chip)
-    down_full = gather_rows(down_weight, core, chip)
-    cotangent = exchange(out_grad.transpose(0, 2, 1, 3, 4).reshape(8, 2, piece, D))
-    cotangent = to_unit(cotangent, part, 0).transpose(1, 0, 2, 3).reshape(2 * half, D)
+    up_shift = small[:, 4 * width:4 * width + up_bias.shape[0]].reshape(1, FF)
 
     cos_part, sin_part = rope_tables(part * half + jnp.arange(half, dtype=jnp.int32))
     cosine = jnp.tile(cos_part, (1, 4))
     sine = jnp.tile(jnp.concatenate([-sin_part, sin_part], axis=1), (1, 2))
     seg_col, seg_row = seg[:, None], seg[None, :]
 
-    q, k, v, mixed, lse, resid = fwd_attn(clean, mask, seg_col, seg_row, embed, gain_one, qkv_full, out_full, cosine, sine)
+    q, k, v, mixed, lse, resid, up_full, down_full, cotangent = fwd_attn(
+        clean, mask, seg_col, seg_row, embed, gain_one, qkv_full, out_full, cosine, sine, up_weight, down_weight, out_grad)
+    cotangent = cotangent.reshape(2 * half, D)
     result, active, slope = ffn_fwd(resid, gain_two, up_full, up_shift, down_full, down_shift)
-    up_grad, down_grad, up_shift_grad, down_shift_grad, gain_two_grad, grad_resid, grad_attn = ffn_bwd(
-        resid, gain_two, cotangent, active, slope, up_full, down_full)
-    block_out = from_unit(result.reshape(2, 9, piece, D).transpose(1, 0, 2, 3), part)
-    block_out = exchange(block_out).reshape(4, 2, 2, piece, D).transpose(0, 2, 1, 3, 4)
+    up_grad, down_grad, up_shift_grad, down_shift_grad, gain_two_grad, grad_resid, grad_attn, block_out = ffn_bwd(
+        resid, gain_two, cotangent, active, slope, up_full, down_full, result.reshape(2, 9, piece, D))
     qkv_grad, out_weight_grad, grad_in, embed_grad, gain_one_grad = bwd_attn(
         clean, mask, seg_col, seg_row, embed, gain_one, grad_resid, grad_attn, q, k, v, mixed, lse, qkv_full, out_full,
         cosine, sine)

time: 600 us -> 485 us (0.81)
  Pallas kernels: 161 us -> 233 us
  blocking collectives: 116 us -> 49.7 us
  other arithmetic: 71.5 us -> 26.7 us
  starting transfers between devices: 65.2 us -> 32.3 us
  waiting for transfers between devices: 132 us -> 101 us
  local copies, waits for them, and re-layouts: 47.5 us -> 36.3 us
    pallas_call x2 -> x3, Pallas kernels: 77.9 us -> 150 us  [the longest x1 71.7 us: fwd_attn(): pl.pallas_call(partial(fwd_attn_comm_kernel, half), grid=(PAIRS,), in_spe...]
    all_gather x1 -> x0, blocking collectives: 71.7 us -> none  [even_body(): small = lax.all_gather(small, 'fsdp', axis=0).reshape(4, -1)]
    select_n x23 -> x11, other arithmetic: 39.8 us -> 1.81 us  [order_two(): jnp.where(index == 0, jnp.stack([mine, other], axis), jnp.stack([other, m...]
    all_to_all x5 -> x1, starting transfers between devices: 25.3 us -> 4.69 us  [exchange(): return lax.all_to_all(blocks, 'ctx', 0, 0)]
    ppermute x46 -> x33, waiting for transfers between devices: 121 us -> 101 us  [flip(): return lax.ppermute(values, axis, [(i, i ^ bit) for i in range(count)])]
    ppermute x46 -> x33, starting transfers between devices: 39.9 us -> 27.6 us  [flip(): return lax.ppermute(values, axis, [(i, i ^ bit) for i in range(count)])]
    all_to_all x5 -> x1, waiting for transfers between devices: 11 us -> 0.01 us  [exchange(): return lax.all_to_all(blocks, 'ctx', 0, 0)]
  transfers between devices with their start and end apart: 51 -> 34, of which waited for: 23 -> 21; matrix products, arithmetic and copies ran while one was open for 17% -> 9% of each run, Pallas kernels for 7% -> 0%
where the time goes in v2:
time: 485 us; the launch traced here: 481 us
  Pallas kernels  233 us (48%)
  waiting for transfers between devices  101 us (21%)
  blocking collectives  49.7 us (10%)
  local copies, waits for them, and re-layouts  36.3 us (7%)
  starting transfers between devices  32.3 us (7%)
  other arithmetic  26.7 us (6%)
    ppermute x33, waiting for transfers between devices, flip(): return lax.ppermute(values, axis, [(i, i ^ bit) for i in range(count)])  101 us
    pallas_call x1, Pallas kernels, fwd_attn(): pl.pallas_call(partial(fwd_attn_comm_kernel, half), grid=(PAIRS,), in_spe...  71.7 us
    pallas_call x1, Pallas kernels, bwd_attn(): pl.pallas_call(partial(bwd_attn_kernel, half), grid=(PAIRS,), in_specs=[w...  59.4 us
    psum x1, blocking collectives, even_body(): sums = lax.psum(sums, ('ctx', 'fsdp'))  49.7 us
    pallas_call x1, Pallas kernels, ffn_bwd(): pl.pallas_call(ffn_bwd_comm_kernel, grid=(FF // tile,), in_specs=[whole((...  43.1 us
    pallas_call x1, Pallas kernels, prologue(): pl.pallas_call(prologue_kernel, in_specs=[ANYSPACE] * 2 + [INVMEM] * 5, o...  35.1 us
    ppermute x33, starting transfers between devices, flip(): return lax.ppermute(values, axis, [(i, i ^ bit) for i in range(count)])  27.6 us
    pallas_call x1, Pallas kernels, ffn_fwd(): pl.pallas_call(ffn_fwd_kernel, grid=(FF // tile,), in_specs=[whole((R, D)...  24 us
  transfers between devices with their start and end apart: 34, of which 21 were waited for; matrix products, arithmetic and copies ran while one was open for 9% of the time, Pallas kernels for 0%

profile of v2, /device:TPU:0, one launch (start us, length us, event | category | flops | bytes accessed | tf_op | source)
XLA Modules:
  0.0 481.2 jit_solution(15102222255601649535)
XLA Ops:
  1.4 3.4 concatenate.19
  6.8 35.1 %prologue.1 = (bf16[9,64,768]{2,1,0:T(8,128)(2,1)}, s32[9,8,128]{2,1,0:T(8,128)}, bf16[768,2304]{1,0:T(8,128)(2,1)}, bf16[768,768]{1,0:T(8,128)(2,1)}, bf16[4,16,128]{2,1,0:T(8,128)(2,1)}) custom-call(bf16[4,2,64,768]{3,2,1,0:T(8,128)(2,1)} %clean.1, s32[8,8,128]{2,1,0:T(8,128)} %broadcast_in_dim.13.meta, bf16[192,2304]{1,0:T(8,128)(2,1)} %qkv.1, ...), custom_call_target="tpu_custom_call" | custom-call | tf_op jit(solution)/shard_map/prologue/pallas_call | solution.py:905
  51.7 71.7 %fwd_attn.1 = (bf16[1152,768]{1,0:T(8,128)(2,1)}, bf16[1152,768]{1,0:T(8,128)(2,1)}, bf16[1152,768]{1,0:T(8,128)(2,1)}, bf16[1152,768]{1,0:T(8,128)(2,1)}, f32[6...) custom-call(bf16[576,768]{1,0:T(8,128)(2,1)} %bitcast.265, ...), custom_call_target="tpu_custom_call" | custom-call | flops 17666408448 | bytes 16777216 | tf_op jit(solution)/shard_map/fwd_attn/pallas_call | solution.py:478
  123.4 24.0 %ffn_fwd.1 = (bf16[1152,768]{1,0:T(8,128)(2,1)}, bf16[1152,3072]{1,0:T(8,128)(2,1)}, bf16[1152,3072]{1,0:T(8,128)(2,1)}) custom-call(f32[1152,768]{1,0:T(8,128)} %get-tuple-element.46.x1.refs_0_, bf16[1,768]{1,0:T(2,128)(2,1)} %reshape.447.gain.refs_1_, bf16[768,3072]{1,0:T(8,128)(2,1)} %get-tuple-element.48.wup.refs_5_, bf16[1,3072]{1,0:T(2,128)(2,1)} %bitcast.262, ...), custom_call_target="tpu_custom_call" | custom-call | flops 10871635968 | bytes 31457280 | tf_op jit(solution)/shard_map/ffn_fwd/pallas_call | solution.py:513
  147.4 43.1 %ffn_bwd.1 = (bf16[768,3072]{1,0:T(8,128)(2,1)}, bf16[3072,768]{1,0:T(8,128)(2,1)}, f32[1,3072]{1,0:T(1,128)}, f32[1,768]{1,0:T(1,128)}, f32[1,768]{1,0:T(1,128)...) custom-call(f32[1152,768]{1,0:T(8,128)} %get-tuple-element.46.x1.refs_0_, ...), custom_call_target="tpu_custom_call" | custom-call | flops 21743271936 | bytes 41943040 | tf_op jit(solution)/shard_map/ffn_bwd/pallas_call | solution.py:563
  190.5 59.4 %bwd_attn.1 = (bf16[3,768,768]{2,1,0:T(8,128)(2,1)}, bf16[768,768]{1,0:T(8,128)(2,1)}, bf16[576,768]{1,0:T(8,128)(2,1)}, f32[1,768]{1,0:T(1,128)}, f32[1,768]{1,0:T(1,128)}) custom-call(bf16[576,768]{1,0:T(8,128)(2,1)} %bitcast.266, s32[576,1]{1,0:T(8,128)} %reshape_squeeze.4.refs_1_.noise, s32[576,1]{1,0:T(8,128)} %broadcast_in_dim_reshape_squeeze.8.refs_2_.segc, ...), custom_call_target="tpu_custom_call" | custom-call | flops 41448112128 | bytes 31457280 | tf_op jit(solution)/shard_map/bwd_attn/pallas_call | solution.py:649
  251.1 3.4 dynamic-slice_bitcast_fusion
  255.0 1.6 dynamic-slice_bitcast_fusion.1
  257.8 1.3 dynamic-slice_bitcast_fusion.2
  259.9 2.7 collective-permute-start
  267.7 4.4 collective-permute-done.10
  275.2 49.7 %psum.7 = f32[6144]{0:T(1024)S(1)} all-reduce(f32[6144]{0:T(1024)} %constant_dynamic-update-slice_fusion), channel_id=1, replica_groups=mesh['ctx'=8,'fsdp'=4] {'ctx','fsdp'}, use_global_device_ids=true, to_apply=%region_0.1 | all-reduce | flops 6144 | bytes 49152 | tf_op jit(solution)/shard_map/psum | solution.py:1020
  326.6 2.2 collective-permute-start.12
  329.4 1.7 collective-permute-done.12
  331.1 2.9 collective-permute-start.13
  334.0 2.4 fusion.2
  337.4 2.3 collective-permute-start.2
  339.9 1.9 maximum_select_fusion.3
  341.8 4.7 all-to-all-start
  346.5 2.1 collective-permute-start.15
  348.6 2.9 fusion
  352.5 8.1 %collective-permute-done.2 = bf16[3,192,768]{2,1,0:T(8,128)(2,1)} collective-permute-done((bf16[3,192,768]{2,1,0:T(8,128)(2,1)}, bf16[3,192,768]{2,1,0:T(8,128)(2,1)}, u32[]{:S(2)}, u32[]{:S(2)}) %collective-permute-start.2) | collective-permute-done | bytes 884768 | tf_op jit(solution)/shard_map/ppermute | solution.py:918
  360.6 1.4 fusion.5
  362.0 2.1 collective-permute-start.3
  364.1 3.3 fusion.1
  367.4 4.4 collective-permute-done.3
  372.1 2.3 collective-permute-start.18
  375.6 2.3 collective-permute-done.4
  378.1 1.5 collective-permute-done.16
  379.7 4.7 collective-permute-done.5
  387.0 2.0 collective-permute-start.27
  388.9 18.7 %collective-permute-done.18 = bf16[192,3072]{1,0:T(8,128)(2,1)S(1)} collective-permute-done((bf16[192,3072]{1,0:T(8,128)(2,1)S(1)}, bf16[192,3072]{1,0:T(8,128)(2,1)S(1)}, u32[]{:S(2)}, u32[]{:S(2)}) %collective-permute-start.18) | collective-permute-done | bytes 1179680 | tf_op jit(solution)/shard_map/ppermute | solution.py:918
  408.9 1.7 collective-permute-start.19
  413.1 3.6 collective-permute-done.7
  419.9 5.7 %collective-permute-done.19 = bf16[96,3072]{1,0:T(8,128)(2,1)} collective-permute-done((bf16[96,3072]{1,0:T(8,128)(2,1)}, bf16[96,3072]{1,0:T(8,128)(2,1)}, u32[]{:S(2)}, u32[]{:S(2)}) %collective-permute-start.19) | collective-permute-done | bytes 589856 | tf_op jit(solution)/shard_map/ppermute | solution.py:918
  427.1 1.6 collective-permute-done.28
  429.9 6.8 %collective-permute-done.20 = bf16[48,3072]{1,0:T(8,128)(2,1)S(1)} collective-permute-done((bf16[48,3072]{1,0:T(8,128)(2,1)S(1)}, bf16[48,3072]{1,0:T(8,128)(2,1)S(1)}, u32[]{:S(2)}, u32[]{:S(2)}) %collective-permute-start.20) | collective-permute-done | bytes 294944 | tf_op jit(solution)/shard_map/ppermute | solution.py:918
  436.9 5.5 %collective-permute-done.29 = bf16[96,768]{1,0:T(8,128)(2,1)S(1)} collective-permute-done((bf16[96,768]{1,0:T(8,128)(2,1)S(1)}, bf16[96,768]{1,0:T(8,128)(2,1)S(1)}, u32[]{:S(2)}, u32[]{:S(2)}) %collective-permute-start.29) | collective-permute-done | bytes 147488 | tf_op jit(solution)/shard_map/ppermute | solution.py:918
  442.6 2.8 collective-permute-done.21
  445.7 4.5 collective-permute-done.30
  450.3 2.5 collective-permute-done.22
  453.1 4.8 collective-permute-done.31
  458.0 3.0 collective-permute-done.23
  461.2 1.3 pad_maximum_fusion
  462.5 9.0 %collective-permute-done.32 = bf16[384,768]{1,0:T(8,128)(2,1)S(1)} collective-permute-done((bf16[384,768]{1,0:T(8,128)(2,1)S(1)}, bf16[384,768]{1,0:T(8,128)(2,1)S(1)}, u32[]{:S(2)}, u32[]{:S(2)}) %collective-permute-start.32) | collective-permute-done | bytes 589856 | tf_op jit(solution)/shard_map/ppermute | solution.py:918
  471.8 1.7 bitcast_convert_fusion
  473.4 4.5 collective-permute-done.24
  478.1 1.7 bitcast_convert_fusion.1
  (147 shorter events, 45.5 us)
Async XLA Ops:
  251.0 11.7 %collective-permute-start.9 = (bf16[2,192,768]{2,1,0:T(8,128)(2,1)S(1)}, bf16[2,192,768]{2,1,0:T(8,128)(2,1)S(1)}, u32[]{:S(2)}, u32[]{:S(2)}) collective-permute-start(bf16[2,192,768]{2,1,0:T(8,128)(2,1)S(1)} %dynamic-slice_bitcast_fusion.8), channel_id=1, source_target_pairs={{0,1},{1,0},{2,3},{3,2},{4,5},{5,4},{6,7},{7,6},{8,9},{9,8},{10,11... | collective-permute-start | bytes 1769480 | tf_op jit(solution)/shard_map/ppermute | solution.py:918
  251.1 3.9 copy-start
  254.5 94.1 %collective-permute-start.25 = (bf16[2,768,768]{2,1,0:T(8,128)(2,1)}, bf16[2,768,768]{2,1,0:T(8,128)(2,1)}, u32[]{:S(2)}, u32[]{:S(2)}) collective-permute-start(bf16[2,768,768]{2,1,0:T(8,128)(2,1)} %dynamic-slice_bitcast_fusion), channel_id=1, source_target_pairs={{0,1},{1,0},{2,3},{3,2},{4,5},{5,4},{6,7},{7,6},{8,9},{9,8},{10,11... | collective-permute-start | bytes 7077896 | tf_op jit(solution)/shard_map/ppermute | solution.py:918
  255.0 2.9 copy-start.1
  256.5 107.6 %collective-permute-start.17 = (bf16[2,192,3072]{2,1,0:T(8,128)(2,1)}, bf16[2,192,3072]{2,1,0:T(8,128)(2,1)}, u32[]{:S(2)}, u32[]{:S(2)}) collective-permute-start(bf16[2,192,3072]{2,1,0:T(8,128)(2,1)} %dynamic-slice_bitcast_fusion.1), channel_id=1, source_target_pairs={{0,1},{1,0},{2,3},{3,2},{4,5},{5,4},{6,7},{7,6},{8,9},{9,8},{10,11... | collective-permute-start | bytes 7077896 | tf_op jit(solution)/shard_map/ppermute | solution.py:918
  257.8 1.4 copy-start.2
  257.8 4.7 copy-start.9
  257.8 4.8 copy-start.8
  257.8 4.8 copy-start.7
  257.8 4.8 %copy-start.6 = (f32[1,768]{1,0:T(1,128)S(1)}, f32[1,768]{1,0:T(1,128)}, u32[]{:S(2)}) copy-start(f32[1,768]{1,0:T(1,128)} %get-tuple-element.65) | copy-start | bytes 9220
  257.8 4.9 %copy-start.4 = (bf16[768,768]{1,0:T(8,128)(2,1)S(1)}, bf16[768,768]{1,0:T(8,128)(2,1)}, u32[]{:S(2)}) copy-start(bf16[768,768]{1,0:T(8,128)(2,1)} %get-tuple-element.68) | copy-start | bytes 3538948
  259.2 74.9 %collective-permute-start.1 = (bf16[3,2,192,768]{3,2,1,0:T(8,128)(2,1)}, bf16[3,2,192,768]{3,2,1,0:T(8,128)(2,1)}, u32[]{:S(2)}, u32[]{:S(2)}) collective-permute-start(bf16[3,2,192,768]{3,2,1,0:T(8,128)(2,1)} %dynamic-slice_bitcast_fusion.2), channel_id=1, source_target_pairs={{0,1},{1,0},{2,3},{3,2},{4,5},{5,4},{6,7},{7,6},{8,9},{9,8},{10,11... | collective-permute-start | bytes 5308424 | tf_op jit(solution)/shard_map/ppermute | solution.py:918
  259.9 80.1 %collective-permute-start = (bf16[64,768]{1,0:T(8,128)(2,1)}, bf16[64,768]{1,0:T(8,128)(2,1)}, u32[]{:S(2)}, u32[]{:S(2)}) collective-permute-start(bf16[64,768]{1,0:T(8,128)(2,1)} %slice.60), channel_id=1, source_target_pairs={{0,4},{4,0},{8,12},{12,8},{16,20},{20,16},{24,28},{28,24},{1,5},{5... | collective-permute-start | bytes 294920 | tf_op jit(solution)/shard_map/ppermute | solution.py:918
  262.9 9.2 %collective-permute-start.10 = (bf16[192,768]{1,0:T(8,128)(2,1)S(1)}, bf16[192,768]{1,0:T(8,128)(2,1)S(1)}, u32[]{:S(2)}, u32[]{:S(2)}) collective-permute-start(bf16[192,768]{1,0:T(8,128)(2,1)S(1)} %dynamic-slice_bitcast_fusion.12), channel_id=1, source_target_pairs={{0,2},{1,3},{2,0},{3,1},{4,6},{5,7},{6,4},{7,5},{8,10},{9,11},{10,... | collective-permute-start | bytes 884744 | tf_op jit(solution)/shard_map/ppermute | solution.py:918
  272.2 53.4 %collective-permute-start.11 = (bf16[96,768]{1,0:T(8,128)(2,1)S(1)}, bf16[96,768]{1,0:T(8,128)(2,1)}, u32[]{:S(2)}, u32[]{:S(2)}) collective-permute-start(bf16[96,768]{1,0:T(8,128)(2,1)S(1)} %dynamic-slice_bitcast_fusion.16), channel_id=1, source_target_pairs={{0,4},{4,0},{8,12},{12,8},{16,20},{20,16},{24,28},{28,24},{1,5},{5... | collective-permute-start | bytes 442376 | tf_op jit(solution)/shard_map/ppermute | solution.py:918
  273.9 0.7 copy-start.5
  326.6 4.5 collective-permute-start.12
  331.1 8.6 %collective-permute-start.13 = (bf16[24,768]{1,0:T(8,128)(2,1)S(1)}, bf16[24,768]{1,0:T(8,128)(2,1)S(1)}, u32[]{:S(2)}, u32[]{:S(2)}) collective-permute-start(bf16[24,768]{1,0:T(8,128)(2,1)S(1)} %dynamic-slice_bitcast_fusion.19), channel_id=1, source_target_pairs={{0,16},{4,20},{8,24},{12,28},{16,0},{20,4},{24,8},{28,12},{1,17},{... | collective-permute-start | bytes 110600 | tf_op jit(solution)/shard_map/ppermute | solution.py:918
  337.4 23.2 %collective-permute-start.2 = (bf16[3,192,768]{2,1,0:T(8,128)(2,1)}, bf16[3,192,768]{2,1,0:T(8,128)(2,1)}, u32[]{:S(2)}, u32[]{:S(2)}) collective-permute-start(bf16[3,192,768]{2,1,0:T(8,128)(2,1)} %dynamic-slice_bitcast_fusion.5), channel_id=1, source_target_pairs={{0,2},{1,3},{2,0},{3,1},{4,6},{5,7},{6,4},{7,5},{8,10},{9,11},{10,... | collective-permute-start | bytes 2654216 | tf_op jit(solution)/shard_map/ppermute | solution.py:918
  339.8 6.7 %collective-permute-start.14 = (bf16[24,768]{1,0:T(8,128)(2,1)S(1)}, bf16[24,768]{1,0:T(8,128)(2,1)S(1)}, u32[]{:S(2)}, u32[]{:S(2)}) collective-permute-start(bf16[24,768]{1,0:T(8,128)(2,1)S(1)} %fusion.20), channel_id=1, source_target_pairs={{0,16},{4,20},{8,24},{12,28},{16,0},{20,4},{24,8},{28,12},{1,17},{... | collective-permute-start | bytes 110600 | tf_op jit(solution)/shard_map/ppermute | solution.py:918
  341.8 70.1 %all-to-all-start = ((bf16[8,64,768]{2,1,0:T(8,128)(2,1)}), bf16[8,64,768]{2,1,0:T(8,128)(2,1)S(1)}, u32[]{:S(2)}, u32[]{:S(2)}) async-start(bf16[8,64,768]{2,1,0:T(8,128)(2,1)} %maximum_select_fusion.3), calls=%async_computation | async-start | bytes 1572864 | tf_op jit(solution)/shard_map/all_to_all | solution.py:973
  346.5 27.9 %collective-permute-start.15 = (bf16[48,768]{1,0:T(8,128)(2,1)S(1)}, bf16[48,768]{1,0:T(8,128)(2,1)S(1)}, u32[]{:S(2)}, u32[]{:S(2)}) collective-permute-start(bf16[48,768]{1,0:T(8,128)(2,1)S(1)} %bitcast.246), channel_id=1, source_target_pairs={{0,8},{4,12},{8,0},{12,4},{16,24},{20,28},{24,16},{28,20},{1,9},{5... | collective-permute-start | bytes 221192 | tf_op jit(solution)/shard_map/ppermute | solution.py:918
  351.6 34.2 %collective-permute-start.26 = (bf16[768,768]{1,0:T(8,128)(2,1)S(1)}, bf16[768,768]{1,0:T(8,128)(2,1)S(1)}, u32[]{:S(2)}, u32[]{:S(2)}) collective-permute-start(bf16[768,768]{1,0:T(8,128)(2,1)S(1)} %dynamic-slice_bitcast_fusion.3), channel_id=1, source_target_pairs={{0,2},{1,3},{2,0},{3,1},{4,6},{5,7},{6,4},{7,5},{8,10},{9,11},{10,... | collective-permute-start | bytes 3538952 | tf_op jit(solution)/shard_map/ppermute | solution.py:918
  362.0 9.8 %collective-permute-start.3 = (bf16[3,96,768]{2,1,0:T(8,128)(2,1)S(1)}, bf16[3,96,768]{2,1,0:T(8,128)(2,1)S(1)}, u32[]{:S(2)}, u32[]{:S(2)}) collective-permute-start(bf16[3,96,768]{2,1,0:T(8,128)(2,1)S(1)} %dynamic-slice_bitcast_fusion.9), channel_id=1, source_target_pairs={{0,4},{4,0},{8,12},{12,8},{16,20},{20,16},{24,28},{28,24},{1,5},{5... | collective-permute-start | bytes 1327112 | tf_op jit(solution)/shard_map/ppermute | solution.py:918
  372.0 6.0 %collective-permute-start.4 = (bf16[3,48,768]{2,1,0:T(8,128)(2,1)S(1)}, bf16[3,48,768]{2,1,0:T(8,128)(2,1)S(1)}, u32[]{:S(2)}, u32[]{:S(2)}) collective-permute-start(bf16[3,48,768]{2,1,0:T(8,128)(2,1)S(1)} %dynamic-slice_bitcast_fusion.13), channel_id=1, source_target_pairs={{0,8},{4,12},{8,0},{12,4},{16,24},{20,28},{24,16},{28,20},{1,9},{5... | collective-permute-start | bytes 663560 | tf_op jit(solution)/shard_map/ppermute | solution.py:918
  372.1 35.5 %collective-permute-start.18 = (bf16[192,3072]{1,0:T(8,128)(2,1)S(1)}, bf16[192,3072]{1,0:T(8,128)(2,1)S(1)}, u32[]{:S(2)}, u32[]{:S(2)}) collective-permute-start(bf16[192,3072]{1,0:T(8,128)(2,1)S(1)} %dynamic-slice_bitcast_fusion.4), channel_id=1, source_target_pairs={{0,2},{1,3},{2,0},{3,1},{4,6},{5,7},{6,4},{7,5},{8,10},{9,11},{10,... | collective-permute-start | bytes 3538952 | tf_op jit(solution)/shard_map/ppermute | solution.py:918
  374.4 5.2 %collective-permute-start.16 = (bf16[96,768]{1,0:T(8,128)(2,1)S(1)}, bf16[96,768]{1,0:T(8,128)(2,1)S(1)}, u32[]{:S(2)}, u32[]{:S(2)}) collective-permute-start(bf16[96,768]{1,0:T(8,128)(2,1)S(1)} %bitcast.238), channel_id=1, source_target_pairs={{0,4},{4,0},{8,12},{12,8},{16,20},{20,16},{24,28},{28,24},{1,5},{5... | collective-permute-start | bytes 442376 | tf_op jit(solution)/shard_map/ppermute | solution.py:918
  378.0 6.3 %collective-permute-start.5 = (bf16[3,24,768]{2,1,0:T(8,128)(2,1)S(1)}, bf16[3,24,768]{2,1,0:T(8,128)(2,1)S(1)}, u32[]{:S(2)}, u32[]{:S(2)}) collective-permute-start(bf16[3,24,768]{2,1,0:T(8,128)(2,1)S(1)} %dynamic-slice_bitcast_fusion.17), channel_id=1, source_target_pairs={{0,16},{4,20},{8,24},{12,28},{16,0},{20,4},{24,8},{28,12},{1,17},{... | collective-permute-start | bytes 331784 | tf_op jit(solution)/shard_map/ppermute | solution.py:918
  384.4 26.2 %collective-permute-start.6 = (bf16[3,24,768]{2,1,0:T(8,128)(2,1)S(1)}, bf16[3,24,768]{2,1,0:T(8,128)(2,1)S(1)}, u32[]{:S(2)}, u32[]{:S(2)}) collective-permute-start(bf16[3,24,768]{2,1,0:T(8,128)(2,1)S(1)} %fusion.18), channel_id=1, source_target_pairs={{0,16},{4,20},{8,24},{12,28},{16,0},{20,4},{24,8},{28,12},{1,17},{... | collective-permute-start | bytes 331784 | tf_op jit(solution)/shard_map/ppermute | solution.py:918
  387.0 31.3 %collective-permute-start.27 = (bf16[384,768]{1,0:T(8,128)(2,1)}, bf16[384,768]{1,0:T(8,128)(2,1)}, u32[]{:S(2)}, u32[]{:S(2)}) collective-permute-start(bf16[384,768]{1,0:T(8,128)(2,1)} %dynamic-slice_bitcast_fusion.6), channel_id=1, source_target_pairs={{0,4},{4,0},{8,12},{12,8},{16,20},{20,16},{24,28},{28,24},{1,5},{5... | collective-permute-start | bytes 1769480 | tf_op jit(solution)/shard_map/ppermute | solution.py:918
  408.9 16.6 %collective-permute-start.19 = (bf16[96,3072]{1,0:T(8,128)(2,1)}, bf16[96,3072]{1,0:T(8,128)(2,1)}, u32[]{:S(2)}, u32[]{:S(2)}) collective-permute-start(bf16[96,3072]{1,0:T(8,128)(2,1)} %dynamic-slice_bitcast_fusion.7), channel_id=1, source_target_pairs={{0,4},{4,0},{8,12},{12,8},{16,20},{20,16},{24,28},{28,24},{1,5},{5... | collective-permute-start | bytes 1769480 | tf_op jit(solution)/shard_map/ppermute | solution.py:918
  410.6 6.1 %collective-permute-start.7 = (bf16[3,48,768]{2,1,0:T(8,128)(2,1)S(1)}, bf16[3,48,768]{2,1,0:T(8,128)(2,1)}, u32[]{:S(2)}, u32[]{:S(2)}) collective-permute-start(bf16[3,48,768]{2,1,0:T(8,128)(2,1)S(1)} %bitcast.230), channel_id=1, source_target_pairs={{0,8},{4,12},{8,0},{12,4},{16,24},{20,28},{24,16},{28,20},{1,9},{5... | collective-permute-start | bytes 663560 | tf_op jit(solution)/shard_map/ppermute | solution.py:918
  417.8 27.7 %collective-permute-start.8 = (bf16[3,96,768]{2,1,0:T(8,128)(2,1)S(1)}, bf16[3,96,768]{2,1,0:T(8,128)(2,1)S(1)}, u32[]{:S(2)}, u32[]{:S(2)}) collective-permute-start(bf16[3,96,768]{2,1,0:T(8,128)(2,1)S(1)} %bitcast.214), channel_id=1, source_target_pairs={{0,4},{4,0},{8,12},{12,8},{16,20},{20,16},{24,28},{28,24},{1,5},{5... | collective-permute-start | bytes 1327112 | tf_op jit(solution)/shard_map/ppermute | solution.py:918
  419.5 9.2 %collective-permute-start.28 = (bf16[192,768]{1,0:T(8,128)(2,1)S(1)}, bf16[192,768]{1,0:T(8,128)(2,1)S(1)}, u32[]{:S(2)}, u32[]{:S(2)}) collective-permute-start(bf16[192,768]{1,0:T(8,128)(2,1)S(1)} %dynamic-slice_bitcast_fusion.10), channel_id=1, source_target_pairs={{0,8},{4,12},{8,0},{12,4},{16,24},{20,28},{24,16},{28,20},{1,9},{5... | collective-permute-start | bytes 884744 | tf_op jit(solution)/shard_map/ppermute | solution.py:918
  426.8 9.9 %collective-permute-start.20 = (bf16[48,3072]{1,0:T(8,128)(2,1)S(1)}, bf16[48,3072]{1,0:T(8,128)(2,1)S(1)}, u32[]{:S(2)}, u32[]{:S(2)}) collective-permute-start(bf16[48,3072]{1,0:T(8,128)(2,1)S(1)} %dynamic-slice_bitcast_fusion.11), channel_id=1, source_target_pairs={{0,8},{4,12},{8,0},{12,4},{16,24},{20,28},{24,16},{28,20},{1,9},{5... | collective-permute-start | bytes 884744 | tf_op jit(solution)/shard_map/ppermute | solution.py:918
  428.9 13.6 %collective-permute-start.29 = (bf16[96,768]{1,0:T(8,128)(2,1)S(1)}, bf16[96,768]{1,0:T(8,128)(2,1)S(1)}, u32[]{:S(2)}, u32[]{:S(2)}) collective-permute-start(bf16[96,768]{1,0:T(8,128)(2,1)S(1)} %dynamic-slice_bitcast_fusion.14), channel_id=1, source_target_pairs={{0,16},{4,20},{8,24},{12,28},{16,0},{20,4},{24,8},{28,12},{1,17},{... | collective-permute-start | bytes 442376 | tf_op jit(solution)/shard_map/ppermute | solution.py:918
  436.8 8.5 %collective-permute-start.21 = (bf16[24,3072]{1,0:T(8,128)(2,1)S(1)}, bf16[24,3072]{1,0:T(8,128)(2,1)S(1)}, u32[]{:S(2)}, u32[]{:S(2)}) collective-permute-start(bf16[24,3072]{1,0:T(8,128)(2,1)S(1)} %dynamic-slice_bitcast_fusion.15), channel_id=1, source_target_pairs={{0,16},{4,20},{8,24},{12,28},{16,0},{20,4},{24,8},{28,12},{1,17},{... | collective-permute-start | bytes 442376 | tf_op jit(solution)/shard_map/ppermute | solution.py:918
  442.5 7.7 %collective-permute-start.30 = (bf16[96,768]{1,0:T(8,128)(2,1)S(1)}, bf16[96,768]{1,0:T(8,128)(2,1)S(1)}, u32[]{:S(2)}, u32[]{:S(2)}) collective-permute-start(bf16[96,768]{1,0:T(8,128)(2,1)S(1)} %fusion.15), channel_id=1, source_target_pairs={{0,16},{4,20},{8,24},{12,28},{16,0},{20,4},{24,8},{28,12},{1,17},{... | collective-permute-start | bytes 442376 | tf_op jit(solution)/shard_map/ppermute | solution.py:918
  445.4 7.5 %collective-permute-start.22 = (bf16[24,3072]{1,0:T(8,128)(2,1)S(1)}, bf16[24,3072]{1,0:T(8,128)(2,1)S(1)}, u32[]{:S(2)}, u32[]{:S(2)}) collective-permute-start(bf16[24,3072]{1,0:T(8,128)(2,1)S(1)} %fusion.16), channel_id=1, source_target_pairs={{0,16},{4,20},{8,24},{12,28},{16,0},{20,4},{24,8},{28,12},{1,17},{... | collective-permute-start | bytes 442376 | tf_op jit(solution)/shard_map/ppermute | solution.py:918
  450.2 7.6 %collective-permute-start.31 = (bf16[192,768]{1,0:T(8,128)(2,1)S(1)}, bf16[192,768]{1,0:T(8,128)(2,1)S(1)}, u32[]{:S(2)}, u32[]{:S(2)}) collective-permute-start(bf16[192,768]{1,0:T(8,128)(2,1)S(1)} %bitcast.228), channel_id=1, source_target_pairs={{0,8},{4,12},{8,0},{12,4},{16,24},{20,28},{24,16},{28,20},{1,9},{5... | collective-permute-start | bytes 884744 | tf_op jit(solution)/shard_map/ppermute | solution.py:918
  452.9 8.2 %collective-permute-start.23 = (bf16[48,3072]{1,0:T(8,128)(2,1)S(1)}, bf16[48,3072]{1,0:T(8,128)(2,1)S(1)}, u32[]{:S(2)}, u32[]{:S(2)}) collective-permute-start(bf16[48,3072]{1,0:T(8,128)(2,1)S(1)} %bitcast.226), channel_id=1, source_target_pairs={{0,8},{4,12},{8,0},{12,4},{16,24},{20,28},{24,16},{28,20},{1,9},{5... | collective-permute-start | bytes 884744 | tf_op jit(solution)/shard_map/ppermute | solution.py:918
  458.0 13.6 %collective-permute-start.32 = (bf16[384,768]{1,0:T(8,128)(2,1)S(1)}, bf16[384,768]{1,0:T(8,128)(2,1)S(1)}, u32[]{:S(2)}, u32[]{:S(2)}) collective-permute-start(bf16[384,768]{1,0:T(8,128)(2,1)S(1)} %bitcast.204), channel_id=1, source_target_pairs={{0,4},{4,0},{8,12},{12,8},{16,20},{20,16},{24,28},{28,24},{1,5},{5... | collective-permute-start | bytes 1769480 | tf_op jit(solution)/shard_map/ppermute | solution.py:918
  461.1 16.8 %collective-permute-start.24 = (bf16[96,3072]{1,0:T(8,128)(2,1)S(1)}, bf16[96,3072]{1,0:T(8,128)(2,1)S(1)}, u32[]{:S(2)}, u32[]{:S(2)}) collective-permute-start(bf16[96,3072]{1,0:T(8,128)(2,1)S(1)} %bitcast.206), channel_id=1, source_target_pairs={{0,4},{4,0},{8,12},{12,8},{16,20},{20,16},{24,28},{28,24},{1,5},{5... | collective-permute-start | bytes 1769480 | tf_op jit(solution)/shard_map/ppermute | solution.py:918
  478.1 1.8 copy-start.3

commit v3 on v2

--- a/solution.py
+++ b/solution.py
@@ -2,6 +2,7 @@
 
 import jax
 import jax.numpy as jnp
+import numpy as np
 from jax import lax
 from jax.experimental import pallas as pl
 from jax.experimental.pallas import tpu as pltpu
@@ -379,14 +380,16 @@
     noisy=jnp.where(noise_ref[...]==1,emb_ref[...].astype(F32),clean)
     return noisy,clean
 
-def fwd_attn_kernel(half,xc,noise,segc,segr,emb,gain,wq,wk,wv,wout,cos,sin,
+def fwd_attn_kernel(half,xc,noise,segc,segr,small,wqkv,wout,trig,
                     q_o,k_o,v_o,mix_o,lse_o,x1_o,h_s,bias_s,self_s,mix_s):
     p=pl.program_id(0)
     tiles=tiles_of(half)
     @pl.when(p==0)
     def _():
-        g=gain[...].astype(F32)
-        for c,rows in enumerate(layer_rows(xc,noise,emb)):
+        g=vector_row(small,1)
+        clean=jnp.concatenate([xc[i] for i in range(9)],axis=0).astype(F32)
+        noisy=jnp.where(noise[...]==1,vector_row(small,0),clean)
+        for c,rows in enumerate((noisy,clean)):
             x1_o[c*half:(c+1)*half]=rows
             n,_=norm_rows(rows)
             h_s[c*half:(c+1)*half]=(n*g).astype(BF)
@@ -402,11 +405,13 @@
             same=segc[s:n]==segr[:,s:n]
             self_s[s:n,:m]=jnp.where(same&(kb==qb),0.0,NEG)
     h=h_s[...]
-    cs=jnp.concatenate([cos[...],cos[...]],axis=0)
-    sn=jnp.concatenate([sin[...],sin[...]],axis=0)
-    z=dot_nn(h,wq[...]); q_o[...]=((z*cs+swap_halves(z)*sn).astype(BF)*BF(HEAD**-0.5)).astype(BF)
-    z=dot_nn(h,wk[...]); k_o[...]=(z*cs+swap_halves(z)*sn).astype(BF)
-    v_o[...]=dot_nn(h,wv[...]).astype(BF)
+    cs=jnp.concatenate([trig[:,:PAIR]]*2,axis=0)
+    sn=jnp.concatenate([trig[:,PAIR:]]*2,axis=0)
+    block=lambda i: wqkv[:,pl.ds(pl.multiple_of(i*D+p*PAIR,PAIR),PAIR)]
+    zq=dot_nn(h,jnp.concatenate([block(0),block(1)],axis=1))
+    z=zq[:,:PAIR]; q_o[...]=((z*cs+swap_halves(z)*sn).astype(BF)*BF(HEAD**-0.5)).astype(BF)
+    z=zq[:,PAIR:]; k_o[...]=(z*cs+swap_halves(z)*sn).astype(BF)
+    v_o[...]=dot_nn(h,block(2)).astype(BF)
     idx=0
     for s,m in tiles:
         n=s+m
@@ -438,144 +443,287 @@
 
 def whole(shape): return pl.BlockSpec(shape,lambda *i:(0,)*len(shape))
 
+def vector_row(small,i):
+    return jnp.concatenate([small[f,i:i+1,:D//4] for f in range(4)],axis=1).astype(F32)
+
 def fwd_attn_comm_kernel(half,*refs):
-    ins,(up,down,gout,zeros),rest=refs[:12],refs[12:16],refs[16:]
-    outs,(up_o,down_o,cot_o),scratch=rest[:6],rest[6:9],rest[9:13]
-    a_send,a_recv,w_send,w_recv,local=rest[13:]
+    clean,meta,gout,trig,qkv,out,up,down,small,zeros,blank=refs[:11]
+    q_o,k_o,v_o,mix_o,lse_o,x1_o,noise_o,segc_o,segr_o,vec_o,bias_o,qkv_o,out_o,up_o,down_o,cot_o,clean_o=refs[11:28]
+    h_s,bias_s,self_s,mix_s,clean_s,meta_s,small_s,qkv_s,out_s,trig_s=refs[28:38]
+    a_send,a_recv,m_send,m_recv,c_send,c_recv,w_send,w_recv,s_send,s_recv,local=refs[38:]
     p=pl.program_id(0)
-    c,_=place_ids()
-    weights=[GatherRows(up,up_o,w_send.at[0],w_recv.at[0],local.at[0]),GatherRows(down,down_o,w_send.at[1],w_recv.at[1],local.at[1])]
-    rows=[ToUnit(lambda q,h,i=i:gout.at[q,i,h],lambda t,i=i:cot_o.at[i,t],a_send.at[i],a_recv.at[i],local.at[2+i]) for i in range(2)]
-    pads=[pltpu.make_async_copy(zeros,cot_o.at[i,pl.ds(7,2)],local.at[4+i]) for i in range(2)]
+    c,f=place_ids()
+    piece=half//9
+    weight=lambda i,shard,full,parts: GatherRows(shard,full,w_send.at[i],w_recv.at[i],local.at[i],parts)
+    w_qkv,w_out,w_up,w_down=weight(0,qkv,qkv_s,3),weight(1,out,out_s,1),weight(2,up,up_o,3),weight(3,down,down_o,3)
+    rows=ToUnit(lambda q,h:clean.at[q,h],lambda t:clean_s.at[t],a_send,a_recv,local.at[4])
+    notes=ToUnit(lambda q,h:meta.at[2*q+h],lambda t:meta_s.at[t],m_send,m_recv,local.at[5])
+    grads=[ToUnit(lambda q,h:gout.at[q,0,h],lambda t:cot_o.at[t],c_send,c_recv,local.at[6])]
+    copies=[pltpu.make_async_copy(qkv_s,qkv_o,local.at[8]),pltpu.make_async_copy(out_s,out_o,local.at[9]),pltpu.make_async_copy(clean_s,clean_o,local.at[10])]
+    others=[f+1-2*(f%2),(f+2)%4,3-f]
     @pl.when(p==0)
     def _():
-        meet(True,(1,2))
-        for w in weights: w.begin()
-        for r in rows: r.begin()
+        meet(True,(1,2,3))
+        w_qkv.begin()
+        notes.begin()
+        rows.begin()
+        sends=[remote(small,small_s.at[f],s_send.at[i],s_recv.at[i],{"fsdp":other}) for i,other in enumerate(others)]
+        for d in sends: d.start()
+        own=pltpu.make_async_copy(small,small_s.at[f],local.at[11])
+        own.start()
+        table=pltpu.make_async_copy(trig.at[c%2],trig_s,local.at[12])
+        table.start()
+        w_out.begin()
+        w_up.begin()
+        w_down.begin()
+        for i in range(3): w_qkv.relay_far(i)
+        pads=[pltpu.make_async_copy(zeros,clean_s.at[pl.ds(7,2)],local.at[13]),pltpu.make_async_copy(blank,meta_s.at[pl.ds(7,2)],local.at[13])]
+        pads.append(pltpu.make_async_copy(zeros,cot_o.at[pl.ds(7,2)],local.at[13]))
         @pl.when(c%2==1)
         def _():
-            for d in pads: d.start()
-            for d in pads: d.wait()
-    fwd_attn_kernel(half,*ins,*outs,*scratch)
-    @pl.when(p==2)
-    def _():
-        for w in weights: w.relay_far()
-    @pl.when(p==3)
-    def _():
-        for w in weights: w.relay_x()
+            for d in pads:
+                d.start()
+                d.wait()
+        for i in range(3): w_qkv.relay_x(i)
+        for r in grads: r.begin()
+        own.wait()
+        table.wait()
+        for i,other in enumerate(others):
+            sends[i].wait_send()
+            remote(small_s.at[other],small_s.at[other],s_send.at[i],s_recv.at[i],{"fsdp":other}).wait_recv()
+        notes.finish()
+        lane=lax.broadcasted_iota(jnp.int32,(1,128),1)
+        for i in range(9):
+            t=jnp.broadcast_to(meta_s[i,0:1].astype(F32),(128,128)).T
+            segc_o[i*piece:(i+1)*piece]=t[:piece,0:1]
+            noise_o[i*piece:(i+1)*piece]=t[piece:,0:1].astype(jnp.int32)
+        for i in range(5):
+            even=meta_s[2*i,0:1].astype(F32)
+            odd=pltpu.roll(meta_s[min(2*i+1,8)].astype(F32),64,1)[0:1]
+            segr_o[:,i*128:(i+1)*128]=jnp.where(lane<64,even,odd)
+        for i in range(2): vec_o[i:i+1]=vector_row(small_s,2+i)
+        for i in range(2): vec_o[2+i:3+i]=vector_row(small_s,i)
+        for g in range(4):
+            for i in range(3): bias_o[:,g*768+i*256:g*768+(i+1)*256]=small_s[g,4+i:5+i].astype(F32)
+        rows.finish()
+        w_qkv.finish()
+        copies[0].start()
+        copies[2].start()
+    fwd_attn_kernel(half,clean_s,noise_o,segc_o,segr_o,small_s,qkv_s,out_s,trig_s,q_o,k_o,v_o,mix_o,lse_o,x1_o,h_s,bias_s,self_s,mix_s)
+    def at(i,*ops):
+        @pl.when(p==i)
+        def _():
+            for op in ops: op()
+    at(0,w_out.relay_far,*[partial(w_up.relay_far,i) for i in range(3)])
+    at(1,w_out.relay_x,partial(w_up.relay_x,0),partial(w_down.relay_far,0))
+    at(2,partial(w_up.relay_x,1),partial(w_down.relay_far,1),partial(w_down.relay_far,2))
+    at(3,partial(w_up.relay_x,2),w_out.finish,copies[1].start,partial(w_down.relay_x,0))
+    at(4,partial(w_down.relay_x,1),partial(w_down.relay_x,2))
     @pl.when(p==pl.num_programs(0)-1)
     def _():
-        for w in weights: w.finish()
-        for r in rows: r.finish()
-
-def fwd_attn(xc,noise,segc,segr,emb,gain,wqkv,wout,cos,sin,up,down,gout):
-    half=xc.shape[0]; R=2*half
-    piece=gout.shape[3]
+        for w in (w_up,w_down): w.finish()
+        for r in grads: r.finish()
+        for d in copies: d.wait()
+
+def whole(shape): return pl.BlockSpec(shape,lambda *i:(0,)*len(shape))
+def once(shape): return pl.BlockSpec(shape,lambda *i:(0,)*len(shape),pipeline_mode=pl.Buffered(1))
+
+def fwd_attn(clean,meta,gout,trig,qkv,out,up,down,small):
+    piece=clean.shape[2]; half=9*piece; R=2*half
     zeros=jnp.zeros((2,piece,D),BF)
+    blank=jnp.concatenate([jnp.full((2,8,piece),-1,jnp.int32),jnp.zeros((2,8,128-piece),jnp.int32)],axis=2)
     nt=len(tiles_of(half))*2; ntp=-(-nt//8)*8
-    ws=[pl.BlockSpec((D,PAIR),(lambda off:(lambda p:(0,off+p)))(o*PAIRS)) for o in range(3)]
     rows=pl.BlockSpec((R,PAIR),lambda p:(0,p))
+    sds=jax.ShapeDtypeStruct
     return pl.pallas_call(partial(fwd_attn_comm_kernel,half),grid=(PAIRS,),
-        in_specs=[whole((half,D)),whole((half,1)),whole((half,1)),whole((1,half)),whole((1,D)),whole((1,D)),*ws,whole((D,D)),whole((half,PAIR)),whole((half,PAIR)),whole(up.shape),whole(down.shape),ANYSPACE,whole(zeros.shape)],
-        out_specs=[rows,rows,rows,rows,pl.BlockSpec((1,ntp,256),lambda p:(p,0,0)),whole((R,D))]+[ANYSPACE]*3,
-        out_shape=[jax.ShapeDtypeStruct((R,D),BF)]*4+[jax.ShapeDtypeStruct((PAIRS,ntp,256),F32),jax.ShapeDtypeStruct((R,D),F32)]
-            +[jax.ShapeDtypeStruct((D,FF),BF),jax.ShapeDtypeStruct((FF,D),BF),jax.ShapeDtypeStruct((2,9,piece,D),BF)],
+        in_specs=[ANYSPACE]*4+[once(a.shape) for a in (qkv,out,up,down,small,zeros,blank)],
+        out_specs=[rows,rows,rows,rows,pl.BlockSpec((1,ntp,256),lambda p:(p,0,0)),whole((R,D)),whole((half,1)),whole((half,1)),whole((1,640)),whole((4,D)),whole((1,FF))]+[ANYSPACE]*6,
+        out_shape=[sds((R,D),BF)]*4+[sds((PAIRS,ntp,256),F32),sds((R,D),F32),sds((half,1),jnp.int32),sds((half,1),F32),sds((1,640),F32),sds((4,D),F32),sds((1,FF),F32),
+            sds((D,3*D),BF),sds((D,D),BF),sds((D,FF),BF),sds((FF,D),BF),sds((9,piece,D),BF),sds((9,piece,D),BF)],
         scratch_shapes=[pltpu.VMEM((R,D),BF),pltpu.VMEM((2,half,half),F32),pltpu.VMEM((half,128),F32),pltpu.VMEM((PAIRS,R,PAIR),BF),
-            DMA((2,8)),DMA((2,9)),DMA((2,5)),DMA((2,5)),DMA((6,))],
+            pltpu.VMEM((9,piece,D),BF),pltpu.VMEM((9,8,128),jnp.int32),pltpu.VMEM((4,)+small.shape,BF),pltpu.VMEM((D,3*D),BF),pltpu.VMEM((D,D),BF),pltpu.VMEM((half,2*PAIR),F32),
+            DMA((8,)),DMA((9,)),DMA((8,)),DMA((9,)),DMA((8,)),DMA((9,)),DMA((4,13)),DMA((4,13)),DMA((3,)),DMA((3,)),DMA((14,))],
         compiler_params=pltpu.CompilerParams(vmem_limit_bytes=VMEM_LIMIT,dimension_semantics=("arbitrary",),collective_id=1,has_side_effects=True),
         cost_estimate=pl.CostEstimate(flops=2*R*D*(3*D+D)+24*R*half*D//2*2,bytes_accessed=16<<20,transcendentals=R*half*HEADS),
-        name="fwd_attn")(xc,noise,segc,segr,emb,gain,wqkv,wqkv,wqkv,wout,cos,sin,up,down,gout,zeros)
+        name="fwd_attn")(clean,meta,gout,trig,qkv,out,up,down,small,zeros,blank)
 
 GC=(2.0/3.141592653589793)**0.5
-def ffn_fwd_kernel(x1,gain,wup,bup,wdn,bdn,out_o,act_o,dg_o,h_s,acc):
-    j=pl.program_id(0)
-    @pl.when(j==0)
+def cols(refs): return jnp.concatenate([r[...] for r in refs],axis=1)
+def rowcat(refs): return jnp.concatenate([r[...] for r in refs],axis=0)
+STEPS=FF//512
+def up_specs(): return [pl.BlockSpec((D,128),(lambda s:(lambda j:(0,s*STEPS+j)))(s)) for s in range(4)]
+def down_specs(): return [pl.BlockSpec((128,D),(lambda s:(lambda j:(s*STEPS+j,0)))(s)) for s in range(4)]
+def bias_specs(): return [pl.BlockSpec((1,128),(lambda s:(lambda j:(0,s*STEPS+j)))(s)) for s in range(4)]
+
+FFN_TABLE={2: [(0, None, 0)], 3: [(0, 0, 1)], 4: [(1, None, 0)], 5: [(1, 0, 1)], 6: [(2, None, 0), (0, 1, None)], 7: [(2, 0, 1)], 8: [(3, None, 0), (1, 1, None)], 9: [(3, 0, 1)], 10: [(4, None, 0), (2, 1, None)], 11: [(4, 0, 1)], 12: [(5, None, 0)]}
+FFN_END=[(3, 1), (5, 0), (4, 1)]
+ATTN_TABLE={0: [(5, None, 1), (0, None, 2), (1, None, 2), (2, None, 2), (3, None, 2), (4, None, 2)], 1: [(6, None, 0)], 2: [(0, 2, 3), (6, 0, 1)], 3: [(0, 3, 4), (1, 2, 3), (5, 1, 2)], 4: [(7, None, 0), (2, 2, 3), (6, 1, 2)], 5: [(0, 4, 5), (1, 3, 4), (2, 3, 4), (3, 2, 3), (7, 0, 1)], 6: [(0, 5, 6), (4, 2, 3)], 7: [(1, 4, 5), (2, 4, 5), (3, 3, 4), (5, 2, 3), (7, 1, 2), (0, 6, 7)], 8: [(8, None, 0), (4, 3, 4), (6, 2, 3)], 9: [(1, 5, 6), (2, 5, 6), (5, 3, 4), (7, 2, 3), (8, 0, 1), (3, 4, 5)], 10: [(0, 7, None), (1, 6, 7), (4, 4, 5), (6, 3, 4)], 11: [(2, 6, 7), (5, 4, 5), (7, 3, 4), (8, 1, 2)], 12: [(9, None, 0)]}
+ATTN_END=[(1, 7), (3, 5), (4, 5), (6, 4), (2, 7), (9, 0), (5, 5), (8, 2), (7, 4)]
+TAIL_ORDER=[("sums", None, 0), (9, None, 1), (8, None, 3), (6, None, 5), (7, None, 5), (3, None, 6), (4, None, 6), (5, None, 6), ("rows", None, 1), ("rows", None, 2), ("sums", 0, 1), (8, 3, 4), (6, 5, 6), ("sums", 1, 2), (7, 5, 6), (3, 6, 7), (9, 1, 2), ("rows", None, 3), (4, 6, 7), ("sums", 2, 3), (5, 6, 7), (3, 7, None), ("sums", 3, 4), (9, 2, 3), ("rows", None, 4), (8, 4, 5), (6, 6, 7), ("sums", 4, None), (7, 6, 7), (4, 7, None), (9, 3, 4), ("rows", None, 5), (5, 7, None), (8, 5, 6), (9, 4, 5), ("rows", None, 6), (8, 6, 7), (6, 7, None), (9, 5, 6), ("rows", None, 7), (7, 7, None), (9, 6, 7), (8, 7, None), (9, 7, None)]
+
+def after(state,table,end):
+    state=dict(state)
+    for ops in table.values():
+        for chunk,take,start in ops:
+            if take is not None: state[chunk]=take
+    state.update(end)
+    return state
+FFN_STATE=after({},FFN_TABLE,FFN_END)
+ATTN_STATE=after(FFN_STATE,ATTN_TABLE,ATTN_END)
+def in_state(state,ids,low,high): return [i for i in ids if low<=state[i]<=high]
+def started(chunk,table):
+    return [start for ops in table.values() for i,take,start in ops if i==chunk and start is not None]
+
+def run_table(table,chunks,position,pid,steps,per_step):
+    for i in range(steps):
+        ops=table.get(per_step*i+position+1,[])
+        if ops:
+            @pl.when(pid==i)
+            def _(): do_ops(ops,chunks)
+
+def do_ops(ops,chunks):
+    for i,take,start in ops:
+        if take is not None: chunks[i].take(take)
+        if start is not None: chunks[i].start(start)
+
+def ffn_kernel(x1,vec,*refs):
+    wup,bup,wdn,rest=refs[:4],refs[4:8],refs[8:12],refs[12:]
+    gain,bdn=vec.at[0:1],vec.at[1:2]
+    gy0,gout,zeros,dbup_o,dbdn_o,dgain_o,gx1_o,block_o,pair_o,total_o,final_o=rest[:11]
+    h_s,hT_s,acc,gy_s,out_s,act_s,gu_s,grad_s,pair_s,far_s,total_s,send,recv,g_send,g_recv,b_send,b_recv,local=rest[11:]
+    g=pl.program_id(0)
+    R=h_s.shape[0]; ch=R//3; piece=R//18
+    chunks=[Reduce(TILE,send.at[i],recv.at[i],grad=grad_s.at[i%2],pair=pair_s.at[i],far=far_s.at[i],total=total_s.at[i]) for i in range(STEPS)]
+    arrive=ToUnit(lambda q,h:gout.at[q,1,h],lambda t:gy_s.at[9+t],g_send,g_recv,local.at[0])
+    leave=[FromUnit(lambda t,i=i:out_s.at[9*i+t],lambda q,h,i=i:block_o.at[q,i,h],b_send.at[i],b_recv.at[i],local.at[1+i]) for i in range(2)]
+    first=pltpu.make_async_copy(gy0,gy_s.at[pl.ds(0,9)],local.at[3])
+    rows=lambda ref,i: ref[6*i:6*i+6].reshape(ch,D)
+    wu=lambda: cols(wup)
+    wd=lambda: rowcat(wdn)
+    bias=cols(bup).astype(F32)
+    @pl.when(g==0)
     def _():
+        meet(True,(1,2))
+        arrive.begin()
+        first.start()
+        pad_unit(zeros,gy_s.at[pl.ds(9,9)],local.at[4])
         n,_=norm_rows(x1[...])
-        h_s[...]=(n*gain[...].astype(F32)).astype(BF)
+        h=(n*gain[...].astype(F32)).astype(BF)
+        h_s[...]=h
+        hT_s[...]=h.T
         acc[...]=x1[...]+bdn[...].astype(F32)
-    R=h_s.shape[0]; ch=R//3
-    for i in range(3):
-        r=slice(i*ch,(i+1)*ch)
-        u=dot_nn(h_s[r],wup[...])+bup[...].astype(F32)
-        u2=u*u
-        t=jnp.tanh(GC*(u+0.044715*u*u2))
-        a=0.5*(1.0+t)
-        act=(u*a).astype(BF)
-        act_o[r]=act
-        dg_o[r]=(a+0.5*u*(1.0-t*t)*(GC*(1.0+3*0.044715*u2))).astype(BF)
-        acc[r]+=dot_nn(act,wdn[...])
-    @pl.when(j==pl.num_programs(0)-1)
-    def _(): out_o[...]=acc[...].astype(BF)
-
-def ffn_fwd(x1,gain,wup,bup,wdn,bdn,tile=512):
-    R=x1.shape[0]
-    return pl.pallas_call(ffn_fwd_kernel,grid=(FF//tile,),
-        in_specs=[whole((R,D)),whole((1,D)),pl.BlockSpec((D,tile),lambda j:(0,j)),pl.BlockSpec((1,tile),lambda j:(0,j)),pl.BlockSpec((tile,D),lambda j:(j,0)),whole((1,D))],
-        out_specs=[whole((R,D)),pl.BlockSpec((R,tile),lambda j:(0,j)),pl.BlockSpec((R,tile),lambda j:(0,j))],
-        out_shape=[jax.ShapeDtypeStruct((R,D),BF),jax.ShapeDtypeStruct((R,FF),BF),jax.ShapeDtypeStruct((R,FF),BF)],
-        scratch_shapes=[pltpu.VMEM((R,D),BF),pltpu.VMEM((R,D),F32)],
-        compiler_params=pltpu.CompilerParams(vmem_limit_bytes=VMEM_LIMIT,dimension_semantics=("arbitrary",)),
-        cost_estimate=pl.CostEstimate(flops=4*R*D*FF,bytes_accessed=30<<20,transcendentals=R*FF),
-        name="ffn_fwd")(x1,gain,wup,bup,wdn,bdn)
-
-def ffn_bwd_kernel(x1,gain,gy,act,dg,wup,wdn,dwup_o,dwdn_o,dbup_o,dbdn_o,dgain_o,gx1_o,ga_o,hT_s,gh):
-    j=pl.program_id(0)
-    @pl.when(j==0)
+    @pl.when(g<STEPS)
     def _():
-        n,_=norm_rows(x1[...])
-        hT_s[...]=(n*gain[...].astype(F32)).astype(BF).T
-        gh[...]=jnp.zeros_like(gh)
-        dbdn_o[...]=jnp.sum(gy[...].astype(F32),axis=0,keepdims=True)
-    ga=dot_nt(gy[...],wdn[...])
-    gu=(dg[...].astype(F32)*ga).astype(BF)
-    dwdn_o[...]=dot_tn(act[...],gy[...]).astype(BF)
-    dwup_o[...]=dot_nn(hT_s[...],gu).astype(BF)
-    dbup_o[...]=jnp.sum(gu.astype(F32),axis=0,keepdims=True)
-    gh[...]+=dot_nt(gu,wup[...])
-    @pl.when(j==pl.num_programs(0)-1)
+        for i in range(3):
+            r=slice(i*ch,(i+1)*ch)
+            u=dot_nn(h_s[r],wu())+bias
+            act=(0.5*u*(1.0+jnp.tanh(GC*(u+0.044715*u*u*u)))).astype(BF)
+            acc[r]+=dot_nn(act,wd())
+    @pl.when(g==STEPS-1)
+    def _():
+        for i in range(3): out_s[6*i:6*i+6]=acc[i*ch:(i+1)*ch].astype(BF).reshape(6,piece,D)
+        for r in leave: r.begin()
+        arrive.finish()
+        first.wait()
+        acc[...]=jnp.zeros_like(acc)
+        dbdn_o[...]=jnp.sum(gy_s[...].astype(F32).reshape(R,D),axis=0,keepdims=True)
+    @pl.when(g>=STEPS)
+    def _():
+        j=g-STEPS
+        for i in range(2,STEPS):
+            @pl.when(j==i)
+            def _(): chunks[i-2].sent(0)
+        slot=lax.rem(j,2)
+        for i in range(3):
+            r=slice(i*ch,(i+1)*ch)
+            u=dot_nn(h_s[r],wu())+bias
+            ga=dot_nt(rows(gy_s,i),wd())
+            u2=u*u
+            t=jnp.tanh(GC*(u+0.044715*u*u2))
+            a=0.5*(1.0+t)
+            gu=((a+0.5*u*(1.0-t*t)*(GC*(1.0+3*0.044715*u2)))*ga).astype(BF)
+            act_s[r]=(u*a).astype(BF)
+            gu_s[r]=gu
+            acc[r]+=dot_nt(gu,wu())
+        run_table(FFN_TABLE,chunks,0,j,STEPS,2)
+        def put(s,row,value):
+            for k in range(0,value.shape[0],64):
+                grad_s[slot,s%2,s//2,(row+k)//TILE,(row+k)%TILE:(row+k)%TILE+64]=value[k:k+64]
+        r=dot_tn(act_s[...],gy_s[...].reshape(R,D)).astype(BF)
+        for s in range(4):
+            for t in range(6): put(s,768+t*128,r[s*128:(s+1)*128,t*128:(t+1)*128])
+        r=dot_nn(hT_s[...],gu_s[...]).astype(BF)
+        for s in range(4):
+            for t in range(4): put(s,t*192,r[s*192:(s+1)*192,t*128:(t+1)*128])
+        dbup_o[...]=jnp.sum(gu_s[...].astype(F32),axis=0,keepdims=True)
+        run_table(FFN_TABLE,chunks,1,j,STEPS,2)
+    @pl.when(g==pl.num_programs(0)-1)
     def _():
         n,scale=norm_rows(x1[...])
-        g2=gh[...]
+        g2=acc[...]
         dgain_o[...]=jnp.sum(g2*n,axis=0,keepdims=True)
         e=g2*gain[...].astype(F32)
-        gx=gy[...].astype(F32)+scale*(e-jnp.mean(e,axis=-1,keepdims=True)-n*jnp.mean(e*n,axis=-1,keepdims=True))
-        gx1_o[...]=gx
-        ga_o[...]=gx.astype(BF)
-
-def ffn_bwd_comm_kernel(*refs):
-    ins,(res,),outs,(out_o,),scratch,(send,recv,local)=refs[:7],refs[7:8],refs[8:15],refs[15:16],refs[16:18],refs[18:]
-    j=pl.program_id(0)
-    rows=[FromUnit(lambda t,i=i:res.at[i,t],lambda q,h,i=i:out_o.at[q,i,h],send.at[i],recv.at[i],local.at[i]) for i in range(2)]
-    @pl.when(j==0)
-    def _():
-        meet(True,())
-        for r in rows: r.begin()
-    ffn_bwd_kernel(*ins,*outs,*scratch)
-    @pl.when(j==pl.num_programs(0)-1)
-    def _():
-        for r in rows: r.finish()
-
-def ffn_bwd(x1,gain,gy,act,dg,wup,wdn,res,tile=512):
-    R=x1.shape[0]
-    piece=R//18
-    col=pl.BlockSpec((R,tile),lambda j:(0,j))
-    return pl.pallas_call(ffn_bwd_comm_kernel,grid=(FF//tile,),
-        in_specs=[whole((R,D)),whole((1,D)),whole((R,D)),col,col,pl.BlockSpec((D,tile),lambda j:(0,j)),pl.BlockSpec((tile,D),lambda j:(j,0)),ANYSPACE],
-        out_specs=[pl.BlockSpec((D,tile),lambda j:(0,j)),pl.BlockSpec((tile,D),lambda j:(j,0)),pl.BlockSpec((1,tile),lambda j:(0,j)),whole((1,D)),whole((1,D)),whole((R,D)),whole((R,D)),ANYSPACE],
-        out_shape=[jax.ShapeDtypeStruct((D,FF),BF),jax.ShapeDtypeStruct((FF,D),BF),jax.ShapeDtypeStruct((1,FF),F32),jax.ShapeDtypeStruct((1,D),F32),jax.ShapeDtypeStruct((1,D),F32),jax.ShapeDtypeStruct((R,D),F32),jax.ShapeDtypeStruct((R,D),BF),jax.ShapeDtypeStruct((4,2,2,piece,D),BF)],
-        scratch_shapes=[pltpu.VMEM((D,R),BF),pltpu.VMEM((R,D),F32),DMA((2,8)),DMA((2,8)),DMA((2,))],
+        acc[...]=gy_s[...].astype(F32).reshape(R,D)+scale*(e-jnp.mean(e,axis=-1,keepdims=True)-n*jnp.mean(e*n,axis=-1,keepdims=True))
+        outs=[pltpu.make_async_copy(acc,gx1_o,local.at[5])]
+        outs[0].start()
+        for i,stage in FFN_END: chunks[i].take(stage)
+        for low,high,source,target in ((0,0,pair_s,pair_o),(1,3,total_s,total_o)):
+            for place,i in enumerate(in_state(FFN_STATE,range(STEPS),low,high)):
+                outs.append(pltpu.make_async_copy(source.at[i],target.at[place],local.at[5+len(outs)]))
+                outs[-1].start()
+        for i in range(STEPS):
+            stages=started(i,FFN_TABLE)
+            chunks[i].sent(*[x for x in stages if x>0 or i>=STEPS-2])
+        for r in leave: r.finish()
+        for d in outs: d.wait()
+
+def ffn(x1,vec,wup,bup,wdn,gy0,gout):
+    R=x1.shape[0]; half=R//2; piece=half//9
+    zeros=jnp.zeros((2,piece,D),BF)
+    count=lambda low,high: max(1,len(in_state(FFN_STATE,range(STEPS),low,high)))
+    tile=lambda j: lax.rem(j,STEPS)
+    ups=[pl.BlockSpec((D,128),(lambda s:(lambda j:(0,s*STEPS+tile(j))))(s)) for s in range(4)]
+    downs=[pl.BlockSpec((128,D),(lambda s:(lambda j:(s*STEPS+tile(j),0)))(s)) for s in range(4)]
+    biases=[pl.BlockSpec((1,128),(lambda s:(lambda j:(0,s*STEPS+tile(j))))(s)) for s in range(4)]
+    return pl.pallas_call(ffn_kernel,grid=(2*STEPS,),
+        in_specs=[once((R,D)),once((4,D))]+ups+biases+downs+[ANYSPACE]*2+[once(zeros.shape)],
+        out_specs=[pl.BlockSpec((1,512),lambda j:(0,jnp.maximum(j-STEPS,0))),whole((1,D)),whole((1,D))]+[ANYSPACE]*5,
+        out_shape=[jax.ShapeDtypeStruct((1,FF),F32),jax.ShapeDtypeStruct((1,D),F32),jax.ShapeDtypeStruct((1,D),F32),jax.ShapeDtypeStruct((R,D),F32),jax.ShapeDtypeStruct((4,2,2,piece,D),BF),
+            jax.ShapeDtypeStruct((count(0,0),2,2,TILE,128),BF),jax.ShapeDtypeStruct((count(1,3),2,TILE,128),BF),jax.ShapeDtypeStruct((1,2,TILE,128),BF)],
+        scratch_shapes=[pltpu.VMEM((R,D),BF),pltpu.VMEM((D,R),BF),pltpu.VMEM((R,D),F32),pltpu.VMEM((18,piece,D),BF),pltpu.VMEM((18,piece,D),BF),pltpu.VMEM((R,512),BF),pltpu.VMEM((R,512),BF),
+            pltpu.VMEM((2,2,2,2,TILE,128),BF),pltpu.VMEM((STEPS,2,2,TILE,128),BF),pltpu.VMEM((STEPS,2,TILE,128),BF),pltpu.VMEM((STEPS,2,TILE,128),BF),
+            DMA((STEPS,8)),DMA((STEPS,8)),DMA((8,)),DMA((9,)),DMA((2,8)),DMA((2,8)),DMA((STEPS+7,))],
         compiler_params=pltpu.CompilerParams(vmem_limit_bytes=VMEM_LIMIT,dimension_semantics=("arbitrary",),collective_id=2,has_side_effects=True),
-        cost_estimate=pl.CostEstimate(flops=8*R*D*FF,bytes_accessed=40<<20,transcendentals=0),
-        name="ffn_bwd")(x1,gain,gy,act,dg,wup,wdn,res)
-
-def bwd_attn_kernel(half,xc,noise,segc,segr,emb,gain,gx1,ga,q,k,v,mix,lse,wq,wk,wv,wout,cos,sin,
-                    dw_o,dwout_o,gin_o,demb_o,dgain_o,hT_s,gh,biasT_s,selfT_s,dq_s,dk_s,dv_s):
+        cost_estimate=pl.CostEstimate(flops=14*R*D*FF,bytes_accessed=40<<20,transcendentals=2*R*FF),
+        name="ffn")(x1,vec,*[wup]*4,*[bup]*4,*[wdn]*4,gy0,gout,zeros)
+
+def bwd_attn_kernel(half,xc,noise,segc,segr,vec,gx1,q,k,v,mix,lse,wq,wk,wv,wout,trig,mixed,tile_pair,tile_total,tile_final,
+                    gin_o,demb_o,dgain_o,tiles_o,wpair_o,wtotal_o,wfinal_o,hT_s,gh,biasT_s,selfT_s,dq_s,dk_s,dv_s,ga,trig_s,
+                    t_pair,t_far,t_total,t_over,t_final,w_grad,w_pair,w_far,w_total,w_over,w_final,t_send,t_recv,w_send,w_recv,local):
     p=pl.program_id(0)
+    emb,gain=vec.at[2:3],vec.at[3:4]
+    rank,_=place_ids()
     R=2*half
     tiles=tiles_of(half)
+    pairs=in_state(FFN_STATE,range(STEPS),0,0)
+    fars=in_state(FFN_STATE,range(STEPS),0,0)
+    slot=lambda ids,i: ids.index(i) if i in ids else 0
+    chunks=[Reduce(TILE,t_send.at[i],t_recv.at[i],pair=t_pair.at[slot(pairs,i)],far=t_far.at[slot(fars,i)],total=t_total.at[i],over=t_over.at[i],final=t_final.at[i]) for i in range(STEPS)]
+    chunks+=[Reduce(WING,w_send.at[i],w_recv.at[i],grad=w_grad.at[i],pair=w_pair.at[i],far=w_far.at[i],total=w_total.at[i],over=w_over.at[i],final=w_final.at[i]) for i in range(4)]
+    def tick(position):
+        run_table(ATTN_TABLE,chunks,position,p,PAIRS,2)
     @pl.when(p==0)
     def _():
+        loads=[pltpu.make_async_copy(trig.at[rank%2],trig_s,local.at[2])]
+        loads[0].start()
+        for low,high,source,target in ((0,0,tile_pair,t_pair),(1,3,tile_total,t_total),(4,7,tile_final,t_final)):
+            for place,i in enumerate(in_state(FFN_STATE,range(STEPS),low,high)):
+                loads.append(pltpu.make_async_copy(source.at[place],target.at[place if low==0 else i],local.at[2+len(loads)]))
+                loads[-1].start()
+        ga[...]=gx1[...].astype(BF)
+        for d in loads: d.wait()
+        meet(True,(1,2))
+        do_ops(ATTN_TABLE.get(0,[]),chunks)
         g=gain[...].astype(F32)
         for c,rows in enumerate(layer_rows(xc,noise,emb)):
             n,_=norm_rows(rows)
@@ -593,7 +741,11 @@
             same=segc[s:n]==segr[:,s:n]
             selfT_s[s:n,:m]=jnp.where(same&(kb==qb),0.0,NEG)
     gm=dot_nt(ga[...],wout[...]).astype(BF)
-    dwout_o[...]=dot_tn(mix[...],ga[...]).astype(BF)
+    @pl.when(p==0)
+    def _():
+        r=dot_tn(mixed[...],ga[...]).astype(BF)
+        for a in range(4):
+            for t in range(6): w_grad[0,a%2,a//2,t//3,t%3*192:(t%3+1)*192]=r[a*192:(a+1)*192,t*128:(t+1)*128]
     gd=gm.astype(F32)*mix[...].astype(F32)
     dk_s[...]=jnp.zeros_like(dk_s); dv_s[...]=jnp.zeros_like(dv_s)
     idx=0
@@ -617,15 +769,17 @@
             if c==0: dq=dq+part(slice(s,n),selfT_s[s:n,:m])
             dq_s[rs]=head_merge(dq)*HEAD**-0.5
             idx+=1
-    cs=jnp.concatenate([cos[...],cos[...]],axis=0)
-    sn=jnp.concatenate([sin[...],sin[...]],axis=0)
-    total=None
-    for i,(g,w) in enumerate(((dq_s,wq),(dk_s,wk),(dv_s,wv))):
-        z=g[...]
-        if i<2: z=z*cs-swap_halves(z)*sn
-        z=z.astype(BF)
-        dw_o[i]=dot_nn(hT_s[...],z).astype(BF)
-        gh[...]+=dot_nt(z,w[...])
+        if s==256: tick(0)
+    cs=jnp.concatenate([trig_s[:,:PAIR]]*2,axis=0)
+    sn=jnp.concatenate([trig_s[:,PAIR:]]*2,axis=0)
+    z=jnp.concatenate([(g[...]*cs-swap_halves(g[...])*sn).astype(BF) for g in (dq_s,dk_s)]+[dv_s[...].astype(BF)],axis=1)
+    r=dot_nn(hT_s[...],z).astype(BF)
+    group=1+p//2
+    for a in range(4):
+        for t in range(3):
+            w_grad[group,a%2,a//2,lax.rem(p,2),t*192:(t+1)*192]=r[a*192:(a+1)*192,t*128:(t+1)*128]
+    gh[...]+=dot_nt(z,cols((wq,wk,wv)))
+    tick(1)
     @pl.when(p==pl.num_programs(0)-1)
     def _():
         g=gain[...].astype(F32)
@@ -640,23 +794,51 @@
         gin_o[...]=(outs[1]+jnp.where(masked,0.0,outs[0])).astype(gin_o.dtype)
         demb_o[...]=jnp.sum(jnp.where(masked,outs[0],0.0),axis=0,keepdims=True)
         dgain_o[...]=dg
-
-def bwd_attn(xc,noise,segc,segr,emb,gain,gx1,ga,q,k,v,mix,lse,wqkv,wout,cos,sin):
-    half=xc.shape[0]; R=2*half
+        for i,stage in ATTN_END: chunks[i].take(stage)
+        stores=[]
+        for i in in_state(ATTN_STATE,range(STEPS),4,7): stores.append((t_final.at[i],tiles_o.at[i]))
+        for low,high,source,target in ((0,0,w_pair,wpair_o),(1,3,w_total,wtotal_o),(4,7,w_final,wfinal_o)):
+            for place,i in enumerate(in_state(ATTN_STATE,range(STEPS,STEPS+4),low,high)): stores.append((source.at[i-STEPS],target.at[place]))
+        stores=[pltpu.make_async_copy(a,b,local.at[2+n]) for n,(a,b) in enumerate(stores)]
+        for d in stores: d.start()
+        for i,chunk in enumerate(chunks): chunk.sent(*started(i,ATTN_TABLE))
+        for d in stores: d.wait()
+
+def bwd_attn(xc,noise,segc,segr,vec,gx1,q,k,v,mix,lse,wqkv,wout,trig,tile_pair,tile_total,tile_final):
+    half=xc.shape[0]; R=2*half; piece=half//9
     ntp=lse.shape[1]
     ws=[pl.BlockSpec((D,PAIR),(lambda off:(lambda p:(0,off+p)))(o*PAIRS)) for o in range(3)]
     rows=pl.BlockSpec((R,PAIR),lambda p:(0,p))
+    pairs=max(1,len(in_state(FFN_STATE,range(STEPS),0,0)))
+    count=lambda low,high: max(1,len(in_state(ATTN_STATE,range(STEPS,STEPS+4),low,high)))
     return pl.pallas_call(partial(bwd_attn_kernel,half),grid=(PAIRS,),
-        in_specs=[whole((half,D)),whole((half,1)),whole((half,1)),whole((1,half)),whole((1,D)),whole((1,D)),whole((R,D)),whole((R,D)),rows,rows,rows,rows,
-                  pl.BlockSpec((1,ntp,256),lambda p:(p,0,0)),*ws,pl.BlockSpec((PAIR,D),lambda p:(p,0)),whole((half,PAIR)),whole((half,PAIR))],
-        out_specs=[pl.BlockSpec((3,D,PAIR),lambda p:(0,0,p)),pl.BlockSpec((PAIR,D),lambda p:(p,0)),whole((half,D)),whole((1,D)),whole((1,D))],
-        out_shape=[jax.ShapeDtypeStruct((3,D,D),BF),jax.ShapeDtypeStruct((D,D),BF),jax.ShapeDtypeStruct((half,D),BF),jax.ShapeDtypeStruct((1,D),F32),jax.ShapeDtypeStruct((1,D),F32)],
-        scratch_shapes=[pltpu.VMEM((D,R),BF),pltpu.VMEM((R,D),F32),pltpu.VMEM((2,half,-(-half//128)*128),F32),pltpu.VMEM((half,128),F32)]+[pltpu.VMEM((R,PAIR),F32)]*3,
+        in_specs=[once((half,D)),once((half,1)),once((half,1)),once((1,640)),once((4,D)),once((R,D)),rows,rows,rows,rows,
+                  pl.BlockSpec((1,ntp,256),lambda p:(p,0,0)),*ws,pl.BlockSpec((PAIR,D),lambda p:(p,0)),ANYSPACE,once((R,D))]+[ANYSPACE]*3,
+        out_specs=[whole((half,D)),whole((1,D)),whole((1,D))]+[ANYSPACE]*4,
+        out_shape=[jax.ShapeDtypeStruct((half,D),BF),jax.ShapeDtypeStruct((1,D),F32),jax.ShapeDtypeStruct((1,D),F32),jax.ShapeDtypeStruct((STEPS,2,TILE,128),BF),jax.ShapeDtypeStruct((count(0,0),2,2,WING,128),BF),jax.ShapeDtypeStruct((count(1,3),2,WING,128),BF),jax.ShapeDtypeStruct((count(4,7),2,WING,128),BF)],
+        scratch_shapes=[pltpu.VMEM((D,R),BF),pltpu.VMEM((R,D),F32),pltpu.VMEM((2,half,-(-half//128)*128),F32),pltpu.VMEM((half,128),F32)]+[pltpu.VMEM((R,PAIR),F32)]*3+[pltpu.VMEM((R,D),BF),pltpu.VMEM((half,2*PAIR),F32)]
+            +[pltpu.VMEM((pairs,2,2,TILE,128),BF),pltpu.VMEM((pairs,2,TILE,128),BF),pltpu.VMEM((STEPS,2,TILE,128),BF),pltpu.VMEM((STEPS,2*TILE,128),BF),pltpu.VMEM((STEPS,2,TILE,128),BF),
+              pltpu.VMEM((4,2,2,2,WING,128),BF),pltpu.VMEM((4,2,2,WING,128),BF),pltpu.VMEM((4,2,WING,128),BF),pltpu.VMEM((4,2,WING,128),BF),pltpu.VMEM((4,2*WING,128),BF),pltpu.VMEM((4,2,WING,128),BF),
+              DMA((STEPS,8)),DMA((STEPS,8)),DMA((4,8)),DMA((4,8)),DMA((16,))],
+        compiler_params=pltpu.CompilerParams(vmem_limit_bytes=VMEM_LIMIT,dimension_semantics=("arbitrary",),collective_id=3,has_side_effects=True),
+        cost_estimate=pl.CostEstimate(flops=4*R*D*(3*D+D)+60*R*half*D//2*2,bytes_accessed=30<<20,transcendentals=R*half*HEADS),
+        name="bwd_attn")(xc,noise,segc,segr,vec,gx1,q,k,v,mix,lse,wqkv,wqkv,wqkv,wout,trig,mix,tile_pair,tile_total,tile_final)
+
+def assemble(ffn,wings,gin,block):
+    piece=gin.shape[2]
+    up,down,out,qkv,grad,rows=pl.pallas_call(assemble_kernel,grid=(STEPS,),
+        in_specs=[pl.BlockSpec((1,2,TILE,128),lambda i:(i,0,0,0)),whole(wings.shape),
+            pl.BlockSpec((2,piece,D),lambda i:(jnp.minimum(i,3),0,0)),pl.BlockSpec((4,piece,D),lambda i:(jnp.minimum(i,3),0,0))],
+        out_specs=[whole((192,FF)),pl.BlockSpec((128,D),lambda i:(i,0)),whole((192,D)),whole((192,3*D)),
+            pl.BlockSpec((2,piece,D),lambda i:(jnp.minimum(i,3),0,0)),pl.BlockSpec((4,piece,D),lambda i:(jnp.minimum(i,3),0,0))],
+        out_shape=[jax.ShapeDtypeStruct((192,FF),F32),jax.ShapeDtypeStruct((768,D),F32),jax.ShapeDtypeStruct((192,D),F32),jax.ShapeDtypeStruct((192,3*D),F32),
+            jax.ShapeDtypeStruct((8,piece,D),F32),jax.ShapeDtypeStruct((16,piece,D),BF)],
         compiler_params=pltpu.CompilerParams(vmem_limit_bytes=VMEM_LIMIT,dimension_semantics=("arbitrary",)),
-        cost_estimate=pl.CostEstimate(flops=4*R*D*(3*D+D)+60*R*half*D//2*2,bytes_accessed=30<<20,transcendentals=R*half*HEADS),
-        name="bwd_attn")(xc,noise,segc,segr,emb,gain,gx1,ga,q,k,v,mix,lse,wqkv,wqkv,wqkv,wout,cos,sin)
-
-
+        name="assemble")(ffn,wings,gin.reshape(8,piece,D),block.reshape(16,piece,D))
+    return up,down,out,qkv,grad,rows
+
+
+DMA = pltpu.SemaphoreType.DMA
 MESH = pl.DeviceIdType.MESH
 INVMEM = pl.BlockSpec(memory_space=pltpu.VMEM)
 ANYSPACE = pl.BlockSpec(memory_space=pl.ANY)
@@ -742,6 +924,16 @@
                 remote(self.target(slot), self.target(slot), self.send.at[0], self.recv.at[slot], {"ctx": c}).wait_recv()
 
 
+def pad_unit(zeros, target, sem):
+    c, _ = place_ids()
+    copy = pltpu.make_async_copy(zeros, target.at[pl.ds(7, 2)], sem)
+
+    @pl.when(c % 2 == 1)
+    def _():
+        copy.start()
+        copy.wait()
+
+
 class FromUnit:
     def __init__(self, source, target, send, recv, local):
         self.source, self.target, self.send, self.recv, self.local = source, target, send, recv, local
@@ -782,6 +974,24 @@
         @pl.when(c != 7)
         def _():
             own_op(self.own())
+
+    def begin_one(self, s):
+        c = self.c
+
+        @pl.when((c % 2 == 0) | ((c + s) % 8 != 7))
+        def _():
+            self.message(s).start()
+
+    def begin_rest(self):
+        c = self.c
+
+        @pl.when(c % 2 == 0)
+        def _():
+            self.extra().start()
+
+        @pl.when(c != 7)
+        def _():
+            self.own().start()
 
     def begin(self):
         self.each(lambda m: m.start(), lambda m: m.start())
@@ -850,174 +1060,228 @@
             copy.wait_recv()
 
 
-def prologue_kernel(clean, meta, qkv, out, small, zeros, blank, clean_o, meta_o, qkv_o, out_o, small_o,
-                    a_send, a_recv, m_send, m_recv, w_send, w_recv, s_send, s_recv, local):
-    c, f = place_ids()
-    meet(True, (1, 2, 3))
-    rows = ToUnit(lambda q, h: clean.at[q, h], lambda i: clean_o.at[i], a_send, a_recv, local.at[0])
-    notes = ToUnit(lambda q, h: meta.at[2 * q + h], lambda i: meta_o.at[i], m_send, m_recv, local.at[1])
-    weights = [GatherRows(qkv, qkv_o, w_send.at[0], w_recv.at[0], local.at[2], 3),
-               GatherRows(out, out_o, w_send.at[1], w_recv.at[1], local.at[3], 3)]
-    weights[0].begin()
-    notes.begin()
-    rows.begin()
-    weights[1].begin()
-    others = [f + 1 - 2 * (f % 2), (f + 2) % 4, 3 - f]
-    sends = [remote(small, small_o.at[f], s_send.at[i], s_recv.at[i], {"fsdp": other}) for i, other in enumerate(others)]
-    for copy in sends:
+class Reduce:
+    def __init__(self, rows, send, recv, across=False, grad=None, pair=None, far=None, total=None, over=None, final=None):
+        c, f = place_ids()
+        self.send, self.recv, self.across = send, recv, across
+        self.grad, self.pair, self.far, self.total, self.over, self.final = grad, pair, far, total, over, final
+        self.core, self.y, self.x = f % 2, f // 2, c % 2
+        z1, z2 = (c // 2) % 2, c // 4
+        self.sib, self.far_id = {"fsdp": f + 1 - 2 * self.core}, {"fsdp": (f + 2) % 4}
+        self.xn, self.z1n, self.z2n = {"ctx": c + 1 - 2 * self.x}, {"ctx": c + 2 - 4 * z1}, {"ctx": c + 4 - 8 * z2}
+        half, quarter = rows // 2, rows // 4
+        self.rows = rows
+        self.levels = [(z1 * half, (1 - z1) * half, half, rows, self.z1n)]
+        base = z1 * half
+        self.levels.append((base + z2 * quarter, base + (1 - z2) * quarter, quarter, rows + half, self.z2n))
+
+    def at(self, ref, start, size):
+        return ref.at[self.x, pl.ds(pl.multiple_of(start, 16), size)]
+
+    def copy(self, stage):
+        x, y = self.x, self.y
+        if stage == 0:
+            source, target, where = self.grad.at[1 - self.core], self.pair, self.sib
+        elif stage == 1 and self.across:
+            source, target, where = self.pair.at[:, 1 - x], self.far, self.xn
+        elif stage == 1:
+            source, target, where = self.pair.at[1 - y], self.far, self.far_id
+        elif stage == 2 and self.across:
+            source, target, where = self.pair.at[1 - y, x], self.over.at[pl.ds(0, self.rows)], self.far_id
+        elif stage == 2:
+            source, target, where = self.total.at[1 - x], self.over.at[pl.ds(0, self.rows)], self.xn
+        elif stage < 5:
+            keep, give, size, offset, where = self.levels[stage - 3]
+            source, target = self.at(self.total, give, size), self.over.at[pl.ds(offset, size)]
+        elif stage < 7:
+            keep, give, size, offset, where = self.levels[6 - stage]
+            source = target = self.at(self.final, keep, size)
+        else:
+            source, target, where = self.final.at[x], self.final.at[x], self.xn
+        return remote(source, target, self.send.at[stage], self.recv.at[stage], where)
+
+    def start(self, stage):
+        self.copy(stage).start()
+
+    def take(self, stage):
+        x, y = self.x, self.y
+        if stage < 5:
+            self.copy(stage).wait_recv()
+        if stage == 0:
+            self.pair[...] = self.pair[...] + self.grad[self.core]
+        elif stage == 1 and self.across:
+            for i in range(2):
+                self.pair[i, x] = self.pair[i, x] + self.far[i]
+        elif stage == 1:
+            self.total[...] = self.far[...] + self.pair[y]
+        elif stage == 2 and self.across:
+            self.total[x] = self.pair[y, x] + self.over[pl.ds(0, self.rows)]
+        elif stage == 2:
+            self.total[x] = self.total[x] + self.over[pl.ds(0, self.rows)]
+        elif stage < 5:
+            keep, give, size, offset, where = self.levels[stage - 3]
+            into = self.at(self.final if stage == 4 else self.total, keep, size)
+            into[...] = self.at(self.total, keep, size)[...] + self.over[pl.ds(offset, size)]
+        elif stage < 7:
+            keep, give, size, offset, where = self.levels[6 - stage]
+            ref = self.at(self.final, give, size)
+            remote(ref, ref, self.send.at[stage], self.recv.at[stage], where).wait_recv()
+        else:
+            ref = self.final.at[1 - x]
+            remote(ref, ref, self.send.at[7], self.recv.at[7], self.xn).wait_recv()
+
+    def sent(self, *stages):
+        for stage in stages:
+            self.copy(stage).wait_send()
+
+
+TILE = 768
+WING = 576
+
+
+def tail_kernel(tiles, wpair, wtotal, wfinal, gin, embed, gain_one, gain_two, down_shift, up_shift, tiles_o, wings_o, gin_o, sums_o,
+                t_over, t_total, t_final, w_pair, w_far, w_over, w_total, w_final, sum_s, in_s,
+                t_send, t_recv, r_send, r_recv, v_send, v_recv, a_send, a_recv, local):
+    rows = FromUnit(lambda i: gin.at[i], lambda q, h: gin_o.at[q, h], a_send, a_recv, local.at[0])
+    open_tiles = in_state(ATTN_STATE, range(STEPS), 4, 6)
+    chunks = {i: Reduce(TILE, t_send.at[k], t_recv.at[k], total=t_total, over=t_over, final=t_final.at[k])
+              for k, i in enumerate(open_tiles)}
+    loads = [(tiles.at[i], t_final.at[k]) for k, i in enumerate(open_tiles)]
+    wings = range(STEPS, STEPS + 4)
+    for w in wings:
+        k = w - STEPS
+        chunks[w] = Reduce(WING, r_send.at[k], r_recv.at[k], pair=w_pair, far=w_far, total=w_total.at[k], over=w_over.at[k],
+                           final=w_final.at[k])
+    for low, high, source, target in ((0, 0, wpair, None), (1, 3, wtotal, w_total), (4, 7, wfinal, w_final)):
+        for place, w in enumerate(in_state(ATTN_STATE, wings, low, high)):
+            loads.append((source.at[place], w_pair if target is None else target.at[w - STEPS]))
+    loads = [pltpu.make_async_copy(a, b, local.at[1 + n]) for n, (a, b) in enumerate(loads)]
+    for copy in loads:
         copy.start()
-    own = pltpu.make_async_copy(small, small_o.at[f], local.at[4])
-    own.start()
-    pads = [pltpu.make_async_copy(zeros, clean_o.at[pl.ds(7, 2)], local.at[5]),
-            pltpu.make_async_copy(blank, meta_o.at[pl.ds(7, 2)], local.at[6])]
-
-    @pl.when(c % 2 == 1)
+    row = 0
+    for part in (embed, gain_one, gain_two, down_shift):
+        for i in range(D // 128):
+            sum_s[0, row:row + 1] = part[:, i * 128:(i + 1) * 128]
+            row += 1
+    for s in range(4):
+        for j in range(STEPS):
+            sum_s[0, row:row + 1] = up_shift[:, j * 512 + s * 128:j * 512 + (s + 1) * 128]
+            row += 1
+    some = chunks[STEPS]
+    vectors = [remote(sum_s.at[i], in_s.at[i], v_send.at[i], v_recv.at[i], where)
+               for i, where in enumerate((some.sib, some.far_id, some.xn, some.z1n, some.z2n))]
+    for copy in loads:
+        copy.wait()
+    meet(True, (1, 2))
+    for chunk, take, start in TAIL_ORDER:
+        if chunk == "rows":
+            if start == 1:
+                rows.begin_rest()
+            rows.begin_one(start)
+        elif chunk == "sums":
+            if take is not None:
+                vectors[take].wait_recv()
+                sum_s[take + 1] = sum_s[take] + in_s[take]
+            if start is not None:
+                vectors[start].start()
+        else:
+            if take is not None:
+                chunks[chunk].take(take)
+            if start is not None:
+                chunks[chunk].start(start)
+    stores = [(t_final.at[k], tiles_o.at[i]) for k, i in enumerate(open_tiles)] + [(w_final, wings_o)]
+    stores = [pltpu.make_async_copy(a, b, local.at[1 + n]) for n, (a, b) in enumerate(stores)]
+    for copy in stores:
+        copy.start()
+    sums_o[...] = sum_s[5]
+    for i in range(5):
+        vectors[i].wait_send()
+    for i, chunk in chunks.items():
+        chunk.sent(*range(ATTN_STATE[i] + 1, 8))
+    rows.finish()
+    for copy in stores:
+        copy.wait()
+
+
+def tail(tiles, wpair, wtotal, wfinal, gin, vectors):
+    piece = gin.shape[1]
+    n = max(1, len(in_state(ATTN_STATE, range(STEPS), 4, 6)))
+    return pl.pallas_call(
+        tail_kernel,
+        in_specs=[ANYSPACE] * 5 + [INVMEM] * 5,
+        out_specs=[ANYSPACE] * 3 + [INVMEM],
+        out_shape=[jax.ShapeDtypeStruct(tiles.shape, BF), jax.ShapeDtypeStruct((4, 2, WING, 128), BF),
+                   jax.ShapeDtypeStruct((4, 2, piece, D), BF), jax.ShapeDtypeStruct((48, 128), F32)],
+        scratch_shapes=[pltpu.VMEM((16, 128), BF), pltpu.VMEM((2, 16, 128), BF), pltpu.VMEM((n, 2, TILE, 128), BF),
+                        pltpu.VMEM((2, 2, WING, 128), BF), pltpu.VMEM((2, WING, 128), BF), pltpu.VMEM((4, 2 * WING, 128), BF),
+                        pltpu.VMEM((4, 2, WING, 128), BF), pltpu.VMEM((4, 2, WING, 128), BF), pltpu.VMEM((6, 48, 128), F32),
+                        pltpu.VMEM((5, 48, 128), F32),
+                        DMA((n, 8)), DMA((n, 8)), DMA((4, 8)), DMA((4, 8)), DMA((5,)), DMA((5,)), DMA((8,)), DMA((8,)), DMA((n + 6,))],
+        input_output_aliases={0: 0},
+        compiler_params=pltpu.CompilerParams(collective_id=4, has_side_effects=True, vmem_limit_bytes=VMEM_LIMIT),
+        name="tail")(tiles, wpair, wtotal, wfinal, gin, *vectors)
+
+
+def assemble_kernel(ffn, wings, gin, block, up_o, down_o, out_o, qkv_o, gin_o, block_o):
+    i = pl.program_id(0)
+    tile = lambda r: ffn[0, r // TILE, r % TILE:r % TILE + 64].astype(F32)
+    for s in range(4):
+        for r in range(0, 192, 64):
+            up_o[r:r + 64, pl.ds(pl.multiple_of((s * STEPS + i) * 128, 128), 128)] = tile(s * 192 + r)
+    for t in range(6):
+        for r in range(0, 128, 64):
+            down_o[r:r + 64, t * 128:(t + 1) * 128] = tile(768 + t * 128 + r)
+    gin_o[...] = gin[...].astype(F32)
+    block_o[...] = block[...]
+
+    @pl.when(i == 0)
     def _():
-        for copy in pads:
-            copy.start()
-        for copy in pads:
-            copy.wait()
-
-    for i in range(3):
-        weights[0].relay_far(i)
-    for i in range(3):
-        weights[0].relay_x(i)
-        weights[1].relay_far(i)
-    for i in range(3):
-        weights[1].relay_x(i)
-    own.wait()
-    for i, other in enumerate(others):
-        sends[i].wait_send()
-        remote(small_o.at[other], small_o.at[other], s_send.at[i], s_recv.at[i], {"fsdp": other}).wait_recv()
-    notes.finish()
-    rows.finish()
-    for weight in weights:
-        weight.finish()
-
-
-DMA = pltpu.SemaphoreType.DMA
-
-
-def prologue(clean, meta, qkv, out, small):
-    piece = clean.shape[2]
-    zeros = jnp.zeros((2, piece, D), BF)
-    blank = jnp.concatenate([jnp.full((2, 8, piece), -1, jnp.int32), jnp.zeros((2, 8, 128 - piece), jnp.int32)], axis=2)
-    return pl.pallas_call(
-        prologue_kernel,
-        in_specs=[ANYSPACE] * 2 + [INVMEM] * 5,
-        out_specs=[ANYSPACE] * 5,
-        out_shape=[jax.ShapeDtypeStruct((9, piece, D), BF), jax.ShapeDtypeStruct((9, 8, 128), jnp.int32),
-                   jax.ShapeDtypeStruct((D, 3 * D), BF), jax.ShapeDtypeStruct((D, D), BF),
-                   jax.ShapeDtypeStruct((4,) + small.shape, BF)],
-        scratch_shapes=[DMA((8,)), DMA((9,)), DMA((8,)), DMA((9,)), DMA((2, 13)), DMA((2, 13)), DMA((3,)), DMA((3,)), DMA((7,))],
-        compiler_params=pltpu.CompilerParams(collective_id=0, has_side_effects=True),
-        name="prologue")(clean, meta, qkv, out, small, zeros, blank)
-
-
-def flip(values, axis, count, bit):
-    return lax.ppermute(values, axis, [(i, i ^ bit) for i in range(count)])
-
-
-def pick(values, index, axis):
-    return lax.dynamic_index_in_dim(values, index, axis, keepdims=False)
-
-
-def order_two(mine, other, index, axis):
-    return jnp.where(index == 0, jnp.stack([mine, other], axis), jnp.stack([other, mine], axis))
-
-
-def gather_rows(shard, core, chip):
-    near = order_two(shard, flip(shard, "fsdp", 4, 2), chip, 0)
-    full = order_two(near, flip(near, "fsdp", 4, 1), core, 1)
-    return full.reshape((4 * shard.shape[0],) + shard.shape[1:])
-
-
-def halve(values, index, axis, mesh_axis, count, bit):
-    received = flip(pick(values, 1 - index, axis), mesh_axis, count, bit)
-    kept = pick(values, index, axis)
-    return (kept.astype(F32) + received.astype(F32)).astype(BF)
-
-
-def reduce_shard(grad, lead, core, chip, ranks):
-    rows, cols = grad.shape[-2] // 4, grad.shape[-1]
-    axis = len(lead)
-    part = grad.reshape(lead + (2, 2, rows, cols))
-    part = halve(part, core, axis + 1, "fsdp", 4, 1)
-    part = halve(part, chip, axis, "fsdp", 4, 2)
-    shape = part.shape
-    for level in range(3):
-        size = part.shape[-2] // 2
-        part = halve(part.reshape(lead + (2, size, cols)), ranks[level], axis, "ctx", 8, 1 << level)
-    for level in (2, 1, 0):
-        size = part.shape[-2]
-        other = flip(part, "ctx", 8, 1 << level)
-        part = order_two(part, other, ranks[level], axis).reshape(lead + (2 * size, cols))
-    return part.reshape(shape).astype(F32)
-
-
-def to_unit(blocks, part, fill):
-    extra = flip(blocks[7], "ctx", 8, 1)[None]
-    pads = jnp.full((2,) + blocks.shape[1:], fill, blocks.dtype)
-    first = jnp.concatenate([blocks, extra], axis=0)
-    second = jnp.concatenate([blocks[6::-1], pads], axis=0)
-    return jnp.where(part == 0, first, second)
-
-
-def from_unit(pieces, part):
-    extra = flip(pieces[8], "ctx", 8, 1)[None]
-    second = jnp.concatenate([pieces[6::-1], extra], axis=0)
-    return jnp.where(part == 0, pieces[:8], second)
-
-
-def exchange(blocks):
-    return lax.all_to_all(blocks, "ctx", 0, 0)
+        def strip(ref, k, r):
+            row = k * 192 + r
+            return ref[row // WING, row % WING:row % WING + 64].astype(F32)
+
+        for r in range(0, 192, 64):
+            for t in range(6):
+                out_o[r:r + 64, t * 128:(t + 1) * 128] = strip(wings.at[0], t, r)
+                source = wings.at[1 + t // 2]
+                for w in range(3):
+                    qkv_o[r:r + 64, w * D + t * 128:w * D + (t + 1) * 128] = strip(source, t % 2 * 3 + w, r)
+
+
+def rope_constant(half):
+    position = np.arange(2 * half, dtype=np.float32)
+    frequency = np.float32(10000.0) ** (-(np.arange(HEAD // 2, dtype=np.float32) * np.float32(2.0)) / np.float32(HEAD))
+    angles = (position[:, None] * frequency[None, :]).astype(np.float64)
+    cosine, sine = np.cos(angles), np.sin(angles)
+    table = np.concatenate([np.tile(cosine, (1, 4)), np.tile(np.concatenate([-sine, sine], axis=1), (1, 2))], axis=1)
+    return jnp.asarray(table.reshape(2, half, 4 * HEAD).astype(np.float32))
 
 
 def even_body(clean_in, segments, noise, mask_embed, norm1_gain, qkv_weight, out_weight, norm2_gain, up_weight, up_bias,
               down_weight, down_bias, out_grad):
-    rank = lax.axis_index("ctx")
     place = lax.axis_index("fsdp")
-    core, chip = place & 1, place >> 1
-    part = rank & 1
-    ranks = (rank & 1, (rank >> 1) & 1, rank >> 2)
     piece = clean_in.shape[2]
     half = 9 * piece
+    width = mask_embed.shape[0]
     meta = jnp.concatenate([segments.reshape(8, 1, piece), noise.reshape(8, 1, piece)], axis=2)
     meta = jnp.broadcast_to(meta, (8, 8, 2 * piece))
-    small = jnp.concatenate([mask_embed, norm1_gain, norm2_gain, down_bias, up_bias]).reshape(-1, 128)
+    small = jnp.stack([mask_embed, norm1_gain, norm2_gain, down_bias])
+    small = jnp.concatenate([jnp.pad(small, ((0, 0), (0, 256 - width))), up_bias.reshape(-1, 256)])
     small = jnp.pad(small, ((0, 16 - small.shape[0]), (0, 0)))
-    clean, meta, qkv_full, out_full, small = prologue(clean_in, meta, qkv_weight, out_weight, small)
+    q, k, v, mixed, lse, resid, mask, seg_col, seg_row, vectors, up_shift, qkv_full, out_full, up_full, down_full, cotangent, clean = fwd_attn(
+        clean_in, meta, out_grad, rope_constant(half), qkv_weight, out_weight, up_weight, down_weight, small)
     clean = clean.reshape(half, D)
-    seg = meta[:, 0, :piece].reshape(half)
-    mask = meta[:, 0, piece:].reshape(half, 1)
-    small = small.reshape(4, -1)
-    width = mask_embed.shape[0]
-    embed, gain_one, gain_two, down_shift = (small[:, i * width:(i + 1) * width].reshape(1, D) for i in range(4))
-    up_shift = small[:, 4 * width:4 * width + up_bias.shape[0]].reshape(1, FF)
-
-    cos_part, sin_part = rope_tables(part * half + jnp.arange(half, dtype=jnp.int32))
-    cosine = jnp.tile(cos_part, (1, 4))
-    sine = jnp.tile(jnp.concatenate([-sin_part, sin_part], axis=1), (1, 2))
-    seg_col, seg_row = seg[:, None], seg[None, :]
-
-    q, k, v, mixed, lse, resid, up_full, down_full, cotangent = fwd_attn(
-        clean, mask, seg_col, seg_row, embed, gain_one, qkv_full, out_full, cosine, sine, up_weight, down_weight, out_grad)
-    cotangent = cotangent.reshape(2 * half, D)
-    result, active, slope = ffn_fwd(resid, gain_two, up_full, up_shift, down_full, down_shift)
-    up_grad, down_grad, up_shift_grad, down_shift_grad, gain_two_grad, grad_resid, grad_attn, block_out = ffn_bwd(
-        resid, gain_two, cotangent, active, slope, up_full, down_full, result.reshape(2, 9, piece, D))
-    qkv_grad, out_weight_grad, grad_in, embed_grad, gain_one_grad = bwd_attn(
-        clean, mask, seg_col, seg_row, embed, gain_one, grad_resid, grad_attn, q, k, v, mixed, lse, qkv_full, out_full,
-        cosine, sine)
-    input_grad = exchange(from_unit(grad_in.reshape(9, piece, D), part)).reshape(4, 2, piece, D).astype(F32)
-
-    down_sum = reduce_shard(down_grad, (), core, chip, ranks)
-    up_sum = reduce_shard(up_grad, (), core, chip, ranks)
-    out_sum = reduce_shard(out_weight_grad, (), core, chip, ranks)
-    qkv_sum = reduce_shard(qkv_grad, (3,), core, chip, ranks)
-    qkv_sum = jnp.concatenate([qkv_sum[0], qkv_sum[1], qkv_sum[2]], axis=1)
-    sums = jnp.concatenate([x.reshape(-1) for x in (embed_grad, gain_one_grad, gain_two_grad, down_shift_grad, up_shift_grad)])
-    sums = lax.psum(sums, ("ctx", "fsdp"))
+    up_shift_grad, down_shift_grad, gain_two_grad, grad_resid, block_out, tile_pair, tile_total, tile_final = ffn(
+        resid, vectors, up_full, up_shift, down_full, cotangent, out_grad)
+    grad_in, embed_grad, gain_one_grad, tiles, wpair, wtotal, wfinal = bwd_attn(
+        clean, mask, seg_col, seg_row, vectors, grad_resid, q, k, v, mixed, lse, qkv_full, out_full, rope_constant(half),
+        tile_pair, tile_total, tile_final)
+    tiles, wings, input_grad, sums = tail(tiles, wpair, wtotal, wfinal, grad_in.reshape(9, piece, D),
+                                          (embed_grad, gain_one_grad, gain_two_grad, down_shift_grad, up_shift_grad))
+    up_sum, down_sum, out_sum, qkv_sum, input_grad, block_out = assemble(tiles, wings, input_grad, block_out)
+    input_grad = input_grad.reshape(clean_in.shape)
+    block_out = block_out.reshape(out_grad.shape)
+    sums = sums.reshape(-1)
     own = [lax.dynamic_slice_in_dim(sums, i * D + place * width, width) for i in range(4)]
     own_up = lax.dynamic_slice_in_dim(sums, 4 * D + place * (FF // 4), FF // 4)
     return (block_out, input_grad, own[0], own[1], qkv_sum, out_sum, own[2], up_sum, own_up, down_sum, own[3])

time: 485 us -> 332 us (0.68)
  waiting for transfers between devices: 101 us -> 0 us
  Pallas kernels: 233 us -> 320 us
  blocking collectives: 49.7 us -> 0 us
  starting transfers between devices: 32.3 us -> 0 us
  local copies, waits for them, and re-layouts: 36.3 us -> 7.47 us
  other arithmetic: 26.7 us -> 1.4 us
    ppermute x33 -> x0, waiting for transfers between devices: 101 us -> none  [flip(): return lax.ppermute(values, axis, [(i, i ^ bit) for i in range(count)])]
    pallas_call x4, Pallas kernels: 162 us -> 238 us  [the longest x1 91.3 us: bwd_attn(): pl.pallas_call(partial(bwd_attn_kernel, half), grid=(PAIRS,), in_specs=[o...]
    psum x1 -> x0, blocking collectives: 49.7 us -> none  [even_body(): sums = lax.psum(sums, ('ctx', 'fsdp'))]
    ppermute x33 -> x0, starting transfers between devices: 27.6 us -> none  [flip(): return lax.ppermute(values, axis, [(i, i ^ bit) for i in range(count)])]
    convert_element_type x26 -> x0, other arithmetic: 20.4 us -> none  [the longest x20 14.8 us: halve(): return (kept.astype(F32) + received.astype(F32)).astype(BF)]
    pallas_call x1, Pallas kernels: 71.7 us -> 82.4 us  [fwd_attn(): pl.pallas_call(partial(fwd_attn_comm_kernel, half), grid=(PAIRS,), in_spe...]
    squeeze x20 -> x0, local copies, waits for them, and re-layouts: 10.5 us -> none  [pick(): return lax.dynamic_index_in_dim(values, index, axis, keepdims=False)]
    unnamed x28 -> x0, local copies, waits for them, and re-layouts: 9.55 us -> none
  transfers between devices with their start and end apart: 34 -> 0, of which waited for: 21 -> 0; matrix products, arithmetic and copies ran while one was open for 9% -> 0% of each run, Pallas kernels for 0% -> 0%
where the time goes in v3:
time: 332 us; the launch traced here: 330 us
  Pallas kernels  320 us (96%)
  local copies, waits for them, and re-layouts  7.47 us (2%)
    pallas_call x1, Pallas kernels, bwd_attn(): pl.pallas_call(partial(bwd_attn_kernel, half), grid=(PAIRS,), in_specs=[o...  91.3 us
    pallas_call x1, Pallas kernels, ffn(): pl.pallas_call(ffn_kernel, grid=(2 * STEPS,), in_specs=[once((R, D)), onc...  82.4 us
    pallas_call x1, Pallas kernels, fwd_attn(): pl.pallas_call(partial(fwd_attn_comm_kernel, half), grid=(PAIRS,), in_spe...  82.4 us
    pallas_call x1, Pallas kernels, tail(): pl.pallas_call(tail_kernel, in_specs=[ANYSPACE] * 5 + [INVMEM] * 5, out_s...  55.1 us
    pallas_call x1, Pallas kernels, assemble(): pl.pallas_call(assemble_kernel, grid=(STEPS,), in_specs=[pl.BlockSpec((1,...  8.87 us

profile of v3, /device:TPU:0, one launch (start us, length us, event | category | flops | bytes accessed | tf_op | source)
XLA Modules:
  0.0 329.8 jit_solution(14385768281645556666)
XLA Ops:
  0.6 0.8 add_bitcast_fusion
  1.4 0.6 broadcast_in_dim.8.refs_1_
  2.0 0.7 stack.15
  2.7 0.7 stack.16
  3.4 0.7 stack.17
  4.0 0.7 stack.18
  4.7 0.7 reshape.54
  5.4 0.6 fusion.2.refs_8_
  6.0 0.7 broadcast_1_refs_9__refs_14_.2.refs_9_.refs_14_
  6.7 82.4 %fwd_attn.1 = (bf16[1152,768]{1,0:T(8,128)(2,1)}, bf16[1152,768]{1,0:T(8,128)(2,1)}, bf16[1152,768]{1,0:T(8,128)(2,1)}, bf16[1152,768]{1,0:T(8,128)(2,1)}, f32[6...) custom-call(bf16[4,2,64,768]{3,2,1,0:T(8,128)(2,1)} %refs_0_.1, ...), custom_call_target="tpu_custom_call" | custom-call | flops 17666408448 | bytes 16777216 | tf_op jit(solution)/shard_map/fwd_attn/pallas_call | solution.py:538
  89.1 82.4 %ffn.1 = (f32[1,3072]{1,0:T(1,128)}, f32[1,768]{1,0:T(1,128)}, f32[1,768]{1,0:T(1,128)}, f32[1152,768]{1,0:T(8,128)}, bf16[4,2,2,64,768]{4,3,2,1,0:T(8,128)(2,1)...) custom-call(f32[1152,768]{1,0:T(8,128)} %get-tuple-element.58.x1, ...), custom_call_target="tpu_custom_call" | custom-call | flops 38050725888 | bytes 41943040 | tf_op jit(solution)/shard_map/ffn/pallas_call | solution.py:688
  171.5 91.3 %bwd_attn.1 = (bf16[576,768]{1,0:T(8,128)(2,1)}, f32[1,768]{1,0:T(1,128)}, f32[1,768]{1,0:T(1,128)}, bf16[6,2,768,128]{3,2,1,0:T(8,128)(2,1)}, bf16[1,2,2,576,12...) custom-call(bf16[576,768]{1,0:T(8,128)(2,1)} %bitcast.20, ...), custom_call_target="tpu_custom_call" | custom-call | flops 41448112128 | bytes 31457280 | tf_op jit(solution)/shard_map/bwd_attn/pallas_call | solution.py:814
  262.8 55.1 %tail.1 = (bf16[6,2,768,128]{3,2,1,0:T(8,128)(2,1)}, bf16[4,2,576,128]{3,2,1,0:T(8,128)(2,1)}, bf16[4,2,64,768]{3,2,1,0:T(8,128)(2,1)}, f32[48,128]{1,0:T(8,128)}) custom-call(bf16[6,2,768,128]{3,2,1,0:T(8,128)(2,1)} %get-tuple-element.74.tiles, bf16[1,2,2,576,128]{4,3,2,1,0:T(8,128)(2,1)} %get-tuple-element.75.wpair, ...), custom_call_target="tpu_custom_call", output_to_operand_aliasing={{0}: (0, {})} | custom-call | tf_op jit(solution)/shard_map/tail/pallas_call | solution.py:1209
  317.9 8.9 %assemble.1 = (f32[192,3072]{1,0:T(8,128)}, f32[768,768]{1,0:T(8,128)}, f32[192,768]{1,0:T(8,128)}, f32[192,2304]{1,0:T(8,128)}, f32[8,64,768]{2,1,0:T(8,128)}, /*index=5*/bf16[16,64,768]{2,1,0:T(8,128)(2,1)}) custom-call(bf16[6,2,768,128]{3,2,1,0:T(8,128)(2,1)} %get-tuple-element.84.ffn, bf16[4,2,576,128]{3,2,1,0:T(8,128)(2,1)} %get-tuple-element.85.wings, ...), custom_call_target="tpu_custom_call" | custom-call | tf_op jit(solution)/shard_map/assemble/pallas_call | solution.py:829
  326.8 1.5 fusion.10
  328.3 1.4 dynamic_slice.18
  (1 shorter events, 0.0 us)

commit v4 on v3

--- a/solution.py
+++ b/solution.py
@@ -455,7 +455,7 @@
     c,f=place_ids()
     piece=half//9
     weight=lambda i,shard,full,parts: GatherRows(shard,full,w_send.at[i],w_recv.at[i],local.at[i],parts)
-    w_qkv,w_out,w_up,w_down=weight(0,qkv,qkv_s,3),weight(1,out,out_s,1),weight(2,up,up_o,3),weight(3,down,down_o,3)
+    w_qkv,w_out,w_up,w_down=weight(0,qkv,qkv_s,3),weight(1,out,out_s,1),weight(2,up,up_o,3),GatherRows(down,down_o,w_send.at[3],w_recv.at[3],local.at[3],3,False)
     rows=ToUnit(lambda q,h:clean.at[q,h],lambda t:clean_s.at[t],a_send,a_recv,local.at[4])
     notes=ToUnit(lambda q,h:meta.at[2*q+h],lambda t:meta_s.at[t],m_send,m_recv,local.at[5])
     grads=[ToUnit(lambda q,h:gout.at[q,0,h],lambda t:cot_o.at[t],c_send,c_recv,local.at[6])]
@@ -485,7 +485,7 @@
                 d.start()
                 d.wait()
         for i in range(3): w_qkv.relay_x(i)
-        for r in grads: r.begin()
+        for r in grads: r.begin_straight()
         own.wait()
         table.wait()
         for i,other in enumerate(others):
@@ -514,11 +514,11 @@
         @pl.when(p==i)
         def _():
             for op in ops: op()
-    at(0,w_out.relay_far,*[partial(w_up.relay_far,i) for i in range(3)])
-    at(1,w_out.relay_x,partial(w_up.relay_x,0),partial(w_down.relay_far,0))
-    at(2,partial(w_up.relay_x,1),partial(w_down.relay_far,1),partial(w_down.relay_far,2))
-    at(3,partial(w_up.relay_x,2),w_out.finish,copies[1].start,partial(w_down.relay_x,0))
-    at(4,partial(w_down.relay_x,1),partial(w_down.relay_x,2))
+    at(0,w_out.relay_far,*[partial(w_up.relay_far,i) for i in range(2)])
+    at(1,w_out.relay_x,partial(w_up.relay_far,2),partial(w_up.relay_x,0),grads[0].begin_across)
+    at(2,w_out.finish,copies[1].start,partial(w_up.relay_x,1),partial(w_down.relay_far,0))
+    at(3,partial(w_up.relay_x,2),partial(w_down.relay_far,1))
+    at(4,partial(w_down.relay_far,2))
     @pl.when(p==pl.num_programs(0)-1)
     def _():
         for w in (w_up,w_down): w.finish()
@@ -530,8 +530,8 @@
 
 def fwd_attn(clean,meta,gout,trig,qkv,out,up,down,small):
     piece=clean.shape[2]; half=9*piece; R=2*half
-    zeros=jnp.zeros((2,piece,D),BF)
-    blank=jnp.concatenate([jnp.full((2,8,piece),-1,jnp.int32),jnp.zeros((2,8,128-piece),jnp.int32)],axis=2)
+    zeros=np.zeros((2,piece,D),BF)
+    blank=np.concatenate([np.full((2,8,piece),-1,np.int32),np.zeros((2,8,128-piece),np.int32)],axis=2)
     nt=len(tiles_of(half))*2; ntp=-(-nt//8)*8
     rows=pl.BlockSpec((R,PAIR),lambda p:(0,p))
     sds=jax.ShapeDtypeStruct
@@ -555,11 +555,11 @@
 def down_specs(): return [pl.BlockSpec((128,D),(lambda s:(lambda j:(s*STEPS+j,0)))(s)) for s in range(4)]
 def bias_specs(): return [pl.BlockSpec((1,128),(lambda s:(lambda j:(0,s*STEPS+j)))(s)) for s in range(4)]
 
-FFN_TABLE={2: [(0, None, 0)], 3: [(0, 0, 1)], 4: [(1, None, 0)], 5: [(1, 0, 1)], 6: [(2, None, 0), (0, 1, None)], 7: [(2, 0, 1)], 8: [(3, None, 0), (1, 1, None)], 9: [(3, 0, 1)], 10: [(4, None, 0), (2, 1, None)], 11: [(4, 0, 1)], 12: [(5, None, 0)]}
-FFN_END=[(3, 1), (5, 0), (4, 1)]
-ATTN_TABLE={0: [(5, None, 1), (0, None, 2), (1, None, 2), (2, None, 2), (3, None, 2), (4, None, 2)], 1: [(6, None, 0)], 2: [(0, 2, 3), (6, 0, 1)], 3: [(0, 3, 4), (1, 2, 3), (5, 1, 2)], 4: [(7, None, 0), (2, 2, 3), (6, 1, 2)], 5: [(0, 4, 5), (1, 3, 4), (2, 3, 4), (3, 2, 3), (7, 0, 1)], 6: [(0, 5, 6), (4, 2, 3)], 7: [(1, 4, 5), (2, 4, 5), (3, 3, 4), (5, 2, 3), (7, 1, 2), (0, 6, 7)], 8: [(8, None, 0), (4, 3, 4), (6, 2, 3)], 9: [(1, 5, 6), (2, 5, 6), (5, 3, 4), (7, 2, 3), (8, 0, 1), (3, 4, 5)], 10: [(0, 7, None), (1, 6, 7), (4, 4, 5), (6, 3, 4)], 11: [(2, 6, 7), (5, 4, 5), (7, 3, 4), (8, 1, 2)], 12: [(9, None, 0)]}
-ATTN_END=[(1, 7), (3, 5), (4, 5), (6, 4), (2, 7), (9, 0), (5, 5), (8, 2), (7, 4)]
-TAIL_ORDER=[("sums", None, 0), (9, None, 1), (8, None, 3), (6, None, 5), (7, None, 5), (3, None, 6), (4, None, 6), (5, None, 6), ("rows", None, 1), ("rows", None, 2), ("sums", 0, 1), (8, 3, 4), (6, 5, 6), ("sums", 1, 2), (7, 5, 6), (3, 6, 7), (9, 1, 2), ("rows", None, 3), (4, 6, 7), ("sums", 2, 3), (5, 6, 7), (3, 7, None), ("sums", 3, 4), (9, 2, 3), ("rows", None, 4), (8, 4, 5), (6, 6, 7), ("sums", 4, None), (7, 6, 7), (4, 7, None), (9, 3, 4), ("rows", None, 5), (5, 7, None), (8, 5, 6), (9, 4, 5), ("rows", None, 6), (8, 6, 7), (6, 7, None), (9, 5, 6), ("rows", None, 7), (7, 7, None), (9, 6, 7), (8, 7, None), (9, 7, None)]
+FFN_TABLE={2: [(0, None, 0)], 4: [(1, None, 0), (0, 0, 1)], 6: [(2, None, 0), (1, 0, 1)], 8: [(3, None, 0), (0, 1, None), (2, 0, 1)], 9: [(3, 0, None)], 10: [(4, None, 0), (1, 1, None)], 12: [(5, None, 0)]}
+FFN_END=[(4, 0), (2, 1), (5, 0)]
+ATTN_TABLE={0: [(3, None, 1), (4, None, 1), (5, None, 1), (0, None, 2), (1, None, 2), (2, None, 2)], 1: [(6, None, 0)], 2: [(0, 2, 3), (6, 0, 1)], 3: [(0, 3, 4), (1, 2, 3), (3, 1, 2)], 4: [(7, None, 0), (2, 2, 3)], 5: [(0, 4, 5), (1, 3, 4), (2, 3, 4), (3, 2, 3), (4, 1, 2), (7, 0, 1)], 6: [(0, 5, 6)], 7: [(1, 4, 5), (2, 4, 5), (3, 3, 4), (4, 2, 3), (5, 1, 2), (0, 6, 7)], 8: [(8, None, 0), (6, 1, 2), (1, 5, 6)], 9: [(2, 5, 6), (4, 3, 4), (3, 4, 5), (5, 2, 3), (8, 0, 1), (1, 6, 7)], 10: [(0, 7, None), (2, 6, 7), (7, 1, 2)], 11: [(3, 5, 6), (4, 4, 5), (5, 3, 4), (6, 2, 3), (8, 1, 2), (1, 7, None)], 12: [(9, None, 0)]}
+ATTN_END=[(3, 6), (2, 7), (4, 5), (9, 0), (7, 2), (6, 3), (5, 4), (8, 2)]
+TAIL_ORDER=[("sums", None, 0), (9, None, 1), (7, None, 3), (8, None, 3), (6, None, 4), (5, None, 5), (4, None, 6), (3, None, 7), ("rows", None, 1), ("rows", None, 2), ("sums", 0, 1), (7, 3, 4), (8, 3, 4), (3, 7, None), ("sums", 1, 2), (6, 4, 5), (9, 1, 2), ("rows", None, 3), (4, 6, 7), (5, 5, 6), ("sums", 2, 3), (9, 2, 3), ("rows", None, 4), ("sums", 3, 4), (7, 4, 5), (8, 4, 5), (4, 7, None), ("sums", 4, None), (6, 5, 6), (5, 6, 7), (9, 3, 4), ("rows", None, 5), (5, 7, None), (7, 5, 6), (6, 6, 7), (8, 5, 6), (9, 4, 5), ("rows", None, 6), (7, 6, 7), (6, 7, None), (8, 6, 7), (9, 5, 6), ("rows", None, 7), (7, 7, None), (9, 6, 7), (8, 7, None), (9, 7, None)]
 
 def after(state,table,end):
     state=dict(state)
@@ -585,6 +585,8 @@
     for i,take,start in ops:
         if take is not None: chunks[i].take(take)
         if start is not None: chunks[i].start(start)
+
+PHASE=2*STEPS
 
 def ffn_kernel(x1,vec,*refs):
     wup,bup,wdn,rest=refs[:4],refs[4:8],refs[8:12],refs[12:]
@@ -612,24 +614,27 @@
         h_s[...]=h
         hT_s[...]=h.T
         acc[...]=x1[...]+bdn[...].astype(F32)
-    @pl.when(g<STEPS)
+    for copy in range(2):
+        @pl.when((g>=copy*STEPS)&(g<(copy+1)*STEPS))
+        def _():
+            for i in range(2):
+                r=slice((2*copy+i)*R//4,(2*copy+i+1)*R//4)
+                u=dot_nn(h_s[r],wu())+bias
+                act=(0.5*u*(1.0+jnp.tanh(GC*(u+0.044715*u*u*u)))).astype(BF)
+                acc[r]+=dot_nn(act,wd())
+        @pl.when(g==(copy+1)*STEPS-1)
+        def _():
+            out_s[9*copy:9*copy+9]=acc[copy*R//2:(copy+1)*R//2].astype(BF).reshape(9,piece,D)
+            leave[copy].begin()
+    @pl.when(g==PHASE-1)
     def _():
-        for i in range(3):
-            r=slice(i*ch,(i+1)*ch)
-            u=dot_nn(h_s[r],wu())+bias
-            act=(0.5*u*(1.0+jnp.tanh(GC*(u+0.044715*u*u*u)))).astype(BF)
-            acc[r]+=dot_nn(act,wd())
-    @pl.when(g==STEPS-1)
-    def _():
-        for i in range(3): out_s[6*i:6*i+6]=acc[i*ch:(i+1)*ch].astype(BF).reshape(6,piece,D)
-        for r in leave: r.begin()
         arrive.finish()
         first.wait()
         acc[...]=jnp.zeros_like(acc)
         dbdn_o[...]=jnp.sum(gy_s[...].astype(F32).reshape(R,D),axis=0,keepdims=True)
-    @pl.when(g>=STEPS)
+    @pl.when(g>=PHASE)
     def _():
-        j=g-STEPS
+        j=g-PHASE
         for i in range(2,STEPS):
             @pl.when(j==i)
             def _(): chunks[i-2].sent(0)
@@ -679,15 +684,15 @@
 
 def ffn(x1,vec,wup,bup,wdn,gy0,gout):
     R=x1.shape[0]; half=R//2; piece=half//9
-    zeros=jnp.zeros((2,piece,D),BF)
+    zeros=np.zeros((2,piece,D),BF)
     count=lambda low,high: max(1,len(in_state(FFN_STATE,range(STEPS),low,high)))
     tile=lambda j: lax.rem(j,STEPS)
     ups=[pl.BlockSpec((D,128),(lambda s:(lambda j:(0,s*STEPS+tile(j))))(s)) for s in range(4)]
     downs=[pl.BlockSpec((128,D),(lambda s:(lambda j:(s*STEPS+tile(j),0)))(s)) for s in range(4)]
     biases=[pl.BlockSpec((1,128),(lambda s:(lambda j:(0,s*STEPS+tile(j))))(s)) for s in range(4)]
-    return pl.pallas_call(ffn_kernel,grid=(2*STEPS,),
+    return pl.pallas_call(ffn_kernel,grid=(PHASE+STEPS,),
         in_specs=[once((R,D)),once((4,D))]+ups+biases+downs+[ANYSPACE]*2+[once(zeros.shape)],
-        out_specs=[pl.BlockSpec((1,512),lambda j:(0,jnp.maximum(j-STEPS,0))),whole((1,D)),whole((1,D))]+[ANYSPACE]*5,
+        out_specs=[pl.BlockSpec((1,512),lambda j:(0,jnp.maximum(j-PHASE,0))),whole((1,D)),whole((1,D))]+[ANYSPACE]*5,
         out_shape=[jax.ShapeDtypeStruct((1,FF),F32),jax.ShapeDtypeStruct((1,D),F32),jax.ShapeDtypeStruct((1,D),F32),jax.ShapeDtypeStruct((R,D),F32),jax.ShapeDtypeStruct((4,2,2,piece,D),BF),
             jax.ShapeDtypeStruct((count(0,0),2,2,TILE,128),BF),jax.ShapeDtypeStruct((count(1,3),2,TILE,128),BF),jax.ShapeDtypeStruct((1,2,TILE,128),BF)],
         scratch_shapes=[pltpu.VMEM((R,D),BF),pltpu.VMEM((D,R),BF),pltpu.VMEM((R,D),F32),pltpu.VMEM((18,piece,D),BF),pltpu.VMEM((18,piece,D),BF),pltpu.VMEM((R,512),BF),pltpu.VMEM((R,512),BF),
@@ -882,7 +887,7 @@
                       {"ctx": t - odd * last})
 
     def begin(self):
-        for s in range(1, 8):
+        for s in (1, 7, 3, 5, 2, 6, 4):
             self.message(s).start()
 
         @pl.when(self.c == 7)
@@ -892,6 +897,22 @@
         @pl.when(self.c != 7)
         def _():
             self.own_safe().start()
+
+    def begin_straight(self):
+        for s in (2, 4, 6):
+            self.message(s).start()
+
+        @pl.when(self.c != 7)
+        def _():
+            self.own_safe().start()
+
+    def begin_across(self):
+        for s in (1, 3, 5, 7):
+            self.message(s).start()
+
+        @pl.when(self.c == 7)
+        def _():
+            self.message(0).start()
 
     def own_safe(self):
         c = self.c
@@ -960,16 +981,16 @@
     def each(self, remote_op, own_op):
         c = self.c
         part = c % 2
-        for s in range(1, 8):
+        @pl.when(part == 0)
+        def _():
+            remote_op(self.extra())
+
+        for s in (1, 7, 3, 5, 2, 6, 4):
             rank = (c + s) % 8
 
             @pl.when((part == 0) | (rank != 7))
             def _():
                 remote_op(self.message(s))
-
-        @pl.when(part == 0)
-        def _():
-            remote_op(self.extra())
 
         @pl.when(c != 7)
         def _():
@@ -1007,12 +1028,12 @@
 
 
 class GatherRows:
-    def __init__(self, shard, full, send, recv, local, parts=1):
+    def __init__(self, shard, full, send, recv, local, parts=1, share=True):
         c, f = place_ids()
         n = shard.shape[0]
-        n2 = n // 2
+        n2 = n // 2 if share else n
         m = n2 // parts
-        h = c % 2
+        h = c % 2 if share else 0
         sib, far, xn = f + 1 - 2 * (f % 2), (f + 2) % 4, c + 1 - 2 * (c % 2)
         diag = (sib + 2) % 4
         rows = lambda start, size: full.at[pl.ds(pl.multiple_of(start, 16), size)]
@@ -1030,12 +1051,13 @@
             self.to_far.append(remote(shard.at[pl.ds(pl.multiple_of(a, 16), m)], rows(f * n + a, m), send.at[k], recv.at[k],
                                       {"fsdp": far}))
             self.from_far.append(same(near, k, {"fsdp": far}))
-            self.to_x.append(same(near, k + 1, {"ctx": xn}))
-            self.from_x.append(same(away, k + 1, {"ctx": xn}))
             self.near_core.append(same(near, k + 2, {"fsdp": sib}))
-            self.away_core.append(same(away, k + 3, {"fsdp": sib}))
             self.from_near.append(same(rows(diag * n + a, m), k + 2, {"fsdp": sib}))
-            self.from_away.append(same(rows(diag * n + b, m), k + 3, {"fsdp": sib}))
+            if share:
+                self.to_x.append(same(near, k + 1, {"ctx": xn}))
+                self.from_x.append(same(away, k + 1, {"ctx": xn}))
+                self.away_core.append(same(away, k + 3, {"fsdp": sib}))
+                self.from_away.append(same(rows(diag * n + b, m), k + 3, {"fsdp": sib}))
 
     def begin(self):
         for copy in self.to_far:
@@ -1045,7 +1067,8 @@
 
     def relay_far(self, i=0):
         self.from_far[i].wait_recv()
-        self.to_x[i].start()
+        if self.to_x:
+            self.to_x[i].start()
         self.near_core[i].start()
 
     def relay_x(self, i=0):
@@ -1265,9 +1288,12 @@
     width = mask_embed.shape[0]
     meta = jnp.concatenate([segments.reshape(8, 1, piece), noise.reshape(8, 1, piece)], axis=2)
     meta = jnp.broadcast_to(meta, (8, 8, 2 * piece))
-    small = jnp.stack([mask_embed, norm1_gain, norm2_gain, down_bias])
-    small = jnp.concatenate([jnp.pad(small, ((0, 0), (0, 256 - width))), up_bias.reshape(-1, 256)])
-    small = jnp.pad(small, ((0, 16 - small.shape[0]), (0, 0)))
+    row = lax.broadcasted_iota(jnp.int32, (16, 256), 0)
+    small = jnp.zeros((16, 256), BF)
+    for i, vector in enumerate((mask_embed, norm1_gain, norm2_gain, down_bias)):
+        small = jnp.where(row == i, jnp.pad(vector, (0, 256 - width))[None], small)
+    for i in range(up_bias.shape[0] // 256):
+        small = jnp.where(row == 4 + i, up_bias[i * 256:(i + 1) * 256][None], small)
     q, k, v, mixed, lse, resid, mask, seg_col, seg_row, vectors, up_shift, qkv_full, out_full, up_full, down_full, cotangent, clean = fwd_attn(
         clean_in, meta, out_grad, rope_constant(half), qkv_weight, out_weight, up_weight, down_weight, small)
     clean = clean.reshape(half, D)

time: 332 us -> 324 us (0.976)
  Pallas kernels: 320 us -> 313 us
    pallas_call x1, Pallas kernels: 82.4 us -> 75.2 us  [fwd_attn(): pl.pallas_call(partial(fwd_attn_comm_kernel, half), grid=(PAIRS,), in_spe...]
    pallas_call x1, Pallas kernels: 55.1 us -> 60 us  [tail(): pl.pallas_call(tail_kernel, in_specs=[ANYSPACE] * 5 + [INVMEM] * 5, out_s...]
    pallas_call x1, Pallas kernels: 91.3 us -> 86.6 us  [bwd_attn(): pl.pallas_call(partial(bwd_attn_kernel, half), grid=(PAIRS,), in_specs=[o...]
where the time goes in v4:
time: 324 us; the launch traced here: 323 us
  Pallas kernels  313 us (97%)
  local copies, waits for them, and re-layouts  7.58 us (2%)
    pallas_call x1, Pallas kernels, bwd_attn(): pl.pallas_call(partial(bwd_attn_kernel, half), grid=(PAIRS,), in_specs=[o...  86.6 us
    pallas_call x1, Pallas kernels, ffn(): pl.pallas_call(ffn_kernel, grid=(PHASE + STEPS,), in_specs=[once((R, D)),...  81.9 us
    pallas_call x1, Pallas kernels, fwd_attn(): pl.pallas_call(partial(fwd_attn_comm_kernel, half), grid=(PAIRS,), in_spe...  75.2 us
    pallas_call x1, Pallas kernels, tail(): pl.pallas_call(tail_kernel, in_specs=[ANYSPACE] * 5 + [INVMEM] * 5, out_s...  60 us
    pallas_call x1, Pallas kernels, assemble(): pl.pallas_call(assemble_kernel, grid=(STEPS,), in_specs=[pl.BlockSpec((1,...  8.87 us

profile of v4, /device:TPU:0, one launch (start us, length us, event | category | flops | bytes accessed | tf_op | source)
XLA Modules:
  0.0 322.5 jit_solution(14039717291780367400)
XLA Ops:
  0.6 0.8 fusion.1
  1.5 0.7 pad.13
  2.1 0.7 pad.14
  2.8 0.7 pad.15
  3.5 0.7 pad.16
  4.1 0.7 select_select_fusion.refs_8_
  4.8 0.8 add_bitcast_fusion
  5.6 0.6 broadcast_in_dim.56.refs_1_
  6.2 0.7 call_exported.0.refs_9_.refs_14_
  6.9 75.2 %fwd_attn.1 = (bf16[1152,768]{1,0:T(8,128)(2,1)}, bf16[1152,768]{1,0:T(8,128)(2,1)}, bf16[1152,768]{1,0:T(8,128)(2,1)}, bf16[1152,768]{1,0:T(8,128)(2,1)}, f32[6...) custom-call(bf16[4,2,64,768]{3,2,1,0:T(8,128)(2,1)} %refs_0_.1, ...), custom_call_target="tpu_custom_call" | custom-call | flops 17666408448 | bytes 16777216 | tf_op jit(solution)/shard_map/fwd_attn/pallas_call | solution.py:538
  82.1 81.9 %ffn.1 = (f32[1,3072]{1,0:T(1,128)}, f32[1,768]{1,0:T(1,128)}, f32[1,768]{1,0:T(1,128)}, f32[1152,768]{1,0:T(8,128)}, bf16[4,2,2,64,768]{4,3,2,1,0:T(8,128)(2,1)...) custom-call(f32[1152,768]{1,0:T(8,128)} %get-tuple-element.58.x1, ...), custom_call_target="tpu_custom_call" | custom-call | flops 38050725888 | bytes 41943040 | tf_op jit(solution)/shard_map/ffn/pallas_call | solution.py:693
  164.0 86.6 %bwd_attn.1 = (bf16[576,768]{1,0:T(8,128)(2,1)}, f32[1,768]{1,0:T(1,128)}, f32[1,768]{1,0:T(1,128)}, bf16[6,2,768,128]{3,2,1,0:T(8,128)(2,1)}, bf16[1,2,2,576,12...) custom-call(bf16[576,768]{1,0:T(8,128)(2,1)} %bitcast.20, ...), custom_call_target="tpu_custom_call" | custom-call | flops 41448112128 | bytes 31457280 | tf_op jit(solution)/shard_map/bwd_attn/pallas_call | solution.py:819
  250.6 60.0 %tail.1 = (bf16[6,2,768,128]{3,2,1,0:T(8,128)(2,1)}, bf16[4,2,576,128]{3,2,1,0:T(8,128)(2,1)}, bf16[4,2,64,768]{3,2,1,0:T(8,128)(2,1)}, f32[48,128]{1,0:T(8,128)}) custom-call(bf16[6,2,768,128]{3,2,1,0:T(8,128)(2,1)} %get-tuple-element.74.tiles, bf16[1,2,2,576,128]{4,3,2,1,0:T(8,128)(2,1)} %get-tuple-element.75.wpair, ...), custom_call_target="tpu_custom_call", output_to_operand_aliasing={{0}: (0, {})} | custom-call | tf_op jit(solution)/shard_map/tail/pallas_call | solution.py:1232
  310.6 8.9 %assemble.1 = (f32[192,3072]{1,0:T(8,128)}, f32[768,768]{1,0:T(8,128)}, f32[192,768]{1,0:T(8,128)}, f32[192,2304]{1,0:T(8,128)}, f32[8,64,768]{2,1,0:T(8,128)}, /*index=5*/bf16[16,64,768]{2,1,0:T(8,128)(2,1)}) custom-call(bf16[6,2,768,128]{3,2,1,0:T(8,128)(2,1)} %get-tuple-element.84.ffn, bf16[4,2,576,128]{3,2,1,0:T(8,128)(2,1)} %get-tuple-element.85.wings, ...), custom_call_target="tpu_custom_call" | custom-call | tf_op jit(solution)/shard_map/assemble/pallas_call | solution.py:834
  319.5 1.5 fusion
  321.0 1.4 dynamic_slice.18
  (4 shorter events, 0.0 us)

commit v5 on v4

--- a/solution.py
+++ b/solution.py
@@ -447,10 +447,10 @@
     return jnp.concatenate([small[f,i:i+1,:D//4] for f in range(4)],axis=1).astype(F32)
 
 def fwd_attn_comm_kernel(half,*refs):
-    clean,meta,gout,trig,qkv,out,up,down,small,zeros,blank=refs[:11]
-    q_o,k_o,v_o,mix_o,lse_o,x1_o,noise_o,segc_o,segr_o,vec_o,bias_o,qkv_o,out_o,up_o,down_o,cot_o,clean_o=refs[11:28]
-    h_s,bias_s,self_s,mix_s,clean_s,meta_s,small_s,qkv_s,out_s,trig_s=refs[28:38]
-    a_send,a_recv,m_send,m_recv,c_send,c_recv,w_send,w_recv,s_send,s_recv,local=refs[38:]
+    clean,meta,gout,trig,qkv,out,up,down,small=refs[:9]
+    q_o,k_o,v_o,mix_o,lse_o,x1_o,noise_o,segc_o,segr_o,vec_o,bias_o,qkv_o,out_o,up_o,down_o,cot_o,clean_o=refs[9:26]
+    h_s,bias_s,self_s,mix_s,clean_s,meta_s,small_s,qkv_s,out_s,trig_s=refs[26:36]
+    a_send,a_recv,m_send,m_recv,c_send,c_recv,w_send,w_recv,s_send,s_recv,local=refs[36:]
     p=pl.program_id(0)
     c,f=place_ids()
     piece=half//9
@@ -477,13 +477,14 @@
         w_up.begin()
         w_down.begin()
         for i in range(3): w_qkv.relay_far(i)
-        pads=[pltpu.make_async_copy(zeros,clean_s.at[pl.ds(7,2)],local.at[13]),pltpu.make_async_copy(blank,meta_s.at[pl.ds(7,2)],local.at[13])]
-        pads.append(pltpu.make_async_copy(zeros,cot_o.at[pl.ds(7,2)],local.at[13]))
         @pl.when(c%2==1)
         def _():
-            for d in pads:
-                d.start()
-                d.wait()
+            clean_s[7:9]=jnp.zeros((2,)+clean_s.shape[1:],BF)
+            line=lax.broadcasted_iota(jnp.int32,(2,)+meta_s.shape[1:],1)
+            meta_s[7:9]=jnp.where(line==0,-1,0)
+            pad=pltpu.make_async_copy(clean_s.at[pl.ds(7,2)],cot_o.at[pl.ds(7,2)],local.at[13])
+            pad.start()
+            pad.wait()
         for i in range(3): w_qkv.relay_x(i)
         for r in grads: r.begin_straight()
         own.wait()
@@ -492,19 +493,15 @@
             sends[i].wait_send()
             remote(small_s.at[other],small_s.at[other],s_send.at[i],s_recv.at[i],{"fsdp":other}).wait_recv()
         notes.finish()
-        lane=lax.broadcasted_iota(jnp.int32,(1,128),1)
+        note=lambda i: jnp.concatenate([meta_s[i,0:1],meta_s[i,1:2]],axis=1).astype(F32)
         for i in range(9):
-            t=jnp.broadcast_to(meta_s[i,0:1].astype(F32),(128,128)).T
+            t=jnp.broadcast_to(note(i),(128,128)).T
             segc_o[i*piece:(i+1)*piece]=t[:piece,0:1]
             noise_o[i*piece:(i+1)*piece]=t[piece:,0:1].astype(jnp.int32)
         for i in range(5):
-            even=meta_s[2*i,0:1].astype(F32)
-            odd=pltpu.roll(meta_s[min(2*i+1,8)].astype(F32),64,1)[0:1]
-            segr_o[:,i*128:(i+1)*128]=jnp.where(lane<64,even,odd)
-        for i in range(2): vec_o[i:i+1]=vector_row(small_s,2+i)
-        for i in range(2): vec_o[2+i:3+i]=vector_row(small_s,i)
-        for g in range(4):
-            for i in range(3): bias_o[:,g*768+i*256:g*768+(i+1)*256]=small_s[g,4+i:5+i].astype(F32)
+            segr_o[:,i*128:(i+1)*128]=jnp.concatenate([meta_s[2*i,0:1],meta_s[min(2*i+1,8),0:1]],axis=1).astype(F32)
+        for i in range(4): vec_o[i:i+1]=vector_row(small_s,(2,3,0,1)[i])
+        for g in range(4): bias_o[:,g*768:(g+1)*768]=jnp.concatenate([small_s[g,4+i:5+i] for i in range(4)],axis=1).astype(F32)
         rows.finish()
         w_qkv.finish()
         copies[0].start()
@@ -530,22 +527,20 @@
 
 def fwd_attn(clean,meta,gout,trig,qkv,out,up,down,small):
     piece=clean.shape[2]; half=9*piece; R=2*half
-    zeros=np.zeros((2,piece,D),BF)
-    blank=np.concatenate([np.full((2,8,piece),-1,np.int32),np.zeros((2,8,128-piece),np.int32)],axis=2)
     nt=len(tiles_of(half))*2; ntp=-(-nt//8)*8
     rows=pl.BlockSpec((R,PAIR),lambda p:(0,p))
     sds=jax.ShapeDtypeStruct
     return pl.pallas_call(partial(fwd_attn_comm_kernel,half),grid=(PAIRS,),
-        in_specs=[ANYSPACE]*4+[once(a.shape) for a in (qkv,out,up,down,small,zeros,blank)],
+        in_specs=[ANYSPACE]*4+[once(a.shape) for a in (qkv,out,up,down,small)],
         out_specs=[rows,rows,rows,rows,pl.BlockSpec((1,ntp,256),lambda p:(p,0,0)),whole((R,D)),whole((half,1)),whole((half,1)),whole((1,640)),whole((4,D)),whole((1,FF))]+[ANYSPACE]*6,
         out_shape=[sds((R,D),BF)]*4+[sds((PAIRS,ntp,256),F32),sds((R,D),F32),sds((half,1),jnp.int32),sds((half,1),F32),sds((1,640),F32),sds((4,D),F32),sds((1,FF),F32),
             sds((D,3*D),BF),sds((D,D),BF),sds((D,FF),BF),sds((FF,D),BF),sds((9,piece,D),BF),sds((9,piece,D),BF)],
         scratch_shapes=[pltpu.VMEM((R,D),BF),pltpu.VMEM((2,half,half),F32),pltpu.VMEM((half,128),F32),pltpu.VMEM((PAIRS,R,PAIR),BF),
-            pltpu.VMEM((9,piece,D),BF),pltpu.VMEM((9,8,128),jnp.int32),pltpu.VMEM((4,)+small.shape,BF),pltpu.VMEM((D,3*D),BF),pltpu.VMEM((D,D),BF),pltpu.VMEM((half,2*PAIR),F32),
+            pltpu.VMEM((9,piece,D),BF),pltpu.VMEM((9,)+meta.shape[1:],jnp.int32),pltpu.VMEM((4,)+small.shape,BF),pltpu.VMEM((D,3*D),BF),pltpu.VMEM((D,D),BF),pltpu.VMEM((half,2*PAIR),F32),
             DMA((8,)),DMA((9,)),DMA((8,)),DMA((9,)),DMA((8,)),DMA((9,)),DMA((4,13)),DMA((4,13)),DMA((3,)),DMA((3,)),DMA((14,))],
         compiler_params=pltpu.CompilerParams(vmem_limit_bytes=VMEM_LIMIT,dimension_semantics=("arbitrary",),collective_id=1,has_side_effects=True),
         cost_estimate=pl.CostEstimate(flops=2*R*D*(3*D+D)+24*R*half*D//2*2,bytes_accessed=16<<20,transcendentals=R*half*HEADS),
-        name="fwd_attn")(clean,meta,gout,trig,qkv,out,up,down,small,zeros,blank)
+        name="fwd_attn")(clean,meta,gout,trig,qkv,out,up,down,small)
 
 GC=(2.0/3.141592653589793)**0.5
 def cols(refs): return jnp.concatenate([r[...] for r in refs],axis=1)
@@ -557,9 +552,8 @@
 
 FFN_TABLE={2: [(0, None, 0)], 4: [(1, None, 0), (0, 0, 1)], 6: [(2, None, 0), (1, 0, 1)], 8: [(3, None, 0), (0, 1, None), (2, 0, 1)], 9: [(3, 0, None)], 10: [(4, None, 0), (1, 1, None)], 12: [(5, None, 0)]}
 FFN_END=[(4, 0), (2, 1), (5, 0)]
-ATTN_TABLE={0: [(3, None, 1), (4, None, 1), (5, None, 1), (0, None, 2), (1, None, 2), (2, None, 2)], 1: [(6, None, 0)], 2: [(0, 2, 3), (6, 0, 1)], 3: [(0, 3, 4), (1, 2, 3), (3, 1, 2)], 4: [(7, None, 0), (2, 2, 3)], 5: [(0, 4, 5), (1, 3, 4), (2, 3, 4), (3, 2, 3), (4, 1, 2), (7, 0, 1)], 6: [(0, 5, 6)], 7: [(1, 4, 5), (2, 4, 5), (3, 3, 4), (4, 2, 3), (5, 1, 2), (0, 6, 7)], 8: [(8, None, 0), (6, 1, 2), (1, 5, 6)], 9: [(2, 5, 6), (4, 3, 4), (3, 4, 5), (5, 2, 3), (8, 0, 1), (1, 6, 7)], 10: [(0, 7, None), (2, 6, 7), (7, 1, 2)], 11: [(3, 5, 6), (4, 4, 5), (5, 3, 4), (6, 2, 3), (8, 1, 2), (1, 7, None)], 12: [(9, None, 0)]}
-ATTN_END=[(3, 6), (2, 7), (4, 5), (9, 0), (7, 2), (6, 3), (5, 4), (8, 2)]
-TAIL_ORDER=[("sums", None, 0), (9, None, 1), (7, None, 3), (8, None, 3), (6, None, 4), (5, None, 5), (4, None, 6), (3, None, 7), ("rows", None, 1), ("rows", None, 2), ("sums", 0, 1), (7, 3, 4), (8, 3, 4), (3, 7, None), ("sums", 1, 2), (6, 4, 5), (9, 1, 2), ("rows", None, 3), (4, 6, 7), (5, 5, 6), ("sums", 2, 3), (9, 2, 3), ("rows", None, 4), ("sums", 3, 4), (7, 4, 5), (8, 4, 5), (4, 7, None), ("sums", 4, None), (6, 5, 6), (5, 6, 7), (9, 3, 4), ("rows", None, 5), (5, 7, None), (7, 5, 6), (6, 6, 7), (8, 5, 6), (9, 4, 5), ("rows", None, 6), (7, 6, 7), (6, 7, None), (8, 6, 7), (9, 5, 6), ("rows", None, 7), (7, 7, None), (9, 6, 7), (8, 7, None), (9, 7, None)]
+ATTN_TABLE={0: [(3, None, 1), (4, None, 1), (5, None, 1), (0, None, 2), (1, None, 2), (2, None, 2)], 1: [(6, None, 0)], 2: [(0, 2, 3), (6, 0, 1)], 3: [(0, 3, 4), (1, 2, 3), (3, 1, 2)], 4: [(7, None, 0), (0, 4, 5), (2, 2, 3)], 5: [(1, 3, 4), (0, 5, 6), (3, 2, 3), (4, 1, 2), (7, 0, 1), (2, 3, 4)], 6: [(0, 6, 7), (1, 4, 5), (5, 1, 2)], 7: [(2, 4, 5), (3, 3, 4), (4, 2, 3)], 8: [(8, None, 0), (0, 7, None), (1, 5, 6), (2, 5, 6), (6, 1, 2)], 9: [(1, 6, 7), (3, 4, 5), (4, 3, 4), (5, 2, 3), (7, 1, 2), (8, 0, 1), (6, 2, 3)], 10: [(2, 6, 7), (3, 5, 6)], 11: [(1, 7, None), (3, 6, 7), (4, 4, 5), (5, 3, 4), (6, 3, 4), (7, 2, 3), (8, 1, 2)], 12: [(9, None, 0)]}
+TAIL_ORDER=[("sums", None, 0), (3, 7, None), (2, 7, None), (4, 5, 6), (5, 4, 5), (6, 4, 5), (7, 3, 4), (9, 0, 1), ("rows", None, 1), ("rows", None, 2), (8, 2, 3), ("sums", 0, 1), (4, 6, 7), ("sums", 1, 2), (5, 5, 6), (6, 5, 6), (9, 1, 2), ("rows", None, 3), (4, 7, None), (7, 4, 5), ("sums", 2, 3), (8, 3, 4), (9, 2, 3), ("rows", None, 4), ("sums", 3, 4), (5, 6, 7), (6, 6, 7), ("sums", 4, None), (7, 5, 6), (5, 7, None), (9, 3, 4), ("rows", None, 5), (8, 4, 5), (6, 7, None), (7, 6, 7), (9, 4, 5), ("rows", None, 6), (7, 7, None), (8, 5, 6), (9, 5, 6), ("rows", None, 7), (8, 6, 7), (9, 6, 7), (8, 7, None), (9, 7, None)]
 
 def after(state,table,end):
     state=dict(state)
@@ -569,7 +563,6 @@
     state.update(end)
     return state
 FFN_STATE=after({},FFN_TABLE,FFN_END)
-ATTN_STATE=after(FFN_STATE,ATTN_TABLE,ATTN_END)
 def in_state(state,ids,low,high): return [i for i in ids if low<=state[i]<=high]
 def started(chunk,table):
     return [start for ops in table.values() for i,take,start in ops if i==chunk and start is not None]
@@ -591,8 +584,8 @@
 def ffn_kernel(x1,vec,*refs):
     wup,bup,wdn,rest=refs[:4],refs[4:8],refs[8:12],refs[12:]
     gain,bdn=vec.at[0:1],vec.at[1:2]
-    gy0,gout,zeros,dbup_o,dbdn_o,dgain_o,gx1_o,block_o,pair_o,total_o,final_o=rest[:11]
-    h_s,hT_s,acc,gy_s,out_s,act_s,gu_s,grad_s,pair_s,far_s,total_s,send,recv,g_send,g_recv,b_send,b_recv,local=rest[11:]
+    gy0,gout,dbup_o,dbdn_o,dgain_o,gx1_o,block_o,pair_o,total_o,final_o=rest[:10]
+    h_s,hT_s,acc,gy_s,out_s,act_s,gu_s,grad_s,pair_s,far_s,total_s,send,recv,g_send,g_recv,b_send,b_recv,local=rest[10:]
     g=pl.program_id(0)
     R=h_s.shape[0]; ch=R//3; piece=R//18
     chunks=[Reduce(TILE,send.at[i],recv.at[i],grad=grad_s.at[i%2],pair=pair_s.at[i],far=far_s.at[i],total=total_s.at[i]) for i in range(STEPS)]
@@ -608,7 +601,9 @@
         meet(True,(1,2))
         arrive.begin()
         first.start()
-        pad_unit(zeros,gy_s.at[pl.ds(9,9)],local.at[4])
+        @pl.when(lax.rem(place_ids()[0],2)==1)
+        def _():
+            gy_s[16:18]=jnp.zeros((2,)+gy_s.shape[1:],BF)
         n,_=norm_rows(x1[...])
         h=(n*gain[...].astype(F32)).astype(BF)
         h_s[...]=h
@@ -684,14 +679,13 @@
 
 def ffn(x1,vec,wup,bup,wdn,gy0,gout):
     R=x1.shape[0]; half=R//2; piece=half//9
-    zeros=np.zeros((2,piece,D),BF)
     count=lambda low,high: max(1,len(in_state(FFN_STATE,range(STEPS),low,high)))
     tile=lambda j: lax.rem(j,STEPS)
     ups=[pl.BlockSpec((D,128),(lambda s:(lambda j:(0,s*STEPS+tile(j))))(s)) for s in range(4)]
     downs=[pl.BlockSpec((128,D),(lambda s:(lambda j:(s*STEPS+tile(j),0)))(s)) for s in range(4)]
     biases=[pl.BlockSpec((1,128),(lambda s:(lambda j:(0,s*STEPS+tile(j))))(s)) for s in range(4)]
     return pl.pallas_call(ffn_kernel,grid=(PHASE+STEPS,),
-        in_specs=[once((R,D)),once((4,D))]+ups+biases+downs+[ANYSPACE]*2+[once(zeros.shape)],
+        in_specs=[once((R,D)),once((4,D))]+ups+biases+downs+[ANYSPACE]*2,
         out_specs=[pl.BlockSpec((1,512),lambda j:(0,jnp.maximum(j-PHASE,0))),whole((1,D)),whole((1,D))]+[ANYSPACE]*5,
         out_shape=[jax.ShapeDtypeStruct((1,FF),F32),jax.ShapeDtypeStruct((1,D),F32),jax.ShapeDtypeStruct((1,D),F32),jax.ShapeDtypeStruct((R,D),F32),jax.ShapeDtypeStruct((4,2,2,piece,D),BF),
             jax.ShapeDtypeStruct((count(0,0),2,2,TILE,128),BF),jax.ShapeDtypeStruct((count(1,3),2,TILE,128),BF),jax.ShapeDtypeStruct((1,2,TILE,128),BF)],
@@ -700,11 +694,11 @@
             DMA((STEPS,8)),DMA((STEPS,8)),DMA((8,)),DMA((9,)),DMA((2,8)),DMA((2,8)),DMA((STEPS+7,))],
         compiler_params=pltpu.CompilerParams(vmem_limit_bytes=VMEM_LIMIT,dimension_semantics=("arbitrary",),collective_id=2,has_side_effects=True),
         cost_estimate=pl.CostEstimate(flops=14*R*D*FF,bytes_accessed=40<<20,transcendentals=2*R*FF),
-        name="ffn")(x1,vec,*[wup]*4,*[bup]*4,*[wdn]*4,gy0,gout,zeros)
-
-def bwd_attn_kernel(half,xc,noise,segc,segr,vec,gx1,q,k,v,mix,lse,wq,wk,wv,wout,trig,mixed,tile_pair,tile_total,tile_final,
-                    gin_o,demb_o,dgain_o,tiles_o,wpair_o,wtotal_o,wfinal_o,hT_s,gh,biasT_s,selfT_s,dq_s,dk_s,dv_s,ga,trig_s,
-                    t_pair,t_far,t_total,t_over,t_final,w_grad,w_pair,w_far,w_total,w_over,w_final,t_send,t_recv,w_send,w_recv,local):
+        name="ffn")(x1,vec,*[wup]*4,*[bup]*4,*[wdn]*4,gy0,gout)
+
+def bwd_attn_kernel(half,xc,noise,segc,segr,vec,gx1,q,k,v,mix,lse,wq,wk,wv,wout,trig,mixed,gain_two,down_shift,up_shift,tile_pair,tile_total,tile_final,
+                    tiles_o,wings_o,gin_o,sums_o,hT_s,gh,biasT_s,selfT_s,dq_s,dk_s,dv_s,ga,trig_s,
+                    t_pair,t_far,t_total,t_over,t_final,w_grad,w_pair,w_far,w_total,w_over,w_final,gin_s,sum_s,in_s,t_send,t_recv,w_send,w_recv,v_send,v_recv,a_send,a_recv,local):
     p=pl.program_id(0)
     emb,gain=vec.at[2:3],vec.at[3:4]
     rank,_=place_ids()
@@ -796,38 +790,58 @@
             e=g1*g
             outs.append(gx1[c*half:(c+1)*half]+scale*(e-jnp.mean(e,axis=-1,keepdims=True)-n*jnp.mean(e*n,axis=-1,keepdims=True)))
         masked=noise[...]==1
-        gin_o[...]=(outs[1]+jnp.where(masked,0.0,outs[0])).astype(gin_o.dtype)
-        demb_o[...]=jnp.sum(jnp.where(masked,outs[0],0.0),axis=0,keepdims=True)
-        dgain_o[...]=dg
-        for i,stage in ATTN_END: chunks[i].take(stage)
-        stores=[]
-        for i in in_state(ATTN_STATE,range(STEPS),4,7): stores.append((t_final.at[i],tiles_o.at[i]))
-        for low,high,source,target in ((0,0,w_pair,wpair_o),(1,3,w_total,wtotal_o),(4,7,w_final,wfinal_o)):
-            for place,i in enumerate(in_state(ATTN_STATE,range(STEPS,STEPS+4),low,high)): stores.append((source.at[i-STEPS],target.at[place]))
-        stores=[pltpu.make_async_copy(a,b,local.at[2+n]) for n,(a,b) in enumerate(stores)]
+        gin=(outs[1]+jnp.where(masked,0.0,outs[0])).astype(BF)
+        gin_s[...]=gin.reshape(gin_s.shape)
+        demb=jnp.sum(jnp.where(masked,outs[0],0.0),axis=0,keepdims=True)
+        row=0
+        for part in (demb,dg,gain_two,down_shift):
+            for n in range(D//128):
+                sum_s[0,row:row+1]=part[:,n*128:(n+1)*128]
+                row+=1
+        for a in range(4):
+            for n in range(STEPS):
+                sum_s[0,row:row+1]=up_shift[:,n*512+a*128:n*512+(a+1)*128]
+                row+=1
+        units=FromUnit(lambda t:gin_s.at[t],lambda q,h:gin_o.at[q,h],a_send,a_recv,local.at[0])
+        some=chunks[STEPS]
+        vectors=[remote(sum_s.at[n],in_s.at[n],v_send.at[n],v_recv.at[n],where) for n,where in enumerate((some.sib,some.far_id,some.xn,some.z1n,some.z2n))]
+        for item,take,start in TAIL_ORDER:
+            if item=="rows":
+                if start==1: units.begin_rest()
+                units.begin_one(start)
+            elif item=="sums":
+                if take is not None:
+                    vectors[take].wait_recv()
+                    sum_s[take+1]=sum_s[take]+in_s[take]
+                if start is not None: vectors[start].start()
+            else: do_ops([(item,take,start)],chunks)
+        stores=[pltpu.make_async_copy(t_final,tiles_o,local.at[1]),pltpu.make_async_copy(w_final,wings_o,local.at[2])]
         for d in stores: d.start()
-        for i,chunk in enumerate(chunks): chunk.sent(*started(i,ATTN_TABLE))
+        sums_o[...]=sum_s[5]
+        for d in vectors: d.wait_send()
+        for n,chunk in enumerate(chunks):
+            chunk.sent(*(started(n,ATTN_TABLE)+[start for item,take,start in TAIL_ORDER if item==n and start is not None]))
+        units.finish()
         for d in stores: d.wait()
 
-def bwd_attn(xc,noise,segc,segr,vec,gx1,q,k,v,mix,lse,wqkv,wout,trig,tile_pair,tile_total,tile_final):
+def bwd_attn(xc,noise,segc,segr,vec,gx1,q,k,v,mix,lse,wqkv,wout,trig,vectors,tile_pair,tile_total,tile_final):
     half=xc.shape[0]; R=2*half; piece=half//9
     ntp=lse.shape[1]
     ws=[pl.BlockSpec((D,PAIR),(lambda off:(lambda p:(0,off+p)))(o*PAIRS)) for o in range(3)]
     rows=pl.BlockSpec((R,PAIR),lambda p:(0,p))
     pairs=max(1,len(in_state(FFN_STATE,range(STEPS),0,0)))
-    count=lambda low,high: max(1,len(in_state(ATTN_STATE,range(STEPS,STEPS+4),low,high)))
     return pl.pallas_call(partial(bwd_attn_kernel,half),grid=(PAIRS,),
         in_specs=[once((half,D)),once((half,1)),once((half,1)),once((1,640)),once((4,D)),once((R,D)),rows,rows,rows,rows,
-                  pl.BlockSpec((1,ntp,256),lambda p:(p,0,0)),*ws,pl.BlockSpec((PAIR,D),lambda p:(p,0)),ANYSPACE,once((R,D))]+[ANYSPACE]*3,
-        out_specs=[whole((half,D)),whole((1,D)),whole((1,D))]+[ANYSPACE]*4,
-        out_shape=[jax.ShapeDtypeStruct((half,D),BF),jax.ShapeDtypeStruct((1,D),F32),jax.ShapeDtypeStruct((1,D),F32),jax.ShapeDtypeStruct((STEPS,2,TILE,128),BF),jax.ShapeDtypeStruct((count(0,0),2,2,WING,128),BF),jax.ShapeDtypeStruct((count(1,3),2,WING,128),BF),jax.ShapeDtypeStruct((count(4,7),2,WING,128),BF)],
+                  pl.BlockSpec((1,ntp,256),lambda p:(p,0,0)),*ws,pl.BlockSpec((PAIR,D),lambda p:(p,0)),ANYSPACE,once((R,D))]+[once(a.shape) for a in vectors]+[ANYSPACE]*3,
+        out_specs=[ANYSPACE]*3+[whole((48,128))],
+        out_shape=[jax.ShapeDtypeStruct((STEPS,2,TILE,128),BF),jax.ShapeDtypeStruct((4,2,WING,128),BF),jax.ShapeDtypeStruct((4,2,piece,D),BF),jax.ShapeDtypeStruct((48,128),F32)],
         scratch_shapes=[pltpu.VMEM((D,R),BF),pltpu.VMEM((R,D),F32),pltpu.VMEM((2,half,-(-half//128)*128),F32),pltpu.VMEM((half,128),F32)]+[pltpu.VMEM((R,PAIR),F32)]*3+[pltpu.VMEM((R,D),BF),pltpu.VMEM((half,2*PAIR),F32)]
             +[pltpu.VMEM((pairs,2,2,TILE,128),BF),pltpu.VMEM((pairs,2,TILE,128),BF),pltpu.VMEM((STEPS,2,TILE,128),BF),pltpu.VMEM((STEPS,2*TILE,128),BF),pltpu.VMEM((STEPS,2,TILE,128),BF),
-              pltpu.VMEM((4,2,2,2,WING,128),BF),pltpu.VMEM((4,2,2,WING,128),BF),pltpu.VMEM((4,2,WING,128),BF),pltpu.VMEM((4,2,WING,128),BF),pltpu.VMEM((4,2*WING,128),BF),pltpu.VMEM((4,2,WING,128),BF),
-              DMA((STEPS,8)),DMA((STEPS,8)),DMA((4,8)),DMA((4,8)),DMA((16,))],
+              pltpu.VMEM((4,2,2,2,WING,128),BF),pltpu.VMEM((4,2,2,WING,128),BF),pltpu.VMEM((4,2,WING,128),BF),pltpu.VMEM((4,2,WING,128),BF),pltpu.VMEM((4,2*WING,128),BF),pltpu.VMEM((4,2,WING,128),BF),pltpu.VMEM((9,piece,D),BF),pltpu.VMEM((6,48,128),F32),pltpu.VMEM((5,48,128),F32),
+              DMA((STEPS,8)),DMA((STEPS,8)),DMA((4,8)),DMA((4,8)),DMA((5,)),DMA((5,)),DMA((8,)),DMA((8,)),DMA((16,))],
         compiler_params=pltpu.CompilerParams(vmem_limit_bytes=VMEM_LIMIT,dimension_semantics=("arbitrary",),collective_id=3,has_side_effects=True),
         cost_estimate=pl.CostEstimate(flops=4*R*D*(3*D+D)+60*R*half*D//2*2,bytes_accessed=30<<20,transcendentals=R*half*HEADS),
-        name="bwd_attn")(xc,noise,segc,segr,vec,gx1,q,k,v,mix,lse,wqkv,wqkv,wqkv,wout,trig,mix,tile_pair,tile_total,tile_final)
+        name="bwd_attn")(xc,noise,segc,segr,vec,gx1,q,k,v,mix,lse,wqkv,wqkv,wqkv,wout,trig,mix,*vectors,tile_pair,tile_total,tile_final)
 
 def assemble(ffn,wings,gin,block):
     piece=gin.shape[2]
@@ -943,16 +957,6 @@
             @pl.when(take)
             def _():
                 remote(self.target(slot), self.target(slot), self.send.at[0], self.recv.at[slot], {"ctx": c}).wait_recv()
-
-
-def pad_unit(zeros, target, sem):
-    c, _ = place_ids()
-    copy = pltpu.make_async_copy(zeros, target.at[pl.ds(7, 2)], sem)
-
-    @pl.when(c % 2 == 1)
-    def _():
-        copy.start()
-        copy.wait()
 
 
 class FromUnit:
@@ -1162,89 +1166,6 @@
 WING = 576
 
 
-def tail_kernel(tiles, wpair, wtotal, wfinal, gin, embed, gain_one, gain_two, down_shift, up_shift, tiles_o, wings_o, gin_o, sums_o,
-                t_over, t_total, t_final, w_pair, w_far, w_over, w_total, w_final, sum_s, in_s,
-                t_send, t_recv, r_send, r_recv, v_send, v_recv, a_send, a_recv, local):
-    rows = FromUnit(lambda i: gin.at[i], lambda q, h: gin_o.at[q, h], a_send, a_recv, local.at[0])
-    open_tiles = in_state(ATTN_STATE, range(STEPS), 4, 6)
-    chunks = {i: Reduce(TILE, t_send.at[k], t_recv.at[k], total=t_total, over=t_over, final=t_final.at[k])
-              for k, i in enumerate(open_tiles)}
-    loads = [(tiles.at[i], t_final.at[k]) for k, i in enumerate(open_tiles)]
-    wings = range(STEPS, STEPS + 4)
-    for w in wings:
-        k = w - STEPS
-        chunks[w] = Reduce(WING, r_send.at[k], r_recv.at[k], pair=w_pair, far=w_far, total=w_total.at[k], over=w_over.at[k],
-                           final=w_final.at[k])
-    for low, high, source, target in ((0, 0, wpair, None), (1, 3, wtotal, w_total), (4, 7, wfinal, w_final)):
-        for place, w in enumerate(in_state(ATTN_STATE, wings, low, high)):
-            loads.append((source.at[place], w_pair if target is None else target.at[w - STEPS]))
-    loads = [pltpu.make_async_copy(a, b, local.at[1 + n]) for n, (a, b) in enumerate(loads)]
-    for copy in loads:
-        copy.start()
-    row = 0
-    for part in (embed, gain_one, gain_two, down_shift):
-        for i in range(D // 128):
-            sum_s[0, row:row + 1] = part[:, i * 128:(i + 1) * 128]
-            row += 1
-    for s in range(4):
-        for j in range(STEPS):
-            sum_s[0, row:row + 1] = up_shift[:, j * 512 + s * 128:j * 512 + (s + 1) * 128]
-            row += 1
-    some = chunks[STEPS]
-    vectors = [remote(sum_s.at[i], in_s.at[i], v_send.at[i], v_recv.at[i], where)
-               for i, where in enumerate((some.sib, some.far_id, some.xn, some.z1n, some.z2n))]
-    for copy in loads:
-        copy.wait()
-    meet(True, (1, 2))
-    for chunk, take, start in TAIL_ORDER:
-        if chunk == "rows":
-            if start == 1:
-                rows.begin_rest()
-            rows.begin_one(start)
-        elif chunk == "sums":
-            if take is not None:
-                vectors[take].wait_recv()
-                sum_s[take + 1] = sum_s[take] + in_s[take]
-            if start is not None:
-                vectors[start].start()
-        else:
-            if take is not None:
-                chunks[chunk].take(take)
-            if start is not None:
-                chunks[chunk].start(start)
-    stores = [(t_final.at[k], tiles_o.at[i]) for k, i in enumerate(open_tiles)] + [(w_final, wings_o)]
-    stores = [pltpu.make_async_copy(a, b, local.at[1 + n]) for n, (a, b) in enumerate(stores)]
-    for copy in stores:
-        copy.start()
-    sums_o[...] = sum_s[5]
-    for i in range(5):
-        vectors[i].wait_send()
-    for i, chunk in chunks.items():
-        chunk.sent(*range(ATTN_STATE[i] + 1, 8))
-    rows.finish()
-    for copy in stores:
-        copy.wait()
-
-
-def tail(tiles, wpair, wtotal, wfinal, gin, vectors):
-    piece = gin.shape[1]
-    n = max(1, len(in_state(ATTN_STATE, range(STEPS), 4, 6)))
-    return pl.pallas_call(
-        tail_kernel,
-        in_specs=[ANYSPACE] * 5 + [INVMEM] * 5,
-        out_specs=[ANYSPACE] * 3 + [INVMEM],
-        out_shape=[jax.ShapeDtypeStruct(tiles.shape, BF), jax.ShapeDtypeStruct((4, 2, WING, 128), BF),
-                   jax.ShapeDtypeStruct((4, 2, piece, D), BF), jax.ShapeDtypeStruct((48, 128), F32)],
-        scratch_shapes=[pltpu.VMEM((16, 128), BF), pltpu.VMEM((2, 16, 128), BF), pltpu.VMEM((n, 2, TILE, 128), BF),
-                        pltpu.VMEM((2, 2, WING, 128), BF), pltpu.VMEM((2, WING, 128), BF), pltpu.VMEM((4, 2 * WING, 128), BF),
-                        pltpu.VMEM((4, 2, WING, 128), BF), pltpu.VMEM((4, 2, WING, 128), BF), pltpu.VMEM((6, 48, 128), F32),
-                        pltpu.VMEM((5, 48, 128), F32),
-                        DMA((n, 8)), DMA((n, 8)), DMA((4, 8)), DMA((4, 8)), DMA((5,)), DMA((5,)), DMA((8,)), DMA((8,)), DMA((n + 6,))],
-        input_output_aliases={0: 0},
-        compiler_params=pltpu.CompilerParams(collective_id=4, has_side_effects=True, vmem_limit_bytes=VMEM_LIMIT),
-        name="tail")(tiles, wpair, wtotal, wfinal, gin, *vectors)
-
-
 def assemble_kernel(ffn, wings, gin, block, up_o, down_o, out_o, qkv_o, gin_o, block_o):
     i = pl.program_id(0)
     tile = lambda r: ffn[0, r // TILE, r % TILE:r % TILE + 64].astype(F32)
@@ -1286,24 +1207,22 @@
     piece = clean_in.shape[2]
     half = 9 * piece
     width = mask_embed.shape[0]
-    meta = jnp.concatenate([segments.reshape(8, 1, piece), noise.reshape(8, 1, piece)], axis=2)
-    meta = jnp.broadcast_to(meta, (8, 8, 2 * piece))
-    row = lax.broadcasted_iota(jnp.int32, (16, 256), 0)
-    small = jnp.zeros((16, 256), BF)
+    line = lax.broadcasted_iota(jnp.int32, (8, 8, piece), 1)
+    meta = jnp.where(line == 0, segments.reshape(8, 1, piece), noise.reshape(8, 1, piece))
+    row = lax.broadcasted_iota(jnp.int32, (16, width), 0)
+    small = jnp.zeros((16, width), BF)
     for i, vector in enumerate((mask_embed, norm1_gain, norm2_gain, down_bias)):
-        small = jnp.where(row == i, jnp.pad(vector, (0, 256 - width))[None], small)
-    for i in range(up_bias.shape[0] // 256):
-        small = jnp.where(row == 4 + i, up_bias[i * 256:(i + 1) * 256][None], small)
+        small = jnp.where(row == i, vector[None], small)
+    for i in range(4):
+        small = jnp.where(row == 4 + i, up_bias[i * width:(i + 1) * width][None], small)
     q, k, v, mixed, lse, resid, mask, seg_col, seg_row, vectors, up_shift, qkv_full, out_full, up_full, down_full, cotangent, clean = fwd_attn(
         clean_in, meta, out_grad, rope_constant(half), qkv_weight, out_weight, up_weight, down_weight, small)
     clean = clean.reshape(half, D)
     up_shift_grad, down_shift_grad, gain_two_grad, grad_resid, block_out, tile_pair, tile_total, tile_final = ffn(
         resid, vectors, up_full, up_shift, down_full, cotangent, out_grad)
-    grad_in, embed_grad, gain_one_grad, tiles, wpair, wtotal, wfinal = bwd_attn(
+    tiles, wings, input_grad, sums = bwd_attn(
         clean, mask, seg_col, seg_row, vectors, grad_resid, q, k, v, mixed, lse, qkv_full, out_full, rope_constant(half),
-        tile_pair, tile_total, tile_final)
-    tiles, wings, input_grad, sums = tail(tiles, wpair, wtotal, wfinal, grad_in.reshape(9, piece, D),
-                                          (embed_grad, gain_one_grad, gain_two_grad, down_shift_grad, up_shift_grad))
+        (gain_two_grad, down_shift_grad, up_shift_grad), tile_pair, tile_total, tile_final)
     up_sum, down_sum, out_sum, qkv_sum, input_grad, block_out = assemble(tiles, wings, input_grad, block_out)
     input_grad = input_grad.reshape(clean_in.shape)
     block_out = block_out.reshape(out_grad.shape)

time: 324 us -> 308 us (0.951)
  Pallas kernels: 313 us -> 298 us
  local copies, waits for them, and re-layouts: 7.58 us -> 3.73 us
    pallas_call x1 -> x0, Pallas kernels: 60 us -> none  [tail(): pl.pallas_call(tail_kernel, in_specs=[ANYSPACE] * 5 + [INVMEM] * 5, out_s...]
    pallas_call x1, Pallas kernels: 86.6 us -> 132 us  [bwd_attn(): pl.pallas_call(partial(bwd_attn_kernel, half), grid=(PAIRS,), in_specs=[o...]
where the time goes in v5:
time: 308 us; the launch traced here: 305 us
  Pallas kernels  298 us (97%)
  local copies, waits for them, and re-layouts  3.73 us (1%)
    pallas_call x1, Pallas kernels, bwd_attn(): pl.pallas_call(partial(bwd_attn_kernel, half), grid=(PAIRS,), in_specs=[o...  132 us
    pallas_call x1, Pallas kernels, ffn(): pl.pallas_call(ffn_kernel, grid=(PHASE + STEPS,), in_specs=[once((R, D)),...  81.9 us
    pallas_call x1, Pallas kernels, fwd_attn(): pl.pallas_call(partial(fwd_attn_comm_kernel, half), grid=(PAIRS,), in_spe...  75.1 us
    pallas_call x1, Pallas kernels, assemble(): pl.pallas_call(assemble_kernel, grid=(STEPS,), in_specs=[pl.BlockSpec((1,...  8.87 us

profile of v5, /device:TPU:0, one launch (start us, length us, event | category | flops | bytes accessed | tf_op | source)
XLA Modules:
  0.0 305.0 jit_solution(5642426215352993029)
XLA Ops:
  0.6 0.9 fusion.1
  1.6 1.4 select_select_fusion.refs_8_
  3.0 1.4 broadcast_select_fusion.refs_1_
  4.4 75.1 %fwd_attn.1 = (bf16[1152,768]{1,0:T(8,128)(2,1)}, bf16[1152,768]{1,0:T(8,128)(2,1)}, bf16[1152,768]{1,0:T(8,128)(2,1)}, bf16[1152,768]{1,0:T(8,128)(2,1)}, f32[6...) custom-call(bf16[4,2,64,768]{3,2,1,0:T(8,128)(2,1)} %refs_0_.1, ...), custom_call_target="tpu_custom_call" | custom-call | flops 17666408448 | bytes 16777216 | tf_op jit(solution)/shard_map/fwd_attn/pallas_call | solution.py:533
  79.5 81.9 %ffn.1 = (f32[1,3072]{1,0:T(1,128)}, f32[1,768]{1,0:T(1,128)}, f32[1,768]{1,0:T(1,128)}, f32[1152,768]{1,0:T(8,128)}, bf16[4,2,2,64,768]{4,3,2,1,0:T(8,128)(2,1)...) custom-call(f32[1152,768]{1,0:T(8,128)} %get-tuple-element.51.x1, ...), custom_call_target="tpu_custom_call" | custom-call | flops 38050725888 | bytes 41943040 | tf_op jit(solution)/shard_map/ffn/pallas_call | solution.py:687
  161.4 131.7 %bwd_attn.1 = (bf16[6,2,768,128]{3,2,1,0:T(8,128)(2,1)}, bf16[4,2,576,128]{3,2,1,0:T(8,128)(2,1)}, bf16[4,2,64,768]{3,2,1,0:T(8,128)(2,1)}, f32[48,128]{1,0:T(8,128)}) custom-call(bf16[576,768]{1,0:T(8,128)(2,1)} %bitcast.16, s32[576,1]{1,0:T(8,128)} %get-tuple-element.47.noise, f32[576,1]{1,0:T(8,128)} %get-tuple-element.48.segc, ...), custom_call_target="tpu_custom_call" | custom-call | flops 41448112128 | bytes 31457280 | tf_op jit(solution)/shard_map/bwd_attn/pallas_call | solution.py:833
  293.1 8.9 %assemble.1 = (f32[192,3072]{1,0:T(8,128)}, f32[768,768]{1,0:T(8,128)}, f32[192,768]{1,0:T(8,128)}, f32[192,2304]{1,0:T(8,128)}, f32[8,64,768]{2,1,0:T(8,128)}, /*index=5*/bf16[16,64,768]{2,1,0:T(8,128)(2,1)}) custom-call(bf16[6,2,768,128]{3,2,1,0:T(8,128)(2,1)} %get-tuple-element.70.ffn, bf16[4,2,576,128]{3,2,1,0:T(8,128)(2,1)} %get-tuple-element.71.wings, ...), custom_call_target="tpu_custom_call" | custom-call | tf_op jit(solution)/shard_map/assemble/pallas_call | solution.py:848
  302.0 1.5 fusion
  303.4 1.4 dynamic_slice.18
  (5 shorter events, 0.0 us)

commit v6 on v5

--- a/solution.py
+++ b/solution.py
@@ -552,8 +552,8 @@
 
 FFN_TABLE={2: [(0, None, 0)], 4: [(1, None, 0), (0, 0, 1)], 6: [(2, None, 0), (1, 0, 1)], 8: [(3, None, 0), (0, 1, None), (2, 0, 1)], 9: [(3, 0, None)], 10: [(4, None, 0), (1, 1, None)], 12: [(5, None, 0)]}
 FFN_END=[(4, 0), (2, 1), (5, 0)]
-ATTN_TABLE={0: [(3, None, 1), (4, None, 1), (5, None, 1), (0, None, 2), (1, None, 2), (2, None, 2)], 1: [(6, None, 0)], 2: [(0, 2, 3), (6, 0, 1)], 3: [(0, 3, 4), (1, 2, 3), (3, 1, 2)], 4: [(7, None, 0), (0, 4, 5), (2, 2, 3)], 5: [(1, 3, 4), (0, 5, 6), (3, 2, 3), (4, 1, 2), (7, 0, 1), (2, 3, 4)], 6: [(0, 6, 7), (1, 4, 5), (5, 1, 2)], 7: [(2, 4, 5), (3, 3, 4), (4, 2, 3)], 8: [(8, None, 0), (0, 7, None), (1, 5, 6), (2, 5, 6), (6, 1, 2)], 9: [(1, 6, 7), (3, 4, 5), (4, 3, 4), (5, 2, 3), (7, 1, 2), (8, 0, 1), (6, 2, 3)], 10: [(2, 6, 7), (3, 5, 6)], 11: [(1, 7, None), (3, 6, 7), (4, 4, 5), (5, 3, 4), (6, 3, 4), (7, 2, 3), (8, 1, 2)], 12: [(9, None, 0)]}
-TAIL_ORDER=[("sums", None, 0), (3, 7, None), (2, 7, None), (4, 5, 6), (5, 4, 5), (6, 4, 5), (7, 3, 4), (9, 0, 1), ("rows", None, 1), ("rows", None, 2), (8, 2, 3), ("sums", 0, 1), (4, 6, 7), ("sums", 1, 2), (5, 5, 6), (6, 5, 6), (9, 1, 2), ("rows", None, 3), (4, 7, None), (7, 4, 5), ("sums", 2, 3), (8, 3, 4), (9, 2, 3), ("rows", None, 4), ("sums", 3, 4), (5, 6, 7), (6, 6, 7), ("sums", 4, None), (7, 5, 6), (5, 7, None), (9, 3, 4), ("rows", None, 5), (8, 4, 5), (6, 7, None), (7, 6, 7), (9, 4, 5), ("rows", None, 6), (7, 7, None), (8, 5, 6), (9, 5, 6), ("rows", None, 7), (8, 6, 7), (9, 6, 7), (8, 7, None), (9, 7, None)]
+ATTN_TABLE={0: [(3, None, 1), (4, None, 1), (5, None, 1), (0, None, 2), (1, None, 2), (2, None, 2)], 1: [(6, None, 0)], 2: [(0, 2, 3), (6, 0, 1)], 3: [(0, 3, 4), (1, 2, 3), (3, 1, 2)], 4: [(7, None, 0), (0, 4, 5), (2, 2, 3)], 5: [(0, 5, 6), (1, 3, 4), (3, 2, 3), (4, 1, 2), (7, 0, 1), (2, 3, 4)], 6: [(0, 6, 7)], 7: [(1, 4, 5), (3, 3, 4), (4, 2, 3), (2, 4, 5), (5, 1, 2)], 8: [(8, None, 0), (0, 7, None), (1, 5, 6), (6, 1, 2)], 9: [(1, 6, 7), (2, 5, 6), (3, 4, 5), (4, 3, 4), (5, 2, 3), (7, 1, 2), (6, 2, 3), (8, 0, 1)], 10: [(2, 6, 7)], 11: [(1, 7, None), (3, 5, 6), (4, 4, 5), (5, 3, 4), (6, 3, 4), (7, 2, 3), (8, 1, 2)], 12: [(9, None, 0)]}
+TAIL_ORDER=[("sums", None, 0), (2, 7, None), (3, 6, 7), (4, 5, 6), (5, 4, 5), (6, 4, 5), (7, 3, 4), (8, 2, 3), (9, 0, 1), ("rows", None, 1), ("rows", None, 2), ("sums", 0, 1), (4, 6, 7), ("sums", 1, 2), (3, 7, None), (5, 5, 6), (6, 5, 6), (8, 3, 4), (9, 1, 2), ("rows", None, 3), (7, 4, 5), ("sums", 2, 3), (4, 7, None), ("sums", 3, 4), (5, 6, 7), (9, 2, 3), ("rows", None, 4), (6, 6, 7), (8, 4, 5), ("sums", 4, None), (9, 3, 4), ("rows", None, 5), (5, 7, None), (7, 5, 6), (6, 7, None), (8, 5, 6), (9, 4, 5), ("rows", None, 6), (7, 6, 7), (8, 6, 7), (9, 5, 6), ("rows", None, 7), (7, 7, None), (9, 6, 7), (8, 7, None), (9, 7, None)]
 
 def after(state,table,end):
     state=dict(state)
@@ -845,15 +845,16 @@
 
 def assemble(ffn,wings,gin,block):
     piece=gin.shape[2]
-    up,down,out,qkv,grad,rows=pl.pallas_call(assemble_kernel,grid=(STEPS,),
-        in_specs=[pl.BlockSpec((1,2,TILE,128),lambda i:(i,0,0,0)),whole(wings.shape),
-            pl.BlockSpec((2,piece,D),lambda i:(jnp.minimum(i,3),0,0)),pl.BlockSpec((4,piece,D),lambda i:(jnp.minimum(i,3),0,0))],
-        out_specs=[whole((192,FF)),pl.BlockSpec((128,D),lambda i:(i,0)),whole((192,D)),whole((192,3*D)),
-            pl.BlockSpec((2,piece,D),lambda i:(jnp.minimum(i,3),0,0)),pl.BlockSpec((4,piece,D),lambda i:(jnp.minimum(i,3),0,0))],
-        out_shape=[jax.ShapeDtypeStruct((192,FF),F32),jax.ShapeDtypeStruct((768,D),F32),jax.ShapeDtypeStruct((192,D),F32),jax.ShapeDtypeStruct((192,3*D),F32),
-            jax.ShapeDtypeStruct((8,piece,D),F32),jax.ShapeDtypeStruct((16,piece,D),BF)],
+    sds=jax.ShapeDtypeStruct
+    quarter=lambda i: (jnp.minimum(i,3),0,0)
+    up,out,qkv,down,grad,rows=pl.pallas_call(assemble_kernel,grid=(STEPS,),
+        in_specs=[pl.BlockSpec((1,2,TILE,128),lambda i:(i,0,0,0)),pl.BlockSpec((None,None,WING,128),lambda i:(1+i//2,lax.rem(i,2),0,0)),
+            pl.BlockSpec((None,None,192,128),lambda i:(0,i//3,lax.rem(i,3),0)),pl.BlockSpec((2,piece,D),quarter),pl.BlockSpec((4,piece,D),quarter)],
+        out_specs=[ANYSPACE]*3+[pl.BlockSpec((128,D),lambda i:(i,0)),pl.BlockSpec((2,piece,D),quarter),pl.BlockSpec((4,piece,D),quarter)],
+        out_shape=[sds((192,FF),F32),sds((192,D),F32),sds((192,3*D),F32),sds((768,D),F32),sds((8,piece,D),F32),sds((16,piece,D),BF)],
+        scratch_shapes=[pltpu.VMEM((2,8,192,128),F32),DMA((2,8))],
         compiler_params=pltpu.CompilerParams(vmem_limit_bytes=VMEM_LIMIT,dimension_semantics=("arbitrary",)),
-        name="assemble")(ffn,wings,gin.reshape(8,piece,D),block.reshape(16,piece,D))
+        name="assemble")(ffn,wings,wings,gin.reshape(8,piece,D),block.reshape(16,piece,D))
     return up,down,out,qkv,grad,rows
 
 
@@ -1166,30 +1167,40 @@
 WING = 576
 
 
-def assemble_kernel(ffn, wings, gin, block, up_o, down_o, out_o, qkv_o, gin_o, block_o):
+def assemble_kernel(ffn, pair, out, gin, block, up_o, out_o, qkv_o, down_o, gin_o, block_o, stage, sem):
     i = pl.program_id(0)
+    slot = lax.rem(i, 2)
+
+    def copies(step, place):
+        column = lambda k: pl.ds(pl.multiple_of(k * 128, 128), 128)
+        targets = [up_o.at[:, column(s * STEPS + step)] for s in range(4)] + [out_o.at[:, column(step)]]
+        targets += [qkv_o.at[:, column(w * PAIRS + step)] for w in range(3)]
+        return [pltpu.make_async_copy(stage.at[place, k], target, sem.at[place, k]) for k, target in enumerate(targets)]
+
+    @pl.when(i >= 2)
+    def _():
+        for copy in copies(i - 2, slot):
+            copy.wait()
+
     tile = lambda r: ffn[0, r // TILE, r % TILE:r % TILE + 64].astype(F32)
-    for s in range(4):
-        for r in range(0, 192, 64):
-            up_o[r:r + 64, pl.ds(pl.multiple_of((s * STEPS + i) * 128, 128), 128)] = tile(s * 192 + r)
+    for r in range(0, 192, 64):
+        for s in range(4):
+            stage[slot, s, r:r + 64] = tile(s * 192 + r)
+        stage[slot, 4, r:r + 64] = out[r:r + 64].astype(F32)
+        for w in range(3):
+            stage[slot, 5 + w, r:r + 64] = pair[w * 192 + r:w * 192 + r + 64].astype(F32)
+    for copy in copies(i, slot):
+        copy.start()
     for t in range(6):
         for r in range(0, 128, 64):
             down_o[r:r + 64, t * 128:(t + 1) * 128] = tile(768 + t * 128 + r)
     gin_o[...] = gin[...].astype(F32)
     block_o[...] = block[...]
 
-    @pl.when(i == 0)
+    @pl.when(i == STEPS - 1)
     def _():
-        def strip(ref, k, r):
-            row = k * 192 + r
-            return ref[row // WING, row % WING:row % WING + 64].astype(F32)
-
-        for r in range(0, 192, 64):
-            for t in range(6):
-                out_o[r:r + 64, t * 128:(t + 1) * 128] = strip(wings.at[0], t, r)
-                source = wings.at[1 + t // 2]
-                for w in range(3):
-                    qkv_o[r:r + 64, w * D + t * 128:w * D + (t + 1) * 128] = strip(source, t % 2 * 3 + w, r)
+        for copy in copies(i - 1, 1 - slot) + copies(i, slot):
+            copy.wait()
 
 
 def rope_constant(half):

time: 308 us -> 308 us (level)
  no operation moved by 1% of the time
where the time goes in v6:
time: 308 us; the launch traced here: 307 us
  Pallas kernels  300 us (97%)
  local copies, waits for them, and re-layouts  3.75 us (1%)
    pallas_call x1, Pallas kernels, bwd_attn(): pl.pallas_call(partial(bwd_attn_kernel, half), grid=(PAIRS,), in_specs=[o...  134 us
    pallas_call x1, Pallas kernels, ffn(): pl.pallas_call(ffn_kernel, grid=(PHASE + STEPS,), in_specs=[once((R, D)),...  81.9 us
    pallas_call x1, Pallas kernels, fwd_attn(): pl.pallas_call(partial(fwd_attn_comm_kernel, half), grid=(PAIRS,), in_spe...  75.1 us
    pallas_call x1, Pallas kernels, assemble(): pl.pallas_call(assemble_kernel, grid=(STEPS,), in_specs=[pl.BlockSpec((1,...  8.23 us

profile of v6, /device:TPU:0, one launch (start us, length us, event | category | flops | bytes accessed | tf_op | source)
XLA Modules:
  0.0 307.0 jit_solution(6016448174389498463)
XLA Ops:
  0.6 0.9 fusion.1
  1.6 1.4 select_select_fusion.refs_8_
  3.0 1.4 broadcast_select_fusion.refs_1_
  4.4 75.1 %fwd_attn.1 = (bf16[1152,768]{1,0:T(8,128)(2,1)}, bf16[1152,768]{1,0:T(8,128)(2,1)}, bf16[1152,768]{1,0:T(8,128)(2,1)}, bf16[1152,768]{1,0:T(8,128)(2,1)}, f32[6...) custom-call(bf16[4,2,64,768]{3,2,1,0:T(8,128)(2,1)} %refs_0_.1, ...), custom_call_target="tpu_custom_call" | custom-call | flops 17666408448 | bytes 16777216 | tf_op jit(solution)/shard_map/fwd_attn/pallas_call | solution.py:533
  79.5 81.9 %ffn.1 = (f32[1,3072]{1,0:T(1,128)}, f32[1,768]{1,0:T(1,128)}, f32[1,768]{1,0:T(1,128)}, f32[1152,768]{1,0:T(8,128)}, bf16[4,2,2,64,768]{4,3,2,1,0:T(8,128)(2,1)...) custom-call(f32[1152,768]{1,0:T(8,128)} %get-tuple-element.51.x1, ...), custom_call_target="tpu_custom_call" | custom-call | flops 38050725888 | bytes 41943040 | tf_op jit(solution)/shard_map/ffn/pallas_call | solution.py:687
  161.4 134.2 %bwd_attn.1 = (bf16[6,2,768,128]{3,2,1,0:T(8,128)(2,1)}, bf16[4,2,576,128]{3,2,1,0:T(8,128)(2,1)}, bf16[4,2,64,768]{3,2,1,0:T(8,128)(2,1)}, f32[48,128]{1,0:T(8,128)}) custom-call(bf16[576,768]{1,0:T(8,128)(2,1)} %bitcast.16, s32[576,1]{1,0:T(8,128)} %get-tuple-element.47.noise, f32[576,1]{1,0:T(8,128)} %get-tuple-element.48.segc, ...), custom_call_target="tpu_custom_call" | custom-call | flops 41448112128 | bytes 31457280 | tf_op jit(solution)/shard_map/bwd_attn/pallas_call | solution.py:833
  295.7 8.2 %assemble.1 = (f32[192,3072]{1,0:T(8,128)}, f32[192,768]{1,0:T(8,128)}, f32[192,2304]{1,0:T(8,128)}, f32[768,768]{1,0:T(8,128)}, f32[8,64,768]{2,1,0:T(8,128)}, /*index=5*/bf16[16,64,768]{2,1,0:T(8,128)(2,1)}) custom-call(bf16[6,2,768,128]{3,2,1,0:T(8,128)(2,1)} %get-tuple-element.70.ffn, bf16[4,2,576,128]{3,2,1,0:T(8,128)(2,1)} %get-tuple-element.71.pair.out, ...), custom_call_target="tpu_custom_call" | custom-call | tf_op jit(solution)/shard_map/assemble/pallas_call | solution.py:850
  303.9 1.5 fusion
  305.4 1.4 dynamic_slice.18
  (5 shorter events, 0.0 us)

commit v7 on v6

--- a/solution.py
+++ b/solution.py
@@ -512,8 +512,8 @@
         def _():
             for op in ops: op()
     at(0,w_out.relay_far,*[partial(w_up.relay_far,i) for i in range(2)])
-    at(1,w_out.relay_x,partial(w_up.relay_far,2),partial(w_up.relay_x,0),grads[0].begin_across)
-    at(2,w_out.finish,copies[1].start,partial(w_up.relay_x,1),partial(w_down.relay_far,0))
+    at(1,w_out.relay_x,partial(w_up.relay_far,2),partial(w_up.relay_x,0))
+    at(2,w_out.finish,copies[1].start,partial(w_up.relay_x,1),partial(w_down.relay_far,0),grads[0].begin_across)
     at(3,partial(w_up.relay_x,2),partial(w_down.relay_far,1))
     at(4,partial(w_down.relay_far,2))
     @pl.when(p==pl.num_programs(0)-1)

time: 308 us -> 308 us (level)
    pallas_call x1, Pallas kernels: 75.1 us -> 71.2 us  [fwd_attn(): pl.pallas_call(partial(fwd_attn_comm_kernel, half), grid=(PAIRS,), in_spe...]
    pallas_call x1, Pallas kernels: 81.9 us -> 85.3 us  [ffn(): pl.pallas_call(ffn_kernel, grid=(PHASE + STEPS,), in_specs=[once((R, D)),...]
where the time goes in v7:
time: 308 us; the launch traced here: 306 us
  Pallas kernels  299 us (97%)
  local copies, waits for them, and re-layouts  3.75 us (1%)
    pallas_call x1, Pallas kernels, bwd_attn(): pl.pallas_call(partial(bwd_attn_kernel, half), grid=(PAIRS,), in_specs=[o...  134 us
    pallas_call x1, Pallas kernels, ffn(): pl.pallas_call(ffn_kernel, grid=(PHASE + STEPS,), in_specs=[once((R, D)),...  85.3 us
    pallas_call x1, Pallas kernels, fwd_attn(): pl.pallas_call(partial(fwd_attn_comm_kernel, half), grid=(PAIRS,), in_spe...  71.2 us
    pallas_call x1, Pallas kernels, assemble(): pl.pallas_call(assemble_kernel, grid=(STEPS,), in_specs=[pl.BlockSpec((1,...  8.23 us

profile of v7, /device:TPU:0, one launch (start us, length us, event | category | flops | bytes accessed | tf_op | source)
XLA Modules:
  0.0 306.4 jit_solution(6679676086917197269)
XLA Ops:
  0.6 0.9 fusion.1
  1.6 1.4 select_select_fusion.refs_8_
  3.0 1.4 broadcast_select_fusion.refs_1_
  4.4 71.2 %fwd_attn.1 = (bf16[1152,768]{1,0:T(8,128)(2,1)}, bf16[1152,768]{1,0:T(8,128)(2,1)}, bf16[1152,768]{1,0:T(8,128)(2,1)}, bf16[1152,768]{1,0:T(8,128)(2,1)}, f32[6...) custom-call(bf16[4,2,64,768]{3,2,1,0:T(8,128)(2,1)} %refs_0_.1, ...), custom_call_target="tpu_custom_call" | custom-call | flops 17666408448 | bytes 16777216 | tf_op jit(solution)/shard_map/fwd_attn/pallas_call | solution.py:533
  75.5 85.3 %ffn.1 = (f32[1,3072]{1,0:T(1,128)}, f32[1,768]{1,0:T(1,128)}, f32[1,768]{1,0:T(1,128)}, f32[1152,768]{1,0:T(8,128)}, bf16[4,2,2,64,768]{4,3,2,1,0:T(8,128)(2,1)...) custom-call(f32[1152,768]{1,0:T(8,128)} %get-tuple-element.51.x1, ...), custom_call_target="tpu_custom_call" | custom-call | flops 38050725888 | bytes 41943040 | tf_op jit(solution)/shard_map/ffn/pallas_call | solution.py:687
  160.9 134.2 %bwd_attn.1 = (bf16[6,2,768,128]{3,2,1,0:T(8,128)(2,1)}, bf16[4,2,576,128]{3,2,1,0:T(8,128)(2,1)}, bf16[4,2,64,768]{3,2,1,0:T(8,128)(2,1)}, f32[48,128]{1,0:T(8,128)}) custom-call(bf16[576,768]{1,0:T(8,128)(2,1)} %bitcast.16, s32[576,1]{1,0:T(8,128)} %get-tuple-element.47.noise, f32[576,1]{1,0:T(8,128)} %get-tuple-element.48.segc, ...), custom_call_target="tpu_custom_call" | custom-call | flops 41448112128 | bytes 31457280 | tf_op jit(solution)/shard_map/bwd_attn/pallas_call | solution.py:833
  295.1 8.2 %assemble.1 = (f32[192,3072]{1,0:T(8,128)}, f32[192,768]{1,0:T(8,128)}, f32[192,2304]{1,0:T(8,128)}, f32[768,768]{1,0:T(8,128)}, f32[8,64,768]{2,1,0:T(8,128)}, /*index=5*/bf16[16,64,768]{2,1,0:T(8,128)(2,1)}) custom-call(bf16[6,2,768,128]{3,2,1,0:T(8,128)(2,1)} %get-tuple-element.70.ffn, bf16[4,2,576,128]{3,2,1,0:T(8,128)(2,1)} %get-tuple-element.71.pair.out, ...), custom_call_target="tpu_custom_call" | custom-call | tf_op jit(solution)/shard_map/assemble/pallas_call | solution.py:850
  303.4 1.5 fusion
  304.9 1.4 dynamic_slice.18
  (5 shorter events, 0.0 us)
